TPU v7x, 256 devices: a whole 4x4x8 slice. The times are simulated.
256 devices in a mesh: cable: 32 (over y_lo, z, core), grid: 8 (over x, y_hi).
Axes of the slice: x: 4, y: 4 (y_hi: 2, y_lo: 2; y = y_hi * 2 + y_lo), z: 8, core: 2. Of those that a mesh axis runs over, the one named last changes fastest.
Arguments:
- green: bfloat16 [2, 8192, 16384], P(None, 'cable', 'grid'), may hold values from -6 to 6
- source_weight: float32 [16384], P('grid'), may hold values from 0.25 to 4
- observed: float32 [2, 2, 8192, 256], P(None, None, 'cable'), may hold values from -6 to 6
- amp_weight: float32 [2, 8192, 256], P(None, 'cable'), may hold values from 0.25 to 2
- pair_used: int32 [32, 2], P('cable'), may hold values 0 or 1
Outputs:
- adjoint: float32 [2, 8192, 16384], P(None, 'cable', 'grid')
- kernel: float32 [16384], P('grid')
All inputs are finite; a program needn't handle non-finite values. No bound on the sum of `pair_used` on one device may be relied on, other than what follows from the above.
Results may differ from a plain program's by a relative error of at most 0.0037.
Values may be sent and summed in bfloat16 or wider, within the bound.
No kernel may reach another device: no remote copies, remote signals or barrier semaphores. Data moves between devices by JAX's collectives and lax.ppermute only.
A program may use at most 64 MiB of HBM per device.

v0:
```python
import math

import jax
import jax.numpy as jnp
from jax import lax
from jax.sharding import PartitionSpec as P


def shifted(block, axis, distance):
    devices = range(lax.axis_size(axis))
    route = [((i - distance) % len(devices), i) for i in devices]
    return lax.ppermute(block, axis, route)


def build_block(pair_resid):
    resid_real = pair_resid[0]
    resid_imag = pair_resid[1]
    upper_half = jnp.concatenate([resid_real, resid_imag], axis=1)
    lower_half = jnp.concatenate([-resid_imag, resid_real], axis=1)
    return jnp.concatenate([upper_half, lower_half], axis=0)


def residuals(corr, observed_rows, weight_rows, pair_used):
    mask_values = pair_used[0].astype(jnp.float32)
    scaled = mask_values[:, None, None, None] * weight_rows[:, None, :, :] * (corr - observed_rows)
    return scaled.astype(jnp.bfloat16)


def shards(green, source_weight, observed, amp_weight, pair_used):
    row_count = green.shape[1]
    col_count = green.shape[2]
    block_count = lax.axis_size("cable")
    grid_count = lax.axis_size("grid")
    inv_norm = 1.0 / math.sqrt(col_count * grid_count)
    kernel_scale = inv_norm / (2.0 * math.sqrt(2.0 * block_count))
    own_block = green.reshape(2 * row_count, col_count)
    near_blocks = []
    for offset in range(2):
        near_blocks.append(shifted(own_block, "cable", offset + 1))
    weighted = (own_block.astype(jnp.float32) * source_weight[None, :]).astype(jnp.bfloat16)
    partial_list = []
    for offset in range(2):
        products = lax.dot_general(
            weighted,
            near_blocks[offset],
            (((1,), (1,)), ((), ())),
            preferred_element_type=jnp.float32,
        )
        corr_real = products[:row_count, :row_count] + products[row_count:, row_count:]
        corr_imag = products[:row_count, row_count:] - products[row_count:, :row_count]
        partial_list.append(jnp.stack([corr_real, corr_imag]))
    partials = jnp.stack(partial_list)
    summed = lax.psum(partials, "grid")
    resid = residuals(inv_norm * summed, observed, amp_weight, pair_used)
    own_float = own_block.astype(jnp.float32)
    fields = jnp.zeros((2 * row_count, col_count), jnp.float32)
    kernel_part = jnp.zeros((col_count,), jnp.float32)
    for offset in range(2):
        resid_block = build_block(resid[offset])
        later_term = jnp.dot(resid_block, near_blocks[offset], preferred_element_type=jnp.float32)
        kernel_part = kernel_part + jnp.sum(own_float * later_term, axis=0)
        fields = fields + later_term
    for offset in range(2):
        resid_block = build_block(resid[offset])
        early_term = lax.dot_general(
            resid_block, own_block, (((0,), (0,)), ((), ())), preferred_element_type=jnp.float32
        )
        fields = fields + shifted(early_term, "cable", -(offset + 1))
    kernel = lax.psum(kernel_part, "cable") * kernel_scale
    adjoint = (inv_norm * source_weight[None, :] * fields).reshape(2, row_count, col_count)
    return (adjoint, kernel)


def solution(mesh):
    in_specs = (
        P(None, "cable", "grid"),
        P("grid"),
        P(None, None, "cable", None),
        P(None, "cable", None),
        P("cable", None),
    )
    out_specs = (P(None, "cable", "grid"), P("grid"))
    return jax.shard_map(shards, mesh=mesh, in_specs=in_specs, out_specs=out_specs, check_vma=False)
```

profile of v0, /device:TPU:1, one launch (start us, length us, event | category | flops | bytes accessed | tf_op | source)
XLA Modules:
  0.0 386.9 jit_solution(2514229055779088914)
XLA Ops:
  7.2 0.0 all-reduce.2.cloned.1.call-start
  7.2 0.0 copy-start
  7.2 0.0 copy-start.6
  7.2 3.1 collective-permute-start
  10.3 1.6 collective-permute-start.1
  12.0 43.5 %collective-permute-done = bf16[512,2048]{1,0:T(8,128)(2,1)S(1)} collective-permute-done((bf16[512,2048]{1,0:T(8,128)(2,1)}, bf16[512,2048]{1,0:T(8,128)(2,1)S(1)}, u32[]{:S(2)}, u32[]{:S(2)}) %collective-permute-start) | collective-permute-done | bytes 2097184 | tf_op jit(solution)/shard_map/ppermute | solution.py:12
  55.4 0.0 copy-start.1
  55.4 3.6 fusion.5
  59.1 0.0 copy-done.1
  59.1 0.1 fusion.10
  59.2 24.1 %collective-permute-done.1 = bf16[512,2048]{1,0:T(8,128)(2,1)S(1)} collective-permute-done((bf16[512,2048]{1,0:T(8,128)(2,1)}, bf16[512,2048]{1,0:T(8,128)(2,1)S(1)}, u32[]{:S(2)}, u32[]{:S(2)}) %collective-permute-start.1) | collective-permute-done | bytes 2097184 | tf_op jit(solution)/shard_map/ppermute | solution.py:12
  83.3 0.0 copy-done
  83.3 0.0 copy-done.6
  83.3 0.0 copy-start.3
  83.3 1.3 fusion.3
  84.6 0.0 copy-done.3
  84.6 0.1 fusion.8
  84.7 0.1 maximum_bitcast_fusion
  84.8 0.0 copy-start.7
  84.8 0.0 copy-start.5
  84.8 1.1 pad_maximum_fusion
  85.9 0.0 all-reduce.2.cloned.1.call-update
  85.9 0.0 copy-done.7
  85.9 0.1 copy-done.5
  86.0 0.1 broadcast_multiply_fusion
  86.1 88.0 %all-reduce.2.cloned.1.call-done = f32[2,2,256,256]{3,2,1,0:T(8,128)} async-done(((f32[2,2,256,256]{3,2,1,0:T(8,128)}), f32[2,2,256,256]{3,2,1,0:T(8,128)}) %all-reduce.2.cloned.1.call-update) | async-done | bytes 1048592 | tf_op jit(solution)/shard_map/psum | solution.py:53
  174.1 1.7 multiply_convert_fusion
  175.9 1.3 fusion.13
  177.2 5.8 %collective-permute-start.2 = (f32[512,2048]{1,0:T(8,128)S(1)}, f32[512,2048]{1,0:T(8,128)S(1)}, u32[]{:S(2)}, u32[]{:S(2)}) collective-permute-start(f32[512,2048]{1,0:T(8,128)S(1)} %fusion.13), channel_id=1, source_target_pairs={{8,0},{16,8},{24,16},{32,24},{40,32},{48,40},{56,48},{64,56},{72,6... | collective-permute-start | bytes 12582920 | tf_op jit(solution)/shard_map/ppermute | solution.py:12
  182.9 0.0 copy-start.2
  182.9 1.3 fusion.11
  184.2 3.1 collective-permute-start.3
  187.4 0.0 copy-done.2
  187.4 0.0 copy-start.4
  187.4 1.3 fusion.14
  188.6 85.2 %collective-permute-done.2 = f32[512,2048]{1,0:T(8,128)S(1)} collective-permute-done((f32[512,2048]{1,0:T(8,128)S(1)}, f32[512,2048]{1,0:T(8,128)S(1)}, u32[]{:S(2)}, u32[]{:S(2)}) %collective-permute-start.2) | collective-permute-done | bytes 4194336 | tf_op jit(solution)/shard_map/ppermute | solution.py:12
  273.8 3.9 %collective-permute-done.3 = f32[512,2048]{1,0:T(8,128)S(1)} collective-permute-done((f32[512,2048]{1,0:T(8,128)S(1)}, f32[512,2048]{1,0:T(8,128)S(1)}, u32[]{:S(2)}, u32[]{:S(2)}) %collective-permute-start.3) | collective-permute-done | bytes 4194336 | tf_op jit(solution)/shard_map/ppermute | solution.py:12
  277.8 0.0 copy-done.4
  277.8 5.3 %fusion.2 = (f32[2048]{0:T(1024)S(1)}, f32[2048]{0:T(1024)S(1)}, f32[512,2048]{1,0:T(8,128)}) fusion(bf16[2,256,2048]{2,1,0:T(8,128)(2,1)S(1)} %copy-done, f32[512,2048]{1,0:T(8,128)S(1)} %fusion.14, f32[512,2048]{1,0:T(8,128)S(1)} %collective-permute-done.3, f32[512,2048]{1,0:T(8,128)S(1)} %collective-permute-done.2, ...), kind=kOutput, calls=%fused_computation.5 | convolution fusion | flops 1085272064 | bytes 21389312 | tf_op jit(solution)/shard_map/dot_general | solution.py:60
  283.1 96.4 %psum.15 = f32[2048]{0:T(1024)S(1)} all-reduce(f32[2048]{0:T(1024)S(1)} %add.27), channel_id=1, replica_groups=mesh['cable'=32,'grid'=8] {'cable'}, use_global_device_ids=true, to_apply=%region_3.0 | all-reduce | flops 2048 | bytes 16384 | tf_op jit(solution)/shard_map/psum | solution.py:69
  379.5 0.6 broadcast_multiply_fusion.1
  (5 shorter events, 0.1 us)
Async XLA Ops:
  7.2 166.9 %all-reduce.2.cloned.1.call-start = ((), (), s32[]{:S(2)}) async-start(), calls=%async_computation | async-start | bytes 2097152 | tf_op jit(solution)/shard_map/psum | solution.py:53
  7.2 76.1 %copy-start = (bf16[2,256,2048]{2,1,0:T(8,128)(2,1)S(1)}, bf16[2,256,2048]{2,1,0:T(8,128)(2,1)}, u32[]{:S(2)}) copy-start(bf16[2,256,2048]{2,1,0:T(8,128)(2,1)} %param.5) | copy-start | bytes 6291460
  7.2 76.1 %copy-start.6 = (f32[2048]{0:T(1024)S(1)}, f32[2048]{0:T(1024)}, u32[]{:S(2)}) copy-start(f32[2048]{0:T(1024)} %param.6) | copy-start | bytes 24580
  7.2 48.2 %collective-permute-start = (bf16[512,2048]{1,0:T(8,128)(2,1)}, bf16[512,2048]{1,0:T(8,128)(2,1)S(1)}, u32[]{:S(2)}, u32[]{:S(2)}) collective-permute-start(bf16[512,2048]{1,0:T(8,128)(2,1)} %bitcast.36), channel_id=1, source_target_pairs={{248,0},{0,8},{8,16},{16,24},{24,32},{32,40},{40,48},{48,56},{56,6... | collective-permute-start | bytes 6291464 | tf_op jit(solution)/shard_map/ppermute | solution.py:12
  10.3 73.0 %collective-permute-start.1 = (bf16[512,2048]{1,0:T(8,128)(2,1)}, bf16[512,2048]{1,0:T(8,128)(2,1)S(1)}, u32[]{:S(2)}, u32[]{:S(2)}) collective-permute-start(bf16[512,2048]{1,0:T(8,128)(2,1)} %bitcast.37), channel_id=1, source_target_pairs={{240,0},{248,8},{0,16},{8,24},{16,32},{24,40},{32,48},{40,56},{48,... | collective-permute-start | bytes 6291464 | tf_op jit(solution)/shard_map/ppermute | solution.py:12
  55.4 3.7 copy-start.1
  83.3 1.3 copy-start.3
  84.8 1.1 copy-start.7
  84.8 1.2 copy-start.5
  177.2 96.7 %collective-permute-start.2 = (f32[512,2048]{1,0:T(8,128)S(1)}, f32[512,2048]{1,0:T(8,128)S(1)}, u32[]{:S(2)}, u32[]{:S(2)}) collective-permute-start(f32[512,2048]{1,0:T(8,128)S(1)} %fusion.13), channel_id=1, source_target_pairs={{8,0},{16,8},{24,16},{32,24},{40,32},{48,40},{56,48},{64,56},{72,6... | collective-permute-start | bytes 12582920 | tf_op jit(solution)/shard_map/ppermute | solution.py:12
  182.9 4.4 %copy-start.2 = (bf16[512,2048]{1,0:T(8,128)(2,1)S(1)}, bf16[512,2048]{1,0:T(8,128)(2,1)}, u32[]{:S(2)}) copy-start(bf16[512,2048]{1,0:T(8,128)(2,1)} %copy-done.1) | copy-start | bytes 6291460
  184.2 93.5 %collective-permute-start.3 = (f32[512,2048]{1,0:T(8,128)S(1)}, f32[512,2048]{1,0:T(8,128)S(1)}, u32[]{:S(2)}, u32[]{:S(2)}) collective-permute-start(f32[512,2048]{1,0:T(8,128)S(1)} %fusion.11), channel_id=1, source_target_pairs={{16,0},{24,8},{32,16},{40,24},{48,32},{56,40},{64,48},{72,56},{80,... | collective-permute-start | bytes 12582920 | tf_op jit(solution)/shard_map/ppermute | solution.py:12
  187.4 90.4 %copy-start.4 = (bf16[512,2048]{1,0:T(8,128)(2,1)S(1)}, bf16[512,2048]{1,0:T(8,128)(2,1)}, u32[]{:S(2)}) copy-start(bf16[512,2048]{1,0:T(8,128)(2,1)} %copy-done.3) | copy-start | bytes 6291460
Sparse Core Ops, SparseCore 0:
  86.0 88.0 all-reduce.1
where the time goes:
time: 387 us
  waiting for transfers between devices  245 us (63%)
  blocking collectives  96.4 us (25%)
  between operations  14.2 us (4%)
  matrix products  14.1 us (4%)
  starting transfers between devices  13.7 us (4%)
    ppermute x4, waiting for transfers between devices, shifted(): return lax.ppermute(block, axis, route)  157 us
    psum x1, blocking collectives, shards(): kernel = lax.psum(kernel_part, 'cable') * kernel_scale  96.4 us
    psum x1, waiting for transfers between devices, shards(): summed = lax.psum(partials, 'grid')  88 us
    ppermute x4, starting transfers between devices, shifted(): return lax.ppermute(block, axis, route)  13.6 us
  transfers between devices with their start and end apart: 5, of which 5 were waited for; matrix products, arithmetic and copies ran while one was open for 2% of the time, Pallas kernels for 0%

commit v1 on v0

v1 whole, which is shorter than its diff:
```python
import math

import jax
import jax.numpy as jnp
from jax import lax
from jax.experimental import pallas as pl
from jax.experimental.pallas import tpu as pltpu
from jax.sharding import PartitionSpec as P


CHUNK = 512


def permuted(block, axis, source_of):
    size = lax.axis_size(axis)
    return lax.ppermute(block, axis, [(source_of(i) % size, i) for i in range(size)])


def partner(i):
    return i ^ 1


def near_chip(i):
    return i + 2 if i % 2 == 0 else i - 2


def far_chip(i):
    return i - 2 if i % 2 == 0 else i + 2


def corr_kernel(par, scale, own, mate, near, out, acc):
    step = pl.program_id(0)
    even = par[0] == 0
    own_cols = own[...]
    near_cols = near[...]
    earlier = jnp.where(even, own_cols, near_cols)
    for pair, later in enumerate((mate[...], jnp.where(even, near_cols, own_cols))):
        weighted = (later.astype(jnp.float32) * scale[...]).astype(jnp.bfloat16)
        products = lax.dot_general(
            weighted, earlier, (((1,), (1,)), ((), ())), preferred_element_type=jnp.float32
        )

        @pl.when(step == 0)
        def _():
            acc[pair] = products

        @pl.when(step > 0)
        def _():
            acc[pair] += products

    @pl.when(step == pl.num_programs(0) - 1)
    def _():
        parts, _, _, rows, cols = out.shape
        half = parts * rows
        for pair in range(2):
            real = acc[pair, :half, :half] + acc[pair, half:, half:]
            imag = acc[pair, :half, half:] - acc[pair, half:, :half]
            out[:, pair, 0] = real.reshape(parts, rows, cols)
            out[:, pair, 1] = imag.reshape(parts, rows, cols)


def field_kernel(inv_norm, par, scale, mine, mate_resid, far_resid, own, mate, mate_near, near, far, adjoint, kernel_part, mat):
    step = pl.program_id(0)
    parts, rows, cols = mine.shape[0], mine.shape[3], mine.shape[4]
    half = parts * rows

    def fill(position, real, imag, flip):
        real = real.reshape(half, cols)
        imag = imag.reshape(half, cols)
        if flip:
            real = real.astype(jnp.float32).T.astype(jnp.bfloat16)
            imag = (-imag.astype(jnp.float32)).T.astype(jnp.bfloat16)
        base = position * 2 * half
        mat[:half, base : base + half] = real
        mat[half:, base + half : base + 2 * half] = real
        mat[:half, base + half : base + 2 * half] = imag
        mat[half:, base : base + half] = -imag

    @pl.when((step == 0) & (par[0] == 0))
    def _():
        fill(0, mine[:, 0, 0], mine[:, 0, 1], True)
        fill(1, mate_resid[:, 0], mate_resid[:, 1], False)
        fill(2, mine[:, 1, 0], mine[:, 1, 1], True)
        fill(3, far_resid[:, 1, 0], far_resid[:, 1, 1], False)

    @pl.when((step == 0) & (par[0] == 1))
    def _():
        fill(0, mate_resid[:, 0], mate_resid[:, 1], False)
        fill(1, far_resid[:, 0, 0], far_resid[:, 0, 1], True)
        fill(2, mine[:, 1, 0], mine[:, 1, 1], False)
        fill(3, far_resid[:, 1, 0], far_resid[:, 1, 1], True)

    fields = None
    for position, block in enumerate((mate, mate_near, near, far)):
        term = jnp.dot(
            mat[:, position * 2 * half : (position + 1) * 2 * half], block[...], preferred_element_type=jnp.float32
        )
        fields = term if fields is None else fields + term
    kernel_part[...] = 0.5 * jnp.sum(own[...].astype(jnp.float32) * fields, axis=0, keepdims=True)
    adjoint[...] = (fields * (inv_norm * scale[...])).reshape(adjoint.shape)


def correlations(par, scale, own, mate, near, parts):
    both, cols = own.shape
    half = both // 2
    block = pl.BlockSpec((both, CHUNK), lambda j: (0, j))
    return pl.pallas_call(
        corr_kernel,
        out_shape=jax.ShapeDtypeStruct((parts, 2, 2, half // parts, half), jnp.float32),
        grid=(cols // CHUNK,),
        in_specs=[
            pl.BlockSpec(memory_space=pltpu.SMEM),
            pl.BlockSpec((1, CHUNK), lambda j: (0, j)),
            block,
            block,
            block,
        ],
        out_specs=pl.BlockSpec((parts, 2, 2, half // parts, half), lambda j: (0, 0, 0, 0, 0)),
        scratch_shapes=[pltpu.VMEM((2, both, both), jnp.float32)],
        cost_estimate=pl.CostEstimate(flops=4 * both * both * cols, bytes_accessed=8 * both * cols, transcendentals=0),
        compiler_params=pltpu.CompilerParams(vmem_limit_bytes=24 << 20),
        name="corr",
    )(par, scale, own, mate, near)


def fields_of(par, scale, mine, mate_resid, far_resid, own, mate, mate_near, near, far, inv_norm):
    both, cols = own.shape
    half = both // 2
    block = pl.BlockSpec((both, CHUNK), lambda j: (0, j))

    def whole(array):
        return pl.BlockSpec(array.shape, lambda j: (0,) * array.ndim)

    def body(*refs):
        field_kernel(inv_norm, *refs)

    return pl.pallas_call(
        body,
        out_shape=(
            jax.ShapeDtypeStruct((2, half, cols), jnp.float32),
            jax.ShapeDtypeStruct((1, cols), jnp.float32),
        ),
        grid=(cols // CHUNK,),
        in_specs=[
            pl.BlockSpec(memory_space=pltpu.SMEM),
            pl.BlockSpec((1, CHUNK), lambda j: (0, j)),
            whole(mine),
            whole(mate_resid),
            whole(far_resid),
            block,
            block,
            block,
            block,
            block,
        ],
        out_specs=(
            pl.BlockSpec((2, half, CHUNK), lambda j: (0, 0, j)),
            pl.BlockSpec((1, CHUNK), lambda j: (0, j)),
        ),
        scratch_shapes=[pltpu.VMEM((both, 4 * both), jnp.bfloat16)],
        cost_estimate=pl.CostEstimate(flops=8 * both * both * cols, bytes_accessed=18 * both * cols, transcendentals=0),
        compiler_params=pltpu.CompilerParams(vmem_limit_bytes=32 << 20),
        name="fields",
    )(par, scale, mine, mate_resid, far_resid, own, mate, mate_near, near, far)


def shards(green, source_weight, observed, amp_weight, pair_used):
    row_count, col_count = green.shape[1:]
    block_count = lax.axis_size("cable")
    parts = lax.axis_size("grid")
    inv_norm = 1.0 / math.sqrt(col_count * parts)
    kernel_scale = inv_norm / (2.0 * math.sqrt(2.0 * block_count))
    parity = lax.axis_index("cable") % 2
    par = parity.reshape(1)
    scale = source_weight[None, :]
    own = green.reshape(2 * row_count, col_count)

    near = permuted(own, "cable", near_chip)
    mate = permuted(own, "cable", partner)

    slice_rows = row_count // parts
    first = lax.axis_index("grid") * slice_rows
    observed_rows = lax.dynamic_slice_in_dim(observed, first, slice_rows, 2)
    weight_rows = lax.dynamic_slice_in_dim(amp_weight, first, slice_rows, 1)
    weight_rows = weight_rows * pair_used[0].astype(jnp.float32)[:, None, None]
    packed = jnp.concatenate([observed_rows, weight_rows[:, None]], axis=1)
    data_first = permuted(packed[0], "cable", partner)
    data_second = permuted(packed[1], "cable", near_chip)
    data_second = jnp.where(parity == 0, data_second, packed[1])
    data = jnp.stack([data_first, data_second])

    partials = correlations(par, scale, own, mate, near, parts)
    far = permuted(own, "cable", far_chip)
    mate_near = permuted(near, "cable", partner)
    pieces = lax.all_to_all(partials, "grid", 0, 0, tiled=True)
    corr = inv_norm * jnp.sum(pieces, axis=0)
    resid = (data[:, 2:] * (corr - data[:, :2])).astype(jnp.bfloat16)
    mine = lax.all_to_all(jnp.broadcast_to(resid[None], (parts,) + resid.shape), "grid", 0, 0, tiled=True)
    far_resid = permuted(mine, "cable", far_chip)
    mate_resid = permuted(mine[:, 0], "cable", partner)
    adjoint, kernel_part = fields_of(
        par, scale, mine, mate_resid, far_resid, own, mate, mate_near, near, far, inv_norm
    )
    kernel = kernel_part[0] * kernel_scale
    step = 1
    while step < block_count:
        kernel = kernel + permuted(kernel, "cable", lambda i: i ^ step)
        step *= 2
    return (adjoint, kernel)


def solution(mesh):
    in_specs = (
        P(None, "cable", "grid"),
        P("grid"),
        P(None, None, "cable", None),
        P(None, "cable", None),
        P("cable", None),
    )
    out_specs = (P(None, "cable", "grid"), P("grid"))

    return jax.shard_map(shards, mesh=mesh, in_specs=in_specs, out_specs=out_specs, check_vma=False)
```

time: 387 us -> 141 us (0.36)
  waiting for transfers between devices: 245 us -> 59.5 us
  blocking collectives: 96.4 us -> 17.5 us
  starting transfers between devices: 13.7 us -> 37.1 us
  Pallas kernels: 0 us -> 15.4 us
  matrix products: 14.1 us -> 0 us
  between operations: 14.2 us -> 0.76 us
  local copies, waits for them, and re-layouts: 0.2 us -> 4.74 us
    ppermute x4 -> x13, waiting for transfers between devices: 157 us -> 59.5 us  [permuted(): lax.ppermute(block, axis, [(source_of(i) % size, i) for i in range(size)])]
    psum x1 -> x0, blocking collectives: 96.4 us -> none  [shards(): kernel = lax.psum(kernel_part, 'cable') * kernel_scale]
    psum x1 -> x0, waiting for transfers between devices: 88 us -> none  [shards(): summed = lax.psum(partials, 'grid')]
    all_to_all x0 -> x1, blocking collectives: none -> 17.5 us  [shards(): lax.all_to_all(jnp.broadcast_to(resid[None], (parts,) + resid.shape), 'gr...]
    ppermute x4 -> x13, starting transfers between devices: 13.6 us -> 30.8 us  [permuted(): lax.ppermute(block, axis, [(source_of(i) % size, i) for i in range(size)])]
    pallas_call x0 -> x2, Pallas kernels: none -> 15.4 us  [the longest x1 8.39 us: fields_of(): pl.pallas_call(body, out_shape=(jax.ShapeDtypeStruct((2, half, cols), jnp...]
    dot_general x6 -> x0, matrix products: 14.1 us -> none  [the longest x2 6.54 us: shards(): jnp.dot(resid_block, near_blocks[offset], preferred_element_type=jnp.floa...]
    all_to_all x0 -> x1, starting transfers between devices: none -> 6.35 us  [shards(): pieces = lax.all_to_all(partials, 'grid', 0, 0, tiled=True)]
  transfers between devices with their start and end apart: 5 -> 14, of which waited for: 5 -> 9; matrix products, arithmetic and copies ran while one was open for 2% -> 2% of each run, Pallas kernels for 0% -> 5%
where the time goes in v1:
time: 141 us; the launch traced here: 139 us
  waiting for transfers between devices  59.5 us (42%)
  starting transfers between devices  37.1 us (26%)
  blocking collectives  17.5 us (12%)
  Pallas kernels  15.4 us (11%)
  local copies, waits for them, and re-layouts  4.74 us (3%)
  other arithmetic  3.7 us (3%)
    ppermute x13, waiting for transfers between devices, permuted(): lax.ppermute(block, axis, [(source_of(i) % size, i) for i in range(size)])  59.5 us
    ppermute x13, starting transfers between devices, permuted(): lax.ppermute(block, axis, [(source_of(i) % size, i) for i in range(size)])  30.8 us
    all_to_all x1, blocking collectives, shards(): lax.all_to_all(jnp.broadcast_to(resid[None], (parts,) + resid.shape), 'gr...  17.5 us
    pallas_call x1, Pallas kernels, fields_of(): pl.pallas_call(body, out_shape=(jax.ShapeDtypeStruct((2, half, cols), jnp...  8.39 us
    pallas_call x1, Pallas kernels, correlations(): pl.pallas_call(corr_kernel, out_shape=jax.ShapeDtypeStruct((parts, 2, 2,...  7.03 us
    all_to_all x1, starting transfers between devices, shards(): pieces = lax.all_to_all(partials, 'grid', 0, 0, tiled=True)  6.35 us
    unnamed x16, local copies, waits for them, and re-layouts  4.66 us
  transfers between devices with their start and end apart: 14, of which 9 were waited for; matrix products, arithmetic and copies ran while one was open for 2% of the time, Pallas kernels for 5%

profile of v1, /device:TPU:1, one launch (start us, length us, event | category | flops | bytes accessed | tf_op | source)
XLA Modules:
  0.0 138.7 jit_solution(9573714142267138440)
XLA Ops:
  0.6 0.0 copy-start
  0.6 2.5 %collective-permute-start.3 = (bf16[512,2048]{1,0:T(8,128)(2,1)}, bf16[512,2048]{1,0:T(8,128)(2,1)}, u32[]{:S(2)}, u32[]{:S(2)}) collective-permute-start(bf16[512,2048]{1,0:T(8,128)(2,1)} %bitcast.21), channel_id=1, source_target_pairs={{16,0},{248,8},{32,16},{8,24},{48,32},{24,40},{64,48},{40,56},{80,... | collective-permute-start | bytes 6291464 | tf_op jit(solution)/shard_map/ppermute | solution.py:16
  3.2 5.9 %collective-permute-start.2 = (bf16[512,2048]{1,0:T(8,128)(2,1)}, bf16[512,2048]{1,0:T(8,128)(2,1)S(1)}, u32[]{:S(2)}, u32[]{:S(2)}) collective-permute-start(bf16[512,2048]{1,0:T(8,128)(2,1)} %bitcast.22), channel_id=1, source_target_pairs={{8,0},{0,8},{24,16},{16,24},{40,32},{32,40},{56,48},{48,56},{72,64... | collective-permute-start | bytes 6291464 | tf_op jit(solution)/shard_map/ppermute | solution.py:16
  9.1 0.7 collective-permute-start.7
  9.8 39.8 %collective-permute-done.3.near.refs_8_ = bf16[512,2048]{1,0:T(8,128)(2,1)} collective-permute-done((bf16[512,2048]{1,0:T(8,128)(2,1)}, bf16[512,2048]{1,0:T(8,128)(2,1)}, u32[]{:S(2)}, u32[]{:S(2)}) %collective-permute-start.3) | collective-permute-done | bytes 2097184 | tf_op jit(solution)/shard_map/ppermute | solution.py:16
  49.7 0.0 collective-permute-done.2.mate.refs_6_
  49.7 2.3 %copy-done.1 = bf16[2,256,2048]{2,1,0:T(8,128)(2,1)S(1)} copy-done((bf16[2,256,2048]{2,1,0:T(8,128)(2,1)S(1)}, bf16[2,256,2048]{2,1,0:T(8,128)(2,1)}, u32[]{:S(2)}) %copy-start.1) | copy-done | bytes 2097176
  52.0 0.7 copy-done.5
  52.7 7.0 %corr.1 = f32[8,2,2,32,256]{4,3,2,1,0:T(8,128)} custom-call(s32[1]{0:T(128)} %bitcast.par.refs_0_, f32[1,2048]{1,0:T(1,128)S(1)} %bitcast.26, bf16[512,2048]{1,0:T(8,128)(2,1)S(1)} %bitcast.24, bf16[512,2048]{1,0:T(8,128)(2,1)S(1)} %collective-permute-done.2.mate.refs_6_, bf16[512,2048]{1,0:T(8,128)(2,1)} %collective-permute-done.3.near.refs_8_), custom_call_target="tpu_custom_call" | custom-call | flops 2147483648 | bytes 8388608 | tf_op jit(solution)/shard_map/corr/pallas_call | solution.py:107
  59.7 0.0 copy-done.3
  59.7 6.4 %all-to-all-start = ((f32[8,2,2,32,256]{4,3,2,1,0:T(8,128)}), f32[8,2,2,32,256]{4,3,2,1,0:T(8,128)}, u32[]{:S(2)}, u32[]{:S(2)}) async-start(f32[8,2,2,32,256]{4,3,2,1,0:T(8,128)} %corr.1), calls=%async_computation | async-start | bytes 2097152 | tf_op jit(solution)/shard_map/all_to_all | solution.py:195
  66.1 0.0 copy-done.7
  66.1 5.6 %collective-permute-start.6 = (bf16[512,2048]{1,0:T(8,128)(2,1)}, bf16[512,2048]{1,0:T(8,128)(2,1)}, u32[]{:S(2)}, u32[]{:S(2)}) collective-permute-start(bf16[512,2048]{1,0:T(8,128)(2,1)} %collective-permute-done.3.near.refs_8_), channel_id=1, source_target_pairs={{8,0},{0,8},{24,16},{16,24},{40,32},{32,40},{56,48},{48,56},{72,64... | collective-permute-start | bytes 6291464 | tf_op jit(solution)/shard_map/ppermute | solution.py:16
  71.7 0.0 copy-done
  71.7 0.9 multiply_bitcast_fusion
  72.6 0.7 fusion.4
  73.3 0.0 collective-permute-start.1
  73.3 4.0 %collective-permute-start = (f32[3,32,256]{2,1,0:T(8,128)}, f32[3,32,256]{2,1,0:T(8,128)S(1)}, u32[]{:S(2)}, u32[]{:S(2)}) collective-permute-start(f32[3,32,256]{2,1,0:T(8,128)} %get-tuple-element.6), channel_id=1, source_target_pairs={{8,0},{0,8},{24,16},{16,24},{40,32},{32,40},{56,48},{48,56},{72,64... | collective-permute-start | bytes 294920 | tf_op jit(solution)/shard_map/ppermute | solution.py:16
  77.3 2.1 %collective-permute-done.1 = f32[3,32,256]{2,1,0:T(8,128)S(1)} collective-permute-done((f32[3,32,256]{2,1,0:T(8,128)S(1)}, f32[3,32,256]{2,1,0:T(8,128)S(1)}, u32[]{:S(2)}, u32[]{:S(2)}) %collective-permute-start.1) | collective-permute-done | bytes 98336 | tf_op jit(solution)/shard_map/ppermute | solution.py:16
  79.4 0.0 copy-start.2
  79.4 0.0 copy-start.6
  79.5 0.0 collective-permute-done
  79.5 0.0 all-to-all-done
  79.5 1.4 %reduce_sum.9 = f32[2,2,32,256]{3,2,1,0:T(8,128)S(1)} reduce(f32[8,2,2,32,256]{4,3,2,1,0:T(8,128)} %all-to-all-done, f32[]{:T(128)} %constant.30.clone.1), dimensions={0}, to_apply=%region_0.1 | reduce | flops 229376 | bytes 1179652 | tf_op jit(solution)/shard_map/reduce_sum | solution.py:196
  81.0 0.1 broadcast_in_dim.15
  81.0 17.5 %all_to_all.10.refs_2_ = bf16[8,2,2,32,256]{4,3,2,1,0:T(8,128)(2,1)S(1)} all-to-all(bf16[8,2,2,32,256]{4,3,2,1,0:T(8,128)(2,1)S(1)} %broadcast_in_dim.15), channel_id=1, replica_groups=mesh['cable'=32,'grid'=8] {'grid'}, dimensions={0} | all-to-all | bytes 1048576 | tf_op jit(solution)/shard_map/all_to_all | solution.py:198
  98.5 0.0 collective-permute-start.5
  98.5 2.3 %collective-permute-start.4 = (bf16[8,2,32,256]{3,2,1,0:T(8,128)(2,1)S(1)}, bf16[8,2,32,256]{3,2,1,0:T(8,128)(2,1)S(1)}, u32[]{:S(2)}, u32[]{:S(2)}) collective-permute-start(bf16[8,2,32,256]{3,2,1,0:T(8,128)(2,1)S(1)} %slice_bitcast_fusion), channel_id=1, source_target_pairs={{8,0},{0,8},{24,16},{16,24},{40,32},{32,40},{56,48},{48,56},{72,64... | collective-permute-start | bytes 786440 | tf_op jit(solution)/shard_map/ppermute | solution.py:16
  100.8 0.0 collective-permute-done.7.refs_9_
  100.8 1.2 collective-permute-done.4.refs_3_
  102.0 4.8 %collective-permute-done.5.refs_4_ = bf16[8,2,2,32,256]{4,3,2,1,0:T(8,128)(2,1)S(1)} collective-permute-done((bf16[8,2,2,32,256]{4,3,2,1,0:T(8,128)(2,1)S(1)}, bf16[8,2,2,32,256]{4,3,2,1,0:T(8,128)(2,1)S(1)}, u32[]{:S(2)}, u32[]{:S(2)}) %collective-permute-start.5) | collective-permute-done | bytes 524320 | tf_op jit(solution)/shard_map/ppermute | solution.py:16
  106.8 0.0 collective-permute-done.6.refs_7_
  106.8 0.0 copy-done.2
  106.8 0.0 copy-done.6
  106.8 0.0 copy-start.4
  106.8 1.6 %copy-done.4 = bf16[512,2048]{1,0:T(8,128)(2,1)S(1)} copy-done((bf16[512,2048]{1,0:T(8,128)(2,1)S(1)}, bf16[512,2048]{1,0:T(8,128)(2,1)}, u32[]{:S(2)}) %copy-start.4) | copy-done | bytes 2097176
  108.4 8.4 %fields.1 = (f32[2,256,2048]{2,1,0:T(8,128)}, f32[1,2048]{1,0:T(1,128)S(1)}) custom-call(s32[1]{0:T(128)} %bitcast.par.refs_0_, f32[1,2048]{1,0:T(1,128)S(1)} %bitcast.27, bf16[8,2,2,32,256]{4,3,2,1,0:T(8,128)(2,1)S(1)} %all_to_all.10.refs_2_, bf16[8,2,32,256]{3,2,1,0:T(8,128)(2,1)S(1)} %collective-permute-done.4.refs_3_, ...), custom_call_target="tpu_custom_call" | custom-call | flops 4294967296 | bytes 18874368 | tf_op jit(solution)/shard_map/fields/pallas_call | solution.py:137
  116.8 5.3 %collective-permute-start.8 = (f32[2048]{0:T(1024)S(1)}, f32[2048]{0:T(1024)S(1)}, u32[]{:S(2)}, u32[]{:S(2)}) collective-permute-start(f32[2048]{0:T(1024)S(1)} %bitcast.30), channel_id=1, source_target_pairs={{8,0},{0,8},{24,16},{16,24},{40,32},{32,40},{56,48},{48,56},{72,64... | collective-permute-start | bytes 24584 | tf_op jit(solution)/shard_map/ppermute | solution.py:16
  122.1 0.8 collective-permute-done.8
  122.9 0.0 collective-permute-start.9
  122.9 2.5 %collective-permute-done.9 = f32[2048]{0:T(1024)S(1)} collective-permute-done((f32[2048]{0:T(1024)S(1)}, f32[2048]{0:T(1024)S(1)}, u32[]{:S(2)}, u32[]{:S(2)}) %collective-permute-start.9) | collective-permute-done | bytes 8224 | tf_op jit(solution)/shard_map/ppermute | solution.py:16
  125.4 0.0 collective-permute-start.10
  125.4 3.4 %collective-permute-done.10 = f32[2048]{0:T(1024)S(1)} collective-permute-done((f32[2048]{0:T(1024)S(1)}, f32[2048]{0:T(1024)S(1)}, u32[]{:S(2)}, u32[]{:S(2)}) %collective-permute-start.10) | collective-permute-done | bytes 8224 | tf_op jit(solution)/shard_map/ppermute | solution.py:16
  128.8 4.0 %collective-permute-start.11 = (f32[2048]{0:T(1024)S(1)}, f32[2048]{0:T(1024)S(1)}, u32[]{:S(2)}, u32[]{:S(2)}) collective-permute-start(f32[2048]{0:T(1024)S(1)} %add.27), channel_id=1, source_target_pairs={{64,0},{72,8},{80,16},{88,24},{96,32},{104,40},{112,48},{120,56},{... | collective-permute-start | bytes 24584 | tf_op jit(solution)/shard_map/ppermute | solution.py:16
  132.9 2.4 %collective-permute-done.11 = f32[2048]{0:T(1024)S(1)} collective-permute-done((f32[2048]{0:T(1024)S(1)}, f32[2048]{0:T(1024)S(1)}, u32[]{:S(2)}, u32[]{:S(2)}) %collective-permute-start.11) | collective-permute-done | bytes 8224 | tf_op jit(solution)/shard_map/ppermute | solution.py:16
  135.3 0.3 collective-permute-start.12
  135.6 2.5 %collective-permute-done.12 = f32[2048]{0:T(1024)S(1)} collective-permute-done((f32[2048]{0:T(1024)S(1)}, f32[2048]{0:T(1024)S(1)}, u32[]{:S(2)}, u32[]{:S(2)}) %collective-permute-start.12) | collective-permute-done | bytes 8224 | tf_op jit(solution)/shard_map/ppermute | solution.py:16
  138.1 0.6 add.29
  (15 shorter events, 0.1 us)
Async XLA Ops:
  0.6 71.1 %copy-start = (f32[2,2,256,256]{3,2,1,0:T(8,128)S(1)}, f32[2,2,256,256]{3,2,1,0:T(8,128)}, u32[]{:S(2)}) copy-start(f32[2,2,256,256]{3,2,1,0:T(8,128)} %param.7) | copy-start | bytes 3145732
  0.6 49.0 %collective-permute-start.3 = (bf16[512,2048]{1,0:T(8,128)(2,1)}, bf16[512,2048]{1,0:T(8,128)(2,1)}, u32[]{:S(2)}, u32[]{:S(2)}) collective-permute-start(bf16[512,2048]{1,0:T(8,128)(2,1)} %bitcast.21), channel_id=1, source_target_pairs={{16,0},{248,8},{32,16},{8,24},{48,32},{24,40},{64,48},{40,56},{80,... | collective-permute-start | bytes 6291464 | tf_op jit(solution)/shard_map/ppermute | solution.py:16
  3.2 46.5 %collective-permute-start.2 = (bf16[512,2048]{1,0:T(8,128)(2,1)}, bf16[512,2048]{1,0:T(8,128)(2,1)S(1)}, u32[]{:S(2)}, u32[]{:S(2)}) collective-permute-start(bf16[512,2048]{1,0:T(8,128)(2,1)} %bitcast.22), channel_id=1, source_target_pairs={{8,0},{0,8},{24,16},{16,24},{40,32},{32,40},{56,48},{48,56},{72,64... | collective-permute-start | bytes 6291464 | tf_op jit(solution)/shard_map/ppermute | solution.py:16
  9.1 91.7 %collective-permute-start.7 = (bf16[512,2048]{1,0:T(8,128)(2,1)}, bf16[512,2048]{1,0:T(8,128)(2,1)}, u32[]{:S(2)}, u32[]{:S(2)}) collective-permute-start(bf16[512,2048]{1,0:T(8,128)(2,1)} %bitcast.23), channel_id=1, source_target_pairs={{240,0},{24,8},{0,16},{40,24},{16,32},{56,40},{32,48},{72,56},{48,... | collective-permute-start | bytes 6291464 | tf_op jit(solution)/shard_map/ppermute | solution.py:16
  49.7 10.1 %copy-start.3 = (bf16[512,2048]{1,0:T(8,128)(2,1)}, bf16[512,2048]{1,0:T(8,128)(2,1)S(1)}, u32[]{:S(2)}) copy-start(bf16[512,2048]{1,0:T(8,128)(2,1)S(1)} %collective-permute-done.2.mate.refs_6_) | copy-start | bytes 6291460
  49.7 2.3 %copy-start.1 = (bf16[2,256,2048]{2,1,0:T(8,128)(2,1)S(1)}, bf16[2,256,2048]{2,1,0:T(8,128)(2,1)}, u32[]{:S(2)}) copy-start(bf16[2,256,2048]{2,1,0:T(8,128)(2,1)} %param.5) | copy-start | bytes 6291460
  52.0 0.7 copy-start.5
  52.7 13.4 %copy-start.7 = (s32[1,2]{1,0:T(1,128)S(1)}, s32[1,2]{1,0:T(1,128)}, u32[]{:S(2)}) copy-start(s32[1,2]{1,0:T(1,128)} %param.9) | copy-start | bytes 28
  59.7 19.8 %all-to-all-start = ((f32[8,2,2,32,256]{4,3,2,1,0:T(8,128)}), f32[8,2,2,32,256]{4,3,2,1,0:T(8,128)}, u32[]{:S(2)}, u32[]{:S(2)}) async-start(f32[8,2,2,32,256]{4,3,2,1,0:T(8,128)} %corr.1), calls=%async_computation | async-start | bytes 2097152 | tf_op jit(solution)/shard_map/all_to_all | solution.py:195
  66.1 40.7 %collective-permute-start.6 = (bf16[512,2048]{1,0:T(8,128)(2,1)}, bf16[512,2048]{1,0:T(8,128)(2,1)}, u32[]{:S(2)}, u32[]{:S(2)}) collective-permute-start(bf16[512,2048]{1,0:T(8,128)(2,1)} %collective-permute-done.3.near.refs_8_), channel_id=1, source_target_pairs={{8,0},{0,8},{24,16},{16,24},{40,32},{32,40},{56,48},{48,56},{72,64... | collective-permute-start | bytes 6291464 | tf_op jit(solution)/shard_map/ppermute | solution.py:16
  73.3 6.1 %collective-permute-start.1 = (f32[3,32,256]{2,1,0:T(8,128)S(1)}, f32[3,32,256]{2,1,0:T(8,128)S(1)}, u32[]{:S(2)}, u32[]{:S(2)}) collective-permute-start(f32[3,32,256]{2,1,0:T(8,128)S(1)} %get-tuple-element.7), channel_id=1, source_target_pairs={{16,0},{248,8},{32,16},{8,24},{48,32},{24,40},{64,48},{40,56},{80,... | collective-permute-start | bytes 294920 | tf_op jit(solution)/shard_map/ppermute | solution.py:16
  73.3 6.2 %collective-permute-start = (f32[3,32,256]{2,1,0:T(8,128)}, f32[3,32,256]{2,1,0:T(8,128)S(1)}, u32[]{:S(2)}, u32[]{:S(2)}) collective-permute-start(f32[3,32,256]{2,1,0:T(8,128)} %get-tuple-element.6), channel_id=1, source_target_pairs={{8,0},{0,8},{24,16},{16,24},{40,32},{32,40},{56,48},{48,56},{72,64... | collective-permute-start | bytes 294920 | tf_op jit(solution)/shard_map/ppermute | solution.py:16
  79.4 27.4 %copy-start.2 = (bf16[2,256,2048]{2,1,0:T(8,128)(2,1)S(1)}, bf16[2,256,2048]{2,1,0:T(8,128)(2,1)}, u32[]{:S(2)}) copy-start(bf16[2,256,2048]{2,1,0:T(8,128)(2,1)} %param.5) | copy-start | bytes 6291460
  79.4 27.4 %copy-start.6 = (f32[2048]{0:T(1024)S(1)}, f32[2048]{0:T(1024)}, u32[]{:S(2)}) copy-start(f32[2048]{0:T(1024)} %param.6) | copy-start | bytes 24580
  98.5 8.3 %collective-permute-start.5 = (bf16[8,2,2,32,256]{4,3,2,1,0:T(8,128)(2,1)S(1)}, bf16[8,2,2,32,256]{4,3,2,1,0:T(8,128)(2,1)S(1)}, u32[]{:S(2)}, u32[]{:S(2)}) collective-permute-start(bf16[8,2,2,32,256]{4,3,2,1,0:T(8,128)(2,1)S(1)} %all_to_all.10.refs_2_), channel_id=1, source_target_pairs={{240,0},{24,8},{0,16},{40,24},{16,32},{56,40},{32,48},{72,56},{48,... | collective-permute-start | bytes 1572872 | tf_op jit(solution)/shard_map/ppermute | solution.py:16
  98.5 3.5 %collective-permute-start.4 = (bf16[8,2,32,256]{3,2,1,0:T(8,128)(2,1)S(1)}, bf16[8,2,32,256]{3,2,1,0:T(8,128)(2,1)S(1)}, u32[]{:S(2)}, u32[]{:S(2)}) collective-permute-start(bf16[8,2,32,256]{3,2,1,0:T(8,128)(2,1)S(1)} %slice_bitcast_fusion), channel_id=1, source_target_pairs={{8,0},{0,8},{24,16},{16,24},{40,32},{32,40},{56,48},{48,56},{72,64... | collective-permute-start | bytes 786440 | tf_op jit(solution)/shard_map/ppermute | solution.py:16
  106.8 1.6 %copy-start.4 = (bf16[512,2048]{1,0:T(8,128)(2,1)S(1)}, bf16[512,2048]{1,0:T(8,128)(2,1)}, u32[]{:S(2)}) copy-start(bf16[512,2048]{1,0:T(8,128)(2,1)} %copy-done.3) | copy-start | bytes 6291460
  116.8 6.1 %collective-permute-start.8 = (f32[2048]{0:T(1024)S(1)}, f32[2048]{0:T(1024)S(1)}, u32[]{:S(2)}, u32[]{:S(2)}) collective-permute-start(f32[2048]{0:T(1024)S(1)} %bitcast.30), channel_id=1, source_target_pairs={{8,0},{0,8},{24,16},{16,24},{40,32},{32,40},{56,48},{48,56},{72,64... | collective-permute-start | bytes 24584 | tf_op jit(solution)/shard_map/ppermute | solution.py:16
  122.9 2.5 %collective-permute-start.9 = (f32[2048]{0:T(1024)S(1)}, f32[2048]{0:T(1024)S(1)}, u32[]{:S(2)}, u32[]{:S(2)}) collective-permute-start(f32[2048]{0:T(1024)S(1)} %add.25), channel_id=1, source_target_pairs={{16,0},{24,8},{0,16},{8,24},{48,32},{56,40},{32,48},{40,56},{80,64... | collective-permute-start | bytes 24584 | tf_op jit(solution)/shard_map/ppermute | solution.py:16
  125.4 3.4 %collective-permute-start.10 = (f32[2048]{0:T(1024)S(1)}, f32[2048]{0:T(1024)S(1)}, u32[]{:S(2)}, u32[]{:S(2)}) collective-permute-start(f32[2048]{0:T(1024)S(1)} %add.26), channel_id=1, source_target_pairs={{32,0},{40,8},{48,16},{56,24},{0,32},{8,40},{16,48},{24,56},{96,64... | collective-permute-start | bytes 24584 | tf_op jit(solution)/shard_map/ppermute | solution.py:16
  128.8 6.4 %collective-permute-start.11 = (f32[2048]{0:T(1024)S(1)}, f32[2048]{0:T(1024)S(1)}, u32[]{:S(2)}, u32[]{:S(2)}) collective-permute-start(f32[2048]{0:T(1024)S(1)} %add.27), channel_id=1, source_target_pairs={{64,0},{72,8},{80,16},{88,24},{96,32},{104,40},{112,48},{120,56},{... | collective-permute-start | bytes 24584 | tf_op jit(solution)/shard_map/ppermute | solution.py:16
  135.3 2.8 %collective-permute-start.12 = (f32[2048]{0:T(1024)S(1)}, f32[2048]{0:T(1024)S(1)}, u32[]{:S(2)}, u32[]{:S(2)}) collective-permute-start(f32[2048]{0:T(1024)S(1)} %add.28), channel_id=1, source_target_pairs={{128,0},{136,8},{144,16},{152,24},{160,32},{168,40},{176,48},{184,... | collective-permute-start | bytes 24584 | tf_op jit(solution)/shard_map/ppermute | solution.py:16

commit v2 on v1

v2 whole, which is shorter than its diff:
```python
import math

import jax
import jax.numpy as jnp
from jax import lax
from jax.experimental import pallas as pl
from jax.experimental.pallas import tpu as pltpu
from jax.sharding import PartitionSpec as P


CHUNK = 512
HALVES = 2
WIRE = jnp.float32


def permuted(block, axis, source_of):
    size = lax.axis_size(axis)
    return lax.ppermute(block, axis, [(source_of(i) % size, i) for i in range(size)])


def partner(i):
    return i ^ 1


def near_chip(i):
    return i + 2 if i % 2 == 0 else i - 2


def far_chip(i):
    return i - 2 if i % 2 == 0 else i + 2


def whole(array):
    return pl.BlockSpec(array.shape, lambda j: (0,) * array.ndim)


def prep_kernel(par, used, first, observed, amp_weight, natural, second, square):
    rows = natural.shape[1]
    at = pl.ds(pl.multiple_of(first[0], rows), rows)
    masks = [used[0, o].astype(jnp.float32) for o in range(2)]
    natural[:2] = observed[0, :, at, :]
    natural[2] = amp_weight[0, at, :] * masks[0]

    @pl.when(par[0] == 0)
    def _():
        square[0] = observed[1, 0].T
        square[1] = -observed[1, 1].T
        square[2] = amp_weight[1].T * masks[1]
        second[...] = square[:, at, :]

    @pl.when(par[0] == 1)
    def _():
        second[:2] = observed[1, :, at, :]
        second[2] = amp_weight[1, at, :] * masks[1]


def prepared(par, used, first, observed, amp_weight, slice_rows):
    cols = amp_weight.shape[2]
    packed = (3, slice_rows, cols)
    smem = pl.BlockSpec(memory_space=pltpu.SMEM)
    return pl.pallas_call(
        prep_kernel,
        out_shape=(jax.ShapeDtypeStruct(packed, jnp.float32),) * 2,
        grid=(1,),
        in_specs=[smem, smem, smem, whole(observed), whole(amp_weight)],
        out_specs=(pl.BlockSpec(packed, lambda j: (0, 0, 0)),) * 2,
        scratch_shapes=[pltpu.VMEM((3, cols, cols), jnp.float32)],
        cost_estimate=pl.CostEstimate(flops=0, bytes_accessed=8 << 20, transcendentals=0),
        compiler_params=pltpu.CompilerParams(vmem_limit_bytes=8 << 20),
        name="prep",
    )(par, used, first, observed, amp_weight)


def resid_kernel(inv_norm, pieces, data, out):
    total = pieces[0].astype(jnp.float32)
    for part in range(1, pieces.shape[0]):
        total = total + pieces[part].astype(jnp.float32)
    resid = (data[:, 2:] * (inv_norm * total - data[:, :2])).astype(jnp.bfloat16)
    for part in range(out.shape[0]):
        out[part] = resid


def residuals(pieces, data, inv_norm, position):
    def body(*refs):
        resid_kernel(inv_norm, *refs)

    rows, cols = pieces.shape[3:]
    return pl.pallas_call(
        body,
        out_shape=jax.ShapeDtypeStruct(pieces.shape, jnp.bfloat16),
        grid=(1,),
        in_specs=[whole(pieces), pl.BlockSpec((2, 3, rows, cols), lambda j: (0, 0, 0, position))],
        out_specs=whole(pieces),
        cost_estimate=pl.CostEstimate(flops=0, bytes_accessed=2 << 20, transcendentals=0),
        compiler_params=pltpu.CompilerParams(vmem_limit_bytes=6 << 20),
        name="resid",
    )(pieces, data)


def corr_kernel(par, scale, lhs_first, lhs_second, own, near, out, acc):
    step = pl.program_id(0)
    even = par[0] == 0
    near_cols = near[...].reshape(-1, near.shape[2])
    rhs_first = jnp.where(even, own[...].reshape(near_cols.shape), near_cols)
    near_scale = jnp.where(even, scale[...], 1.0)
    rhs_second = (near_cols.astype(jnp.float32) * near_scale).astype(jnp.bfloat16)
    for pair, (lhs, rhs) in enumerate(((lhs_first, rhs_first), (lhs_second, rhs_second))):
        products = lax.dot_general(lhs[...], rhs, (((1,), (1,)), ((), ())), preferred_element_type=jnp.float32)

        @pl.when(step == 0)
        def _():
            acc[pair] = products

        @pl.when(step > 0)
        def _():
            acc[pair] += products

    @pl.when(step == pl.num_programs(0) - 1)
    def _():
        parts, _, _, rows, cols = out.shape
        half = parts * rows
        for pair in range(2):
            real = acc[pair, :half, :cols] + acc[pair, half:, cols:]
            imag = acc[pair, :half, cols:] - acc[pair, half:, :cols]
            out[:, pair, 0] = real.reshape(parts, rows, cols).astype(out.dtype)
            out[:, pair, 1] = imag.reshape(parts, rows, cols).astype(out.dtype)


def correlations(par, scale, lhs_first, lhs_second, green, near, parts, position):
    both, cols = lhs_first.shape
    half = both // 2
    part = half // HALVES
    lhs_block = pl.BlockSpec((both, CHUNK), lambda j: (0, j))
    out_shape = (parts, 2, 2, half // parts, part)
    return pl.pallas_call(
        corr_kernel,
        out_shape=jax.ShapeDtypeStruct(out_shape, WIRE),
        grid=(cols // CHUNK,),
        in_specs=[
            pl.BlockSpec(memory_space=pltpu.SMEM),
            pl.BlockSpec((1, CHUNK), lambda j: (0, j)),
            lhs_block,
            lhs_block,
            pl.BlockSpec((2, part, CHUNK), lambda j: (0, position, j)),
            pl.BlockSpec((2, part, CHUNK), lambda j: (0, 0, j)),
        ],
        out_specs=pl.BlockSpec(out_shape, lambda j: (0, 0, 0, 0, 0)),
        scratch_shapes=[pltpu.VMEM((2, both, 2 * part), jnp.float32)],
        cost_estimate=pl.CostEstimate(
            flops=8 * both * part * cols, bytes_accessed=4 * (both + part) * cols, transcendentals=0
        ),
        compiler_params=pltpu.CompilerParams(vmem_limit_bytes=20 << 20),
        name="corr",
    )(par, scale, lhs_first, lhs_second, green, near)


def assembled(pieces, pair, turned):
    square = []
    for component in range(2):
        strips = [piece[:, pair, component] for piece in pieces]
        strips = [strip.reshape(-1, strip.shape[-1]) for strip in strips]
        square.append(jnp.concatenate(strips, axis=1))
    real, imag = square
    if turned:
        real = real.astype(jnp.float32).T.astype(jnp.bfloat16)
        imag = (-imag.astype(jnp.float32)).T.astype(jnp.bfloat16)
    return real, imag


def place(mat, base, block, strips):
    real, imag = block
    half = real.shape[0]
    width = half // strips
    for strip in range(strips):
        x = real[:, strip * width : (strip + 1) * width]
        y = imag[:, strip * width : (strip + 1) * width]
        at = base + 2 * width * strip
        mat[:half, at : at + width] = x
        mat[half:, at + width : at + 2 * width] = x
        mat[:half, at + width : at + 2 * width] = y
        mat[half:, at : at + width] = -y


def applied(mat, base, pieces):
    total = None
    for piece in pieces:
        block = piece[...].reshape(-1, piece.shape[-1])
        term = jnp.dot(mat[:, base : base + block.shape[0]], block, preferred_element_type=jnp.float32)
        total = term if total is None else total + term
        base += block.shape[0]
    return total


def early_kernel(par, *refs):
    mine = refs[:HALVES]
    mate_resid = refs[HALVES : 2 * HALVES]
    own, mate = refs[2 * HALVES : 2 * HALVES + 2]
    near = refs[2 * HALVES + 2 : 3 * HALVES + 2]
    mate_near = refs[3 * HALVES + 2 : 4 * HALVES + 2]
    early, kernel_part, mat = refs[4 * HALVES + 2 :]
    first = pl.program_id(0) == 0
    even = par[0] == 0
    both = early.shape[0]

    @pl.when(first)
    def _():
        place(mat, 0, assembled(mine, 1, False), HALVES)

    @pl.when(first & even)
    def _():
        place(mat, both, assembled(mine, 0, True), 1)
        place(mat, 2 * both, assembled(mate_resid, 0, False), HALVES)

    @pl.when(first & jnp.logical_not(even))
    def _():
        place(mat, both, assembled(mate_resid, 0, False), 1)

    def finish(term):
        mate_term = applied(mat, both, (mate,))
        own_cols = own[...].astype(jnp.float32)
        kernel_part[...] = jnp.sum(own_cols * (term + 0.5 * mate_term), axis=0, keepdims=True)
        early[...] = term + mate_term

    @pl.when(even)
    def _():
        finish(applied(mat, 0, near) + applied(mat, 2 * both, mate_near))

    @pl.when(jnp.logical_not(even))
    def _():
        finish(applied(mat, 0, near))


def late_kernel(inv_norm, par, scale, *refs):
    far_resid = refs[:HALVES]
    far, early = refs[HALVES : HALVES + 2]
    mate_near = refs[HALVES + 2 : 2 * HALVES + 2]
    adjoint, mat = refs[2 * HALVES + 2 :]
    first = pl.program_id(0) == 0
    even = par[0] == 0
    both = early.shape[0]

    @pl.when(first)
    def _():
        place(mat, 0, assembled(far_resid, 1, True), 1)

    @pl.when(first & jnp.logical_not(even))
    def _():
        place(mat, both, assembled(far_resid, 0, True), HALVES)

    def finish(term):
        fields = early[...] + term
        adjoint[...] = (fields * (inv_norm * scale[...])).reshape(adjoint.shape)

    @pl.when(even)
    def _():
        finish(applied(mat, 0, (far,)))

    @pl.when(jnp.logical_not(even))
    def _():
        finish(applied(mat, 0, (far,)) + applied(mat, both, mate_near))


def column_block(array):
    shape = array.shape[:-1] + (CHUNK,)
    return pl.BlockSpec(shape, lambda j: (0,) * (array.ndim - 1) + (j,))


def early_fields(par, mine, mate_resid, own, mate, near, mate_near):
    both, cols = own.shape
    wholes = (*mine, *mate_resid)
    blocks = (own, mate, *near, *mate_near)
    return pl.pallas_call(
        early_kernel,
        out_shape=(
            jax.ShapeDtypeStruct((both, cols), jnp.float32),
            jax.ShapeDtypeStruct((1, cols), jnp.float32),
        ),
        grid=(cols // CHUNK,),
        in_specs=[pl.BlockSpec(memory_space=pltpu.SMEM)] + [whole(x) for x in wholes] + [column_block(x) for x in blocks],
        out_specs=(
            pl.BlockSpec((both, CHUNK), lambda j: (0, j)),
            pl.BlockSpec((1, CHUNK), lambda j: (0, j)),
        ),
        scratch_shapes=[pltpu.VMEM((both, 3 * both), jnp.bfloat16)],
        cost_estimate=pl.CostEstimate(flops=6 * both * both * cols, bytes_accessed=12 * both * cols, transcendentals=0),
        compiler_params=pltpu.CompilerParams(vmem_limit_bytes=24 << 20),
        name="early",
    )(par, *wholes, *blocks)


def late_fields(par, scale, far_resid, far, early, mate_near, inv_norm):
    both, cols = early.shape
    blocks = (far, early, *mate_near)

    def body(*refs):
        late_kernel(inv_norm, *refs)

    return pl.pallas_call(
        body,
        out_shape=jax.ShapeDtypeStruct((2, both // 2, cols), jnp.float32),
        grid=(cols // CHUNK,),
        in_specs=[pl.BlockSpec(memory_space=pltpu.SMEM), column_block(scale)]
        + [whole(x) for x in far_resid]
        + [column_block(x) for x in blocks],
        out_specs=pl.BlockSpec((2, both // 2, CHUNK), lambda j: (0, 0, j)),
        scratch_shapes=[pltpu.VMEM((both, 2 * both), jnp.bfloat16)],
        cost_estimate=pl.CostEstimate(flops=4 * both * both * cols, bytes_accessed=12 * both * cols, transcendentals=0),
        compiler_params=pltpu.CompilerParams(vmem_limit_bytes=24 << 20),
        name="late",
    )(par, scale, *far_resid, *blocks)


def shards(green, source_weight, observed, amp_weight, pair_used):
    row_count, col_count = green.shape[1:]
    block_count = lax.axis_size("cable")
    parts = lax.axis_size("grid")
    inv_norm = 1.0 / math.sqrt(col_count * parts)
    kernel_scale = inv_norm / (2.0 * math.sqrt(2.0 * block_count))
    parity = lax.axis_index("cable") % 2
    even = parity == 0
    par = parity.reshape(1)
    scale = source_weight[None, :]
    own = green.reshape(2 * row_count, col_count)
    width = row_count // HALVES

    near = []
    for half in range(HALVES):
        near.append(permuted(green[:, half * width : (half + 1) * width], "cable", near_chip))
    mate = permuted(own, "cable", partner)

    slice_rows = row_count // parts
    first = lax.axis_index("grid") * slice_rows
    packed = prepared(par, pair_used, first.reshape(1), observed, amp_weight, slice_rows)
    data_first = permuted(packed[0], "cable", partner)
    data_second = permuted(packed[1], "cable", near_chip)
    data = jnp.stack([data_first, jnp.where(even, data_second, packed[1])])

    lhs_first = (mate.astype(jnp.float32) * scale).astype(jnp.bfloat16)
    lhs_second = (own.astype(jnp.float32) * jnp.where(even, 1.0, scale)).astype(jnp.bfloat16)
    near[0], data, lhs_first, lhs_second = lax.optimization_barrier((near[0], data, lhs_first, lhs_second))

    partials = []
    for half in range(HALVES):
        partials.append(correlations(par, scale, lhs_first, lhs_second, green, near[half], parts, half))
    far = permuted(own, "cable", far_chip)
    mate_near = []
    for half in range(HALVES):
        mate_near.append(permuted(near[half], "cable", partner))
    mine, mate_resid, far_resid = [], [], []
    for half in range(HALVES):
        pieces = lax.all_to_all(partials[half], "grid", 0, 0, tiled=True)
        resid = residuals(pieces, data, inv_norm, half)
        gathered = lax.all_to_all(resid, "grid", 0, 0, tiled=True)
        mine.append(gathered)
        mate_resid.append(permuted(gathered[:, :1], "cable", partner))
        far_resid.append(permuted(gathered, "cable", far_chip))
    early, kernel_part = early_fields(par, mine, mate_resid, own, mate, near, mate_near)
    kernel = kernel_part[0] * kernel_scale
    adjoint = late_fields(par, scale, far_resid, far, early, mate_near, inv_norm)
    step = 1
    while step < block_count:
        kernel = kernel + permuted(kernel, "cable", lambda i: i ^ step)
        step *= 2
    return (adjoint, kernel)


def solution(mesh):
    in_specs = (
        P(None, "cable", "grid"),
        P("grid"),
        P(None, None, "cable", None),
        P(None, "cable", None),
        P("cable", None),
    )
    out_specs = (P(None, "cable", "grid"), P("grid"))

    return jax.shard_map(shards, mesh=mesh, in_specs=in_specs, out_specs=out_specs, check_vma=False)
```

time: 141 us -> 162 us (1.15)
  starting transfers between devices: 37.1 us -> 57.5 us
  blocking collectives: 17.5 us -> 0 us
  Pallas kernels: 15.4 us -> 24.8 us
  local copies, waits for them, and re-layouts: 4.74 us -> 13.7 us
    all_to_all x1 -> x4, starting transfers between devices: 6.35 us -> 35.7 us  [the longest x2 28.9 us: shards(): pieces = lax.all_to_all(partials[half], 'grid', 0, 0, tiled=True)]
    ppermute x13 -> x17, waiting for transfers between devices: 59.5 us -> 33.4 us  [permuted(): lax.ppermute(block, axis, [(source_of(i) % size, i) for i in range(size)])]
    all_to_all x1 -> x4, waiting for transfers between devices: 0.01 us -> 24.7 us  [the longest x2 13.5 us: shards(): pieces = lax.all_to_all(partials[half], 'grid', 0, 0, tiled=True)]
    all_to_all x1 -> x0, blocking collectives: 17.5 us -> none  [shards(): lax.all_to_all(jnp.broadcast_to(resid[None], (parts,) + resid.shape), 'gr...]
    pallas_call x2 -> x7, Pallas kernels: 15.4 us -> 24.8 us  [the longest x2 11.5 us: correlations(): pl.pallas_call(corr_kernel, out_shape=jax.ShapeDtypeStruct(out_shape, WIR...]
    ppermute x13 -> x17, starting transfers between devices: 30.8 us -> 21.8 us  [permuted(): lax.ppermute(block, axis, [(source_of(i) % size, i) for i in range(size)])]
    unnamed x16 -> x26, local copies, waits for them, and re-layouts: 4.66 us -> 10.6 us
    convert_element_type x2, other arithmetic: 0.03 us -> 3.3 us  [the longest x1 2.72 us: shards(): lhs_first = (mate.astype(jnp.float32) * scale).astype(jnp.bfloat16)]
  transfers between devices with their start and end apart: 14 -> 21, of which waited for: 9 -> 10; matrix products, arithmetic and copies ran while one was open for 2% -> 4% of each run, Pallas kernels for 5% -> 12%
where the time goes in v2:
time: 162 us; the launch traced here: 159 us
  waiting for transfers between devices  58.1 us (36%)
  starting transfers between devices  57.5 us (35%)
  Pallas kernels  24.8 us (15%)
  local copies, waits for them, and re-layouts  13.7 us (8%)
  other arithmetic  3.96 us (2%)
    ppermute x17, waiting for transfers between devices, permuted(): lax.ppermute(block, axis, [(source_of(i) % size, i) for i in range(size)])  33.4 us
    all_to_all x2, starting transfers between devices, shards(): pieces = lax.all_to_all(partials[half], 'grid', 0, 0, tiled=True)  28.9 us
    ppermute x17, starting transfers between devices, permuted(): lax.ppermute(block, axis, [(source_of(i) % size, i) for i in range(size)])  21.8 us
    all_to_all x2, waiting for transfers between devices, shards(): pieces = lax.all_to_all(partials[half], 'grid', 0, 0, tiled=True)  13.5 us
    pallas_call x2, Pallas kernels, correlations(): pl.pallas_call(corr_kernel, out_shape=jax.ShapeDtypeStruct(out_shape, WIR...  11.5 us
    all_to_all x2, waiting for transfers between devices, shards(): gathered = lax.all_to_all(resid, 'grid', 0, 0, tiled=True)  11.2 us
    unnamed x26, local copies, waits for them, and re-layouts  10.6 us
    all_to_all x2, starting transfers between devices, shards(): gathered = lax.all_to_all(resid, 'grid', 0, 0, tiled=True)  6.82 us
  transfers between devices with their start and end apart: 21, of which 10 were waited for; matrix products, arithmetic and copies ran while one was open for 4% of the time, Pallas kernels for 12%

profile of v2, /device:TPU:1, one launch (start us, length us, event | category | flops | bytes accessed | tf_op | source)
XLA Modules:
  0.0 158.9 jit_solution(12050654682806874728)
XLA Ops:
  0.6 3.3 %collective-permute-start.3 = (bf16[512,2048]{1,0:T(8,128)(2,1)}, bf16[512,2048]{1,0:T(8,128)(2,1)}, u32[]{:S(2)}, u32[]{:S(2)}) collective-permute-start(bf16[512,2048]{1,0:T(8,128)(2,1)} %bitcast.9), channel_id=1, source_target_pairs={{8,0},{0,8},{24,16},{16,24},{40,32},{32,40},{56,48},{48,56},{72,64... | collective-permute-start | bytes 6291464 | tf_op jit(solution)/shard_map/ppermute | solution.py:18
  3.9 1.2 copy-done.8
  5.1 1.0 copy-done.10
  6.2 0.7 copy-done.12
  6.8 0.6 prep.1
  7.4 0.1 collective-permute-start.2
  7.5 0.0 copy-start
  7.5 5.4 %collective-permute-start.1 = (f32[3,32,256]{2,1,0:T(8,128)S(1)}, f32[3,32,256]{2,1,0:T(8,128)S(1)}, u32[]{:S(2)}, u32[]{:S(2)}) collective-permute-start(f32[3,32,256]{2,1,0:T(8,128)S(1)} %get-tuple-element.10), channel_id=1, source_target_pairs={{8,0},{0,8},{24,16},{16,24},{40,32},{32,40},{56,48},{48,56},{72,64... | collective-permute-start | bytes 294920 | tf_op jit(solution)/shard_map/ppermute | solution.py:18
  12.9 3.1 %fusion = (bf16[2,128,2048]{2,1,0:T(8,128)(2,1)}, bf16[2,128,2048]{2,1,0:T(8,128)(2,1)}) fusion(bf16[2,256,2048]{2,1,0:T(8,128)(2,1)} %own.3), kind=kLoop, calls=%fused_computation.6 | loop fusion | bytes 4194304 | tf_op jit(solution)/shard_map/slice | solution.py:328
  16.1 0.6 multiply_convert_fusion.lhs_second
  16.8 2.7 %multiply_convert_fusion.1.lhs_first = bf16[512,2048]{1,0:T(8,128)(2,1)S(1)} fusion(bf16[512,2048]{1,0:T(8,128)(2,1)} %collective-permute-done.3.refs_5_, f32[2048]{0:T(1024)S(1)} %copy-done.11), kind=kLoop, calls=%fused_computation.1 | loop fusion | flops 3145728 | bytes 4202496 | tf_op jit(solution)/shard_map/convert_element_type | solution.py:338
  19.5 12.5 %collective-permute-done.near.refs_6_ = bf16[2,128,2048]{2,1,0:T(8,128)(2,1)S(1)} collective-permute-done((bf16[2,128,2048]{2,1,0:T(8,128)(2,1)}, bf16[2,128,2048]{2,1,0:T(8,128)(2,1)S(1)}, u32[]{:S(2)}, u32[]{:S(2)}) %collective-permute-start) | collective-permute-done | bytes 1048608 | tf_op jit(solution)/shard_map/ppermute | solution.py:18
  32.0 11.3 %collective-permute-done.5.near.refs_7_ = bf16[2,128,2048]{2,1,0:T(8,128)(2,1)} collective-permute-done((bf16[2,128,2048]{2,1,0:T(8,128)(2,1)}, bf16[2,128,2048]{2,1,0:T(8,128)(2,1)}, u32[]{:S(2)}, u32[]{:S(2)}) %collective-permute-start.5) | collective-permute-done | bytes 1048608 | tf_op jit(solution)/shard_map/ppermute | solution.py:18
  43.4 6.1 %corr.3 = f32[8,2,2,32,128]{4,3,2,1,0:T(8,128)} custom-call(s32[1]{0:T(128)} %bitcast.par.refs_0_, f32[1,2048]{1,0:T(1,128)S(1)} %bitcast.12, bf16[512,2048]{1,0:T(8,128)(2,1)S(1)} %multiply_convert_fusion.1.lhs_first, bf16[512,2048]{1,0:T(8,128)(2,1)S(1)} %multiply_convert_fusion.lhs_second, bf16[2,256,2048]{2,1,0:T(8,128)(2,1)S(1)} %copy-done, ...), custom_call_target="tpu_custom_call" | custom-call | flops 1073741824 | bytes 5242880 | tf_op jit(solution)/shard_map/corr/pallas_call | solution.py:135
  49.5 1.3 copy-done.3
  50.8 6.4 %all-to-all-start.2 = ((f32[8,2,2,32,128]{4,3,2,1,0:T(8,128)}), f32[8,2,2,32,128]{4,3,2,1,0:T(8,128)S(1)}, u32[]{:S(2)}, u32[]{:S(2)}) async-start(f32[8,2,2,32,128]{4,3,2,1,0:T(8,128)} %corr.3), calls=%async_computation.2 | async-start | bytes 1048576 | tf_op jit(solution)/shard_map/all_to_all | solution.py:351
  57.2 0.1 collective-permute-start.11
  57.3 1.6 copy-done.2
  58.9 1.6 %copy-done.4 = bf16[512,2048]{1,0:T(8,128)(2,1)S(1)} copy-done((bf16[512,2048]{1,0:T(8,128)(2,1)S(1)}, bf16[512,2048]{1,0:T(8,128)(2,1)}, u32[]{:S(2)}) %copy-start.4) | copy-done | bytes 2097176
  60.5 1.2 copy-done.6
  61.7 5.4 %corr.2 = f32[8,2,2,32,128]{4,3,2,1,0:T(8,128)} custom-call(s32[1]{0:T(128)} %bitcast.par.refs_0_, f32[1,2048]{1,0:T(1,128)S(1)} %bitcast.13, bf16[512,2048]{1,0:T(8,128)(2,1)S(1)} %copy-done.4, bf16[512,2048]{1,0:T(8,128)(2,1)S(1)} %copy-done.2, bf16[2,256,2048]{2,1,0:T(8,128)(2,1)S(1)} %copy-done, bf16[2,128,2048]{2,1,0:T(8,128)(2,1)S(1)} %copy-done.6), custom_call_target="tpu_custom_call" | custom-call | flops 1073741824 | bytes 5242880 | tf_op jit(solution)/shard_map/corr/pallas_call | solution.py:135
  67.1 4.1 %all-to-all-done.2.refs_0_ = f32[8,2,2,32,128]{4,3,2,1,0:T(8,128)S(1)} async-done(((f32[8,2,2,32,128]{4,3,2,1,0:T(8,128)}), f32[8,2,2,32,128]{4,3,2,1,0:T(8,128)S(1)}, u32[]{:S(2)}, u32[]{:S(2)}) %all-to-all-start.2) | async-done | bytes 524320 | tf_op jit(solution)/shard_map/all_to_all | solution.py:351
  71.1 22.5 %all-to-all-start = ((f32[8,2,2,32,128]{4,3,2,1,0:T(8,128)}), f32[8,2,2,32,128]{4,3,2,1,0:T(8,128)S(1)}, u32[]{:S(2)}, u32[]{:S(2)}) async-start(f32[8,2,2,32,128]{4,3,2,1,0:T(8,128)} %corr.2), calls=%async_computation | async-start | bytes 1048576 | tf_op jit(solution)/shard_map/all_to_all | solution.py:351
  93.7 0.6 collective-permute-start.10
  94.3 0.7 copy-done.9
  95.0 9.4 %all-to-all-done.refs_0_ = f32[8,2,2,32,128]{4,3,2,1,0:T(8,128)S(1)} async-done(((f32[8,2,2,32,128]{4,3,2,1,0:T(8,128)}), f32[8,2,2,32,128]{4,3,2,1,0:T(8,128)S(1)}, u32[]{:S(2)}, u32[]{:S(2)}) %all-to-all-start) | async-done | bytes 524320 | tf_op jit(solution)/shard_map/all_to_all | solution.py:351
  104.4 3.4 %all-to-all-start.3 = ((bf16[8,2,2,32,128]{4,3,2,1,0:T(8,128)(2,1)}), bf16[8,2,2,32,128]{4,3,2,1,0:T(8,128)(2,1)S(1)}, u32[]{:S(2)}, u32[]{:S(2)}) async-start(bf16[8,2,2,32,128]{4,3,2,1,0:T(8,128)(2,1)} %copy-done.9), calls=%async_computation.3 | async-start | bytes 524288 | tf_op jit(solution)/shard_map/all_to_all | solution.py:353
  107.8 0.7 resid.2
  108.5 6.5 %all-to-all-done.3.refs_1_ = bf16[8,2,2,32,128]{4,3,2,1,0:T(8,128)(2,1)S(1)} async-done(((bf16[8,2,2,32,128]{4,3,2,1,0:T(8,128)(2,1)}), bf16[8,2,2,32,128]{4,3,2,1,0:T(8,128)(2,1)S(1)}, u32[]{:S(2)}, u32[]{:S(2)}) %all-to-all-start.3) | async-done | bytes 262176 | tf_op jit(solution)/shard_map/all_to_all | solution.py:353
  115.0 3.4 %all-to-all-start.1 = ((bf16[8,2,2,32,128]{4,3,2,1,0:T(8,128)(2,1)}), bf16[8,2,2,32,128]{4,3,2,1,0:T(8,128)(2,1)S(1)}, u32[]{:S(2)}, u32[]{:S(2)}) async-start(bf16[8,2,2,32,128]{4,3,2,1,0:T(8,128)(2,1)} %resid.2), calls=%async_computation.1 | async-start | bytes 524288 | tf_op jit(solution)/shard_map/all_to_all | solution.py:353
  118.4 2.5 %collective-permute-start.9 = (bf16[8,1,2,32,128]{4,3,2,1,0:T(8,128)(2,1)S(1)}, bf16[8,1,2,32,128]{4,3,2,1,0:T(8,128)(2,1)S(1)}, u32[]{:S(2)}, u32[]{:S(2)}) collective-permute-start(bf16[8,1,2,32,128]{4,3,2,1,0:T(8,128)(2,1)S(1)} %slice.17), channel_id=1, source_target_pairs={{8,0},{0,8},{24,16},{16,24},{40,32},{32,40},{56,48},{48,56},{72,64... | collective-permute-start | bytes 393224 | tf_op jit(solution)/shard_map/ppermute | solution.py:18
  120.9 4.8 %all-to-all-done.1.refs_0_ = bf16[8,2,2,32,128]{4,3,2,1,0:T(8,128)(2,1)S(1)} async-done(((bf16[8,2,2,32,128]{4,3,2,1,0:T(8,128)(2,1)}), bf16[8,2,2,32,128]{4,3,2,1,0:T(8,128)(2,1)S(1)}, u32[]{:S(2)}, u32[]{:S(2)}) %all-to-all-start.1) | async-done | bytes 262176 | tf_op jit(solution)/shard_map/all_to_all | solution.py:353
  125.7 3.6 %collective-permute-start.8 = (bf16[8,1,2,32,128]{4,3,2,1,0:T(8,128)(2,1)S(1)}, bf16[8,1,2,32,128]{4,3,2,1,0:T(8,128)(2,1)S(1)}, u32[]{:S(2)}, u32[]{:S(2)}) collective-permute-start(bf16[8,1,2,32,128]{4,3,2,1,0:T(8,128)(2,1)S(1)} %slice.16), channel_id=1, source_target_pairs={{8,0},{0,8},{24,16},{16,24},{40,32},{32,40},{56,48},{48,56},{72,64... | collective-permute-start | bytes 393224 | tf_op jit(solution)/shard_map/ppermute | solution.py:18
  129.3 0.8 collective-permute-start.6
  130.1 0.3 collective-permute-start.4
  130.4 1.2 copy-done.7
  131.6 5.6 %early.1 = (f32[512,2048]{1,0:T(8,128)S(1)}, f32[1,2048]{1,0:T(1,128)S(1)}) custom-call(s32[1]{0:T(128)} %bitcast.par.refs_0_, bf16[8,2,2,32,128]{4,3,2,1,0:T(8,128)(2,1)S(1)} %all-to-all-done.1.refs_0_, bf16[8,2,2,32,128]{4,3,2,1,0:T(8,128)(2,1)S(1)} %all-to-all-done.3.refs_1_, bf16[8,1,2,32,128]{4,3,2,1,0:T(8,128)(2,1)S(1)} %collective-permute-done.8.refs_2_, ...), custom_call_target="tpu_custom_call" | custom-call | flops 3221225472 | bytes 12582912 | tf_op jit(solution)/shard_map/early/pallas_call | solution.py:272
  137.2 1.2 collective-permute-start.12
  138.4 0.8 collective-permute-done.12
  139.3 0.4 collective-permute-start.13
  139.7 2.1 %collective-permute-done.13 = f32[2048]{0:T(1024)S(1)} collective-permute-done((f32[2048]{0:T(1024)S(1)}, f32[2048]{0:T(1024)S(1)}, u32[]{:S(2)}, u32[]{:S(2)}) %collective-permute-start.13) | collective-permute-done | bytes 8224 | tf_op jit(solution)/shard_map/ppermute | solution.py:18
  141.8 0.8 collective-permute-start.14
  142.5 2.6 %collective-permute-done.14 = f32[2048]{0:T(1024)S(1)} collective-permute-done((f32[2048]{0:T(1024)S(1)}, f32[2048]{0:T(1024)S(1)}, u32[]{:S(2)}, u32[]{:S(2)}) %collective-permute-start.14) | collective-permute-done | bytes 8224 | tf_op jit(solution)/shard_map/ppermute | solution.py:18
  145.2 2.5 %collective-permute-start.15 = (f32[2048]{0:T(1024)S(1)}, f32[2048]{0:T(1024)S(1)}, u32[]{:S(2)}, u32[]{:S(2)}) collective-permute-start(f32[2048]{0:T(1024)S(1)} %add.22), channel_id=1, source_target_pairs={{64,0},{72,8},{80,16},{88,24},{96,32},{104,40},{112,48},{120,56},{... | collective-permute-start | bytes 24584 | tf_op jit(solution)/shard_map/ppermute | solution.py:18
  147.7 3.9 %collective-permute-done.15 = f32[2048]{0:T(1024)S(1)} collective-permute-done((f32[2048]{0:T(1024)S(1)}, f32[2048]{0:T(1024)S(1)}, u32[]{:S(2)}, u32[]{:S(2)}) %collective-permute-start.15) | collective-permute-done | bytes 8224 | tf_op jit(solution)/shard_map/ppermute | solution.py:18
  151.6 0.3 collective-permute-start.16
  151.9 6.4 %late.1 = f32[2,256,2048]{2,1,0:T(8,128)} custom-call(s32[1]{0:T(128)} %bitcast.par.refs_0_, f32[1,2048]{1,0:T(1,128)S(1)} %bitcast.14, bf16[8,2,2,32,128]{4,3,2,1,0:T(8,128)(2,1)S(1)} %collective-permute-done.4.refs_2_, bf16[8,2,2,32,128]{4,3,2,1,0:T(8,128)(2,1)S(1)} %collective-permute-done.6.refs_3_, bf16[512,2048]{1,0:T(8,128)(2,1)} %collective-permute-done.7.refs_4_, ...), custom_call_target="tpu_custom_call" | custom-call | flops 2147483648 | bytes 12582912 | tf_op jit(solution)/shard_map/late/pallas_call | solution.py:298
  158.3 0.6 add.24
  (41 shorter events, 0.2 us)
Async XLA Ops:
  0.6 16.1 %collective-permute-start.3 = (bf16[512,2048]{1,0:T(8,128)(2,1)}, bf16[512,2048]{1,0:T(8,128)(2,1)}, u32[]{:S(2)}, u32[]{:S(2)}) collective-permute-start(bf16[512,2048]{1,0:T(8,128)(2,1)} %bitcast.9), channel_id=1, source_target_pairs={{8,0},{0,8},{24,16},{16,24},{40,32},{32,40},{56,48},{48,56},{72,64... | collective-permute-start | bytes 6291464 | tf_op jit(solution)/shard_map/ppermute | solution.py:18
  3.9 1.2 copy-start.8
  5.1 1.0 copy-start.10
  6.2 0.7 copy-start.12
  7.4 9.3 %collective-permute-start.2 = (f32[3,32,256]{2,1,0:T(8,128)S(1)}, f32[3,32,256]{2,1,0:T(8,128)S(1)}, u32[]{:S(2)}, u32[]{:S(2)}) collective-permute-start(f32[3,32,256]{2,1,0:T(8,128)S(1)} %get-tuple-element.11), channel_id=1, source_target_pairs={{16,0},{248,8},{32,16},{8,24},{48,32},{24,40},{64,48},{40,56},{80,... | collective-permute-start | bytes 294920 | tf_op jit(solution)/shard_map/ppermute | solution.py:18
  7.5 8.6 %copy-start.11 = (f32[2048]{0:T(1024)S(1)}, f32[2048]{0:T(1024)}, u32[]{:S(2)}) copy-start(f32[2048]{0:T(1024)} %param.6) | copy-start | bytes 24580
  7.5 8.6 %copy-start = (bf16[2,256,2048]{2,1,0:T(8,128)(2,1)S(1)}, bf16[2,256,2048]{2,1,0:T(8,128)(2,1)}, u32[]{:S(2)}) copy-start(bf16[2,256,2048]{2,1,0:T(8,128)(2,1)} %own.3) | copy-start | bytes 6291460
  7.5 9.2 %collective-permute-start.1 = (f32[3,32,256]{2,1,0:T(8,128)S(1)}, f32[3,32,256]{2,1,0:T(8,128)S(1)}, u32[]{:S(2)}, u32[]{:S(2)}) collective-permute-start(f32[3,32,256]{2,1,0:T(8,128)S(1)} %get-tuple-element.10), channel_id=1, source_target_pairs={{8,0},{0,8},{24,16},{16,24},{40,32},{32,40},{56,48},{48,56},{72,64... | collective-permute-start | bytes 294920 | tf_op jit(solution)/shard_map/ppermute | solution.py:18
  16.1 16.0 %collective-permute-start = (bf16[2,128,2048]{2,1,0:T(8,128)(2,1)}, bf16[2,128,2048]{2,1,0:T(8,128)(2,1)S(1)}, u32[]{:S(2)}, u32[]{:S(2)}) collective-permute-start(bf16[2,128,2048]{2,1,0:T(8,128)(2,1)} %get-tuple-element.19), channel_id=1, source_target_pairs={{16,0},{248,8},{32,16},{8,24},{48,32},{24,40},{64,48},{40,56},{80,... | collective-permute-start | bytes 3145736 | tf_op jit(solution)/shard_map/ppermute | solution.py:18
  16.1 27.3 %collective-permute-start.5 = (bf16[2,128,2048]{2,1,0:T(8,128)(2,1)}, bf16[2,128,2048]{2,1,0:T(8,128)(2,1)}, u32[]{:S(2)}, u32[]{:S(2)}) collective-permute-start(bf16[2,128,2048]{2,1,0:T(8,128)(2,1)} %get-tuple-element.18), channel_id=1, source_target_pairs={{16,0},{248,8},{32,16},{8,24},{48,32},{24,40},{64,48},{40,56},{80,... | collective-permute-start | bytes 3145736 | tf_op jit(solution)/shard_map/ppermute | solution.py:18
  16.7 26.7 %copy-start.1 = (bf16[512,2048]{1,0:T(8,128)(2,1)}, bf16[512,2048]{1,0:T(8,128)(2,1)S(1)}, u32[]{:S(2)}) copy-start(bf16[512,2048]{1,0:T(8,128)(2,1)S(1)} %multiply_convert_fusion.lhs_second) | copy-start | bytes 6291460
  32.0 17.5 %copy-start.5 = (bf16[2,128,2048]{2,1,0:T(8,128)(2,1)}, bf16[2,128,2048]{2,1,0:T(8,128)(2,1)S(1)}, u32[]{:S(2)}) copy-start(bf16[2,128,2048]{2,1,0:T(8,128)(2,1)S(1)} %collective-permute-done.near.refs_6_) | copy-start | bytes 3145732
  49.5 1.3 copy-start.3
  50.8 20.3 %all-to-all-start.2 = ((f32[8,2,2,32,128]{4,3,2,1,0:T(8,128)}), f32[8,2,2,32,128]{4,3,2,1,0:T(8,128)S(1)}, u32[]{:S(2)}, u32[]{:S(2)}) async-start(f32[8,2,2,32,128]{4,3,2,1,0:T(8,128)} %corr.3), calls=%async_computation.2 | async-start | bytes 1048576 | tf_op jit(solution)/shard_map/all_to_all | solution.py:351
  57.2 94.7 %collective-permute-start.7 = (bf16[512,2048]{1,0:T(8,128)(2,1)S(1)}, bf16[512,2048]{1,0:T(8,128)(2,1)}, u32[]{:S(2)}, u32[]{:S(2)}) collective-permute-start(bf16[512,2048]{1,0:T(8,128)(2,1)S(1)} %bitcast.10), channel_id=1, source_target_pairs={{240,0},{24,8},{0,16},{40,24},{16,32},{56,40},{32,48},{72,56},{48,... | collective-permute-start | bytes 6291464 | tf_op jit(solution)/shard_map/ppermute | solution.py:18
  57.2 72.1 %collective-permute-start.11 = (bf16[2,128,2048]{2,1,0:T(8,128)(2,1)}, bf16[2,128,2048]{2,1,0:T(8,128)(2,1)}, u32[]{:S(2)}, u32[]{:S(2)}) collective-permute-start(bf16[2,128,2048]{2,1,0:T(8,128)(2,1)} %collective-permute-done.5.near.refs_7_), channel_id=1, source_target_pairs={{8,0},{0,8},{24,16},{16,24},{40,32},{32,40},{56,48},{48,56},{72,64... | collective-permute-start | bytes 3145736 | tf_op jit(solution)/shard_map/ppermute | solution.py:18
  57.3 1.6 %copy-start.2 = (bf16[512,2048]{1,0:T(8,128)(2,1)S(1)}, bf16[512,2048]{1,0:T(8,128)(2,1)}, u32[]{:S(2)}) copy-start(bf16[512,2048]{1,0:T(8,128)(2,1)} %copy-done.1) | copy-start | bytes 6291460
  58.9 1.6 %copy-start.4 = (bf16[512,2048]{1,0:T(8,128)(2,1)S(1)}, bf16[512,2048]{1,0:T(8,128)(2,1)}, u32[]{:S(2)}) copy-start(bf16[512,2048]{1,0:T(8,128)(2,1)} %copy-done.3) | copy-start | bytes 6291460
  60.5 1.2 copy-start.6
  71.1 33.2 %all-to-all-start = ((f32[8,2,2,32,128]{4,3,2,1,0:T(8,128)}), f32[8,2,2,32,128]{4,3,2,1,0:T(8,128)S(1)}, u32[]{:S(2)}, u32[]{:S(2)}) async-start(f32[8,2,2,32,128]{4,3,2,1,0:T(8,128)} %corr.2), calls=%async_computation | async-start | bytes 1048576 | tf_op jit(solution)/shard_map/all_to_all | solution.py:351
  93.7 36.7 %collective-permute-start.10 = (bf16[2,128,2048]{2,1,0:T(8,128)(2,1)}, bf16[2,128,2048]{2,1,0:T(8,128)(2,1)}, u32[]{:S(2)}, u32[]{:S(2)}) collective-permute-start(bf16[2,128,2048]{2,1,0:T(8,128)(2,1)} %copy-done.5), channel_id=1, source_target_pairs={{8,0},{0,8},{24,16},{16,24},{40,32},{32,40},{56,48},{48,56},{72,64... | collective-permute-start | bytes 3145736 | tf_op jit(solution)/shard_map/ppermute | solution.py:18
  94.3 0.7 copy-start.9
  104.4 10.6 %all-to-all-start.3 = ((bf16[8,2,2,32,128]{4,3,2,1,0:T(8,128)(2,1)}), bf16[8,2,2,32,128]{4,3,2,1,0:T(8,128)(2,1)S(1)}, u32[]{:S(2)}, u32[]{:S(2)}) async-start(bf16[8,2,2,32,128]{4,3,2,1,0:T(8,128)(2,1)} %copy-done.9), calls=%async_computation.3 | async-start | bytes 524288 | tf_op jit(solution)/shard_map/all_to_all | solution.py:353
  115.0 10.7 %all-to-all-start.1 = ((bf16[8,2,2,32,128]{4,3,2,1,0:T(8,128)(2,1)}), bf16[8,2,2,32,128]{4,3,2,1,0:T(8,128)(2,1)S(1)}, u32[]{:S(2)}, u32[]{:S(2)}) async-start(bf16[8,2,2,32,128]{4,3,2,1,0:T(8,128)(2,1)} %resid.2), calls=%async_computation.1 | async-start | bytes 524288 | tf_op jit(solution)/shard_map/all_to_all | solution.py:353
  118.4 11.7 %collective-permute-start.9 = (bf16[8,1,2,32,128]{4,3,2,1,0:T(8,128)(2,1)S(1)}, bf16[8,1,2,32,128]{4,3,2,1,0:T(8,128)(2,1)S(1)}, u32[]{:S(2)}, u32[]{:S(2)}) collective-permute-start(bf16[8,1,2,32,128]{4,3,2,1,0:T(8,128)(2,1)S(1)} %slice.17), channel_id=1, source_target_pairs={{8,0},{0,8},{24,16},{16,24},{40,32},{32,40},{56,48},{48,56},{72,64... | collective-permute-start | bytes 393224 | tf_op jit(solution)/shard_map/ppermute | solution.py:18
  125.7 4.7 %collective-permute-start.8 = (bf16[8,1,2,32,128]{4,3,2,1,0:T(8,128)(2,1)S(1)}, bf16[8,1,2,32,128]{4,3,2,1,0:T(8,128)(2,1)S(1)}, u32[]{:S(2)}, u32[]{:S(2)}) collective-permute-start(bf16[8,1,2,32,128]{4,3,2,1,0:T(8,128)(2,1)S(1)} %slice.16), channel_id=1, source_target_pairs={{8,0},{0,8},{24,16},{16,24},{40,32},{32,40},{56,48},{48,56},{72,64... | collective-permute-start | bytes 393224 | tf_op jit(solution)/shard_map/ppermute | solution.py:18
  129.3 22.6 %collective-permute-start.6 = (bf16[8,2,2,32,128]{4,3,2,1,0:T(8,128)(2,1)S(1)}, bf16[8,2,2,32,128]{4,3,2,1,0:T(8,128)(2,1)S(1)}, u32[]{:S(2)}, u32[]{:S(2)}) collective-permute-start(bf16[8,2,2,32,128]{4,3,2,1,0:T(8,128)(2,1)S(1)} %all-to-all-done.3.refs_1_), channel_id=1, source_target_pairs={{240,0},{24,8},{0,16},{40,24},{16,32},{56,40},{32,48},{72,56},{48,... | collective-permute-start | bytes 786440 | tf_op jit(solution)/shard_map/ppermute | solution.py:18
  130.1 21.8 %collective-permute-start.4 = (bf16[8,2,2,32,128]{4,3,2,1,0:T(8,128)(2,1)S(1)}, bf16[8,2,2,32,128]{4,3,2,1,0:T(8,128)(2,1)S(1)}, u32[]{:S(2)}, u32[]{:S(2)}) collective-permute-start(bf16[8,2,2,32,128]{4,3,2,1,0:T(8,128)(2,1)S(1)} %all-to-all-done.1.refs_0_), channel_id=1, source_target_pairs={{240,0},{24,8},{0,16},{40,24},{16,32},{56,40},{32,48},{72,56},{48,... | collective-permute-start | bytes 786440 | tf_op jit(solution)/shard_map/ppermute | solution.py:18
  130.4 1.2 copy-start.7
  137.2 2.0 %collective-permute-start.12 = (f32[2048]{0:T(1024)S(1)}, f32[2048]{0:T(1024)S(1)}, u32[]{:S(2)}, u32[]{:S(2)}) collective-permute-start(f32[2048]{0:T(1024)S(1)} %bitcast.16), channel_id=1, source_target_pairs={{8,0},{0,8},{24,16},{16,24},{40,32},{32,40},{56,48},{48,56},{72,64... | collective-permute-start | bytes 24584 | tf_op jit(solution)/shard_map/ppermute | solution.py:18
  139.3 2.5 %collective-permute-start.13 = (f32[2048]{0:T(1024)S(1)}, f32[2048]{0:T(1024)S(1)}, u32[]{:S(2)}, u32[]{:S(2)}) collective-permute-start(f32[2048]{0:T(1024)S(1)} %add.20), channel_id=1, source_target_pairs={{16,0},{24,8},{0,16},{8,24},{48,32},{56,40},{32,48},{40,56},{80,64... | collective-permute-start | bytes 24584 | tf_op jit(solution)/shard_map/ppermute | solution.py:18
  141.8 3.4 %collective-permute-start.14 = (f32[2048]{0:T(1024)S(1)}, f32[2048]{0:T(1024)S(1)}, u32[]{:S(2)}, u32[]{:S(2)}) collective-permute-start(f32[2048]{0:T(1024)S(1)} %add.21), channel_id=1, source_target_pairs={{32,0},{40,8},{48,16},{56,24},{0,32},{8,40},{16,48},{24,56},{96,64... | collective-permute-start | bytes 24584 | tf_op jit(solution)/shard_map/ppermute | solution.py:18
  145.2 6.4 %collective-permute-start.15 = (f32[2048]{0:T(1024)S(1)}, f32[2048]{0:T(1024)S(1)}, u32[]{:S(2)}, u32[]{:S(2)}) collective-permute-start(f32[2048]{0:T(1024)S(1)} %add.22), channel_id=1, source_target_pairs={{64,0},{72,8},{80,16},{88,24},{96,32},{104,40},{112,48},{120,56},{... | collective-permute-start | bytes 24584 | tf_op jit(solution)/shard_map/ppermute | solution.py:18
  151.6 6.7 %collective-permute-start.16 = (f32[2048]{0:T(1024)S(1)}, f32[2048]{0:T(1024)S(1)}, u32[]{:S(2)}, u32[]{:S(2)}) collective-permute-start(f32[2048]{0:T(1024)S(1)} %add.23), channel_id=1, source_target_pairs={{128,0},{136,8},{144,16},{152,24},{160,32},{168,40},{176,48},{184,... | collective-permute-start | bytes 24584 | tf_op jit(solution)/shard_map/ppermute | solution.py:18

commit v3 on v2

v3 whole, which is shorter than its diff:
```python
import math

import jax
import jax.numpy as jnp
from jax import lax
from jax.experimental import pallas as pl
from jax.experimental.pallas import tpu as pltpu
from jax.sharding import PartitionSpec as P


CHUNK = 512
WIRE = jnp.bfloat16


def permuted(block, axis, source_of):
    size = lax.axis_size(axis)
    return lax.ppermute(block, axis, [(source_of(i) % size, i) for i in range(size)])


def partner(i):
    return i ^ 1


def near_chip(i):
    return i + 2 if i % 2 == 0 else i - 2


def far_chip(i):
    return i - 2 if i % 2 == 0 else i + 2


def whole(array):
    return pl.BlockSpec(array.shape, lambda j: (0,) * array.ndim)


def prep_kernel(par, used, first, observed, amp_weight, natural, second, square):
    rows = natural.shape[1]
    at = pl.ds(pl.multiple_of(first[0], rows), rows)
    masks = [used[0, o].astype(jnp.float32) for o in range(2)]
    natural[:2] = observed[0, :, at, :]
    natural[2] = amp_weight[0, at, :] * masks[0]

    @pl.when(par[0] == 0)
    def _():
        square[0] = observed[1, 0].T
        square[1] = -observed[1, 1].T
        square[2] = amp_weight[1].T * masks[1]
        second[...] = square[:, at, :]

    @pl.when(par[0] == 1)
    def _():
        second[:2] = observed[1, :, at, :]
        second[2] = amp_weight[1, at, :] * masks[1]


def prepared(par, used, first, observed, amp_weight, slice_rows):
    cols = amp_weight.shape[2]
    packed = (3, slice_rows, cols)
    smem = pl.BlockSpec(memory_space=pltpu.SMEM)
    return pl.pallas_call(
        prep_kernel,
        out_shape=(jax.ShapeDtypeStruct(packed, jnp.float32),) * 2,
        grid=(1,),
        in_specs=[smem, smem, smem, whole(observed), whole(amp_weight)],
        out_specs=(pl.BlockSpec(packed, lambda j: (0, 0, 0)),) * 2,
        scratch_shapes=[pltpu.VMEM((3, cols, cols), jnp.float32)],
        cost_estimate=pl.CostEstimate(flops=0, bytes_accessed=8 << 20, transcendentals=0),
        compiler_params=pltpu.CompilerParams(vmem_limit_bytes=8 << 20),
        name="prep",
    )(par, used, first, observed, amp_weight)


def sum_kernel(pieces, total, wire):
    value = pieces[0].astype(jnp.float32)
    for part in range(1, pieces.shape[0]):
        value = value + pieces[part].astype(jnp.float32)
    total[...] = value
    wire[...] = value.astype(wire.dtype)


def summed(pieces):
    vmem = pl.BlockSpec(memory_space=pltpu.VMEM)
    shape = pieces.shape[1:]
    return pl.pallas_call(
        sum_kernel,
        out_shape=(jax.ShapeDtypeStruct(shape, jnp.float32), jax.ShapeDtypeStruct(shape, WIRE)),
        in_specs=[vmem],
        out_specs=(vmem, vmem),
        cost_estimate=pl.CostEstimate(flops=0, bytes_accessed=1 << 20, transcendentals=0),
        compiler_params=pltpu.CompilerParams(vmem_limit_bytes=4 << 20),
        name="summed",
    )(pieces)


def resid_kernel(inv_norm, total, other, data, out):
    corr = inv_norm * (total[...] + other[...].astype(jnp.float32))
    resid = (data[:, 2:] * (corr - data[:, :2])).astype(jnp.bfloat16)
    for part in range(out.shape[0]):
        out[part] = resid


def residuals(total, other, data, parts, inv_norm):
    def body(*refs):
        resid_kernel(inv_norm, *refs)

    vmem = pl.BlockSpec(memory_space=pltpu.VMEM)
    return pl.pallas_call(
        body,
        out_shape=jax.ShapeDtypeStruct((parts,) + total.shape, jnp.bfloat16),
        in_specs=[vmem] * 3,
        out_specs=vmem,
        cost_estimate=pl.CostEstimate(flops=0, bytes_accessed=2 << 20, transcendentals=0),
        compiler_params=pltpu.CompilerParams(vmem_limit_bytes=6 << 20),
        name="resid",
    )(total, other, data)


def corr_kernel(par, scale, lhs_first, lhs_second, own, near, out, acc):
    even = par[0] == 0
    acc[...] = jnp.zeros_like(acc)

    @pl.loop(0, own.shape[1] // CHUNK)
    def _(step):
        cols = pl.ds(pl.multiple_of(step * CHUNK, CHUNK), CHUNK)
        near_cols = near[:, cols]
        rhs_first = jnp.where(even, own[:, cols], near_cols)
        near_scale = jnp.where(even, scale[:, cols], 1.0)
        rhs_second = (near_cols.astype(jnp.float32) * near_scale).astype(jnp.bfloat16)
        for pair, (lhs, rhs) in enumerate(((lhs_first, rhs_first), (lhs_second, rhs_second))):
            acc[pair] += lax.dot_general(
                lhs[:, cols], rhs, (((1,), (1,)), ((), ())), preferred_element_type=jnp.float32
            )

    parts, _, _, rows, cols = out.shape
    half = parts * rows
    for pair in range(2):
        real = acc[pair, :half, :cols] + acc[pair, half:, cols:]
        imag = acc[pair, :half, cols:] - acc[pair, half:, :cols]
        out[:, pair, 0] = real.reshape(parts, rows, cols).astype(out.dtype)
        out[:, pair, 1] = imag.reshape(parts, rows, cols).astype(out.dtype)


def correlations(par, scale, lhs_first, lhs_second, own, near, parts):
    both, cols = own.shape
    half = both // 2
    vmem = pl.BlockSpec(memory_space=pltpu.VMEM)
    return pl.pallas_call(
        corr_kernel,
        out_shape=jax.ShapeDtypeStruct((parts, 2, 2, half // parts, half), WIRE),
        in_specs=[pl.BlockSpec(memory_space=pltpu.SMEM)] + [vmem] * 5,
        out_specs=vmem,
        scratch_shapes=[pltpu.VMEM((2, both, both), jnp.float32)],
        cost_estimate=pl.CostEstimate(flops=4 * both * both * cols, bytes_accessed=8 * both * cols, transcendentals=0),
        compiler_params=pltpu.CompilerParams(vmem_limit_bytes=24 << 20),
        name="corr",
    )(par, scale, lhs_first, lhs_second, own, near)


def assembled(gathered, pair, turned):
    real, imag = (gathered[:, pair, c].reshape(-1, gathered.shape[-1]) for c in range(2))
    if turned:
        real = real.astype(jnp.float32).T.astype(jnp.bfloat16)
        imag = (-imag.astype(jnp.float32)).T.astype(jnp.bfloat16)
    return real, imag


def place(mat, base, block):
    real, imag = block
    half = real.shape[0]
    mat[:half, base : base + half] = real
    mat[half:, base + half : base + 2 * half] = real
    mat[:half, base + half : base + 2 * half] = imag
    mat[half:, base : base + half] = -imag


def applied(mat, base, block):
    return jnp.dot(mat[:, base : base + block.shape[0]], block[...], preferred_element_type=jnp.float32)


def early_kernel(par, mine, mate_resid, own, mate, near, mate_near, early, kernel_part, mat):
    first = pl.program_id(0) == 0
    even = par[0] == 0
    both = early.shape[0]

    @pl.when(first)
    def _():
        place(mat, 0, assembled(mine, 1, False))

    @pl.when(first & even)
    def _():
        place(mat, both, assembled(mine, 0, True))
        place(mat, 2 * both, assembled(mate_resid, 0, False))

    @pl.when(first & jnp.logical_not(even))
    def _():
        place(mat, both, assembled(mate_resid, 0, False))

    def finish(term):
        mate_term = applied(mat, both, mate)
        own_cols = own[...].astype(jnp.float32)
        kernel_part[...] = jnp.sum(own_cols * (term + 0.5 * mate_term), axis=0, keepdims=True)
        early[...] = term + mate_term

    @pl.when(even)
    def _():
        finish(applied(mat, 0, near) + applied(mat, 2 * both, mate_near))

    @pl.when(jnp.logical_not(even))
    def _():
        finish(applied(mat, 0, near))


def late_kernel(inv_norm, par, scale, far_resid, far, early, mate_near, adjoint, mat):
    first = pl.program_id(0) == 0
    even = par[0] == 0
    both = early.shape[0]

    @pl.when(first)
    def _():
        place(mat, 0, assembled(far_resid, 1, True))

    @pl.when(first & jnp.logical_not(even))
    def _():
        place(mat, both, assembled(far_resid, 0, True))

    def finish(term):
        fields = early[...] + term
        adjoint[...] = (fields * (inv_norm * scale[...])).reshape(adjoint.shape)

    @pl.when(even)
    def _():
        finish(applied(mat, 0, far))

    @pl.when(jnp.logical_not(even))
    def _():
        finish(applied(mat, 0, far) + applied(mat, both, mate_near))


def column_block(array):
    shape = array.shape[:-1] + (CHUNK,)
    return pl.BlockSpec(shape, lambda j: (0,) * (array.ndim - 1) + (j,))


def early_fields(par, mine, mate_resid, own, mate, near, mate_near):
    both, cols = own.shape
    wholes = (mine, mate_resid)
    blocks = (own, mate, near, mate_near)
    return pl.pallas_call(
        early_kernel,
        out_shape=(
            jax.ShapeDtypeStruct((both, cols), jnp.float32),
            jax.ShapeDtypeStruct((1, cols), jnp.float32),
        ),
        grid=(cols // CHUNK,),
        in_specs=[pl.BlockSpec(memory_space=pltpu.SMEM)] + [whole(x) for x in wholes] + [column_block(x) for x in blocks],
        out_specs=(
            pl.BlockSpec((both, CHUNK), lambda j: (0, j)),
            pl.BlockSpec((1, CHUNK), lambda j: (0, j)),
        ),
        scratch_shapes=[pltpu.VMEM((both, 3 * both), jnp.bfloat16)],
        cost_estimate=pl.CostEstimate(flops=6 * both * both * cols, bytes_accessed=12 * both * cols, transcendentals=0),
        compiler_params=pltpu.CompilerParams(vmem_limit_bytes=24 << 20),
        name="early",
    )(par, *wholes, *blocks)


def late_fields(par, scale, far_resid, far, early, mate_near, inv_norm):
    both, cols = early.shape
    blocks = (far, early, mate_near)

    def body(*refs):
        late_kernel(inv_norm, *refs)

    return pl.pallas_call(
        body,
        out_shape=jax.ShapeDtypeStruct((2, both // 2, cols), jnp.float32),
        grid=(cols // CHUNK,),
        in_specs=[pl.BlockSpec(memory_space=pltpu.SMEM), column_block(scale)]
        + [whole(far_resid)]
        + [column_block(x) for x in blocks],
        out_specs=pl.BlockSpec((2, both // 2, CHUNK), lambda j: (0, 0, j)),
        scratch_shapes=[pltpu.VMEM((both, 2 * both), jnp.bfloat16)],
        cost_estimate=pl.CostEstimate(flops=4 * both * both * cols, bytes_accessed=12 * both * cols, transcendentals=0),
        compiler_params=pltpu.CompilerParams(vmem_limit_bytes=24 << 20),
        name="late",
    )(par, scale, far_resid, *blocks)


def shards(green, source_weight, observed, amp_weight, pair_used):
    row_count, col_count = green.shape[1:]
    block_count = lax.axis_size("cable")
    parts = lax.axis_size("grid")
    inv_norm = 1.0 / math.sqrt(col_count * parts)
    kernel_scale = inv_norm / (2.0 * math.sqrt(2.0 * block_count))
    parity = lax.axis_index("cable") % 2
    even = parity == 0
    par = parity.reshape(1)
    scale = source_weight[None, :]
    own = green.reshape(2 * row_count, col_count)
    pieces_count = parts // 2
    along_x = [list(range(i, parts, 2)) for i in range(2)]

    near = permuted(own, "cable", near_chip)
    mate = permuted(own, "cable", partner)

    slice_rows = row_count // pieces_count
    first = lax.axis_index("grid") // 2 * slice_rows
    packed = prepared(par, pair_used, first.reshape(1), observed, amp_weight, slice_rows)
    data_first = permuted(packed[0], "cable", partner)
    data_second = permuted(packed[1], "cable", near_chip)
    data = jnp.stack([data_first, jnp.where(even, data_second, packed[1])])

    lhs_first = (mate.astype(jnp.float32) * scale).astype(jnp.bfloat16)
    lhs_second = (own.astype(jnp.float32) * jnp.where(even, 1.0, scale)).astype(jnp.bfloat16)
    near, data, lhs_first, lhs_second = lax.optimization_barrier((near, data, lhs_first, lhs_second))

    partials = correlations(par, scale, lhs_first, lhs_second, own, near, pieces_count)
    far = permuted(own, "cable", far_chip)
    mate_near = permuted(near, "cable", partner)
    pieces = lax.all_to_all(partials, "grid", 0, 0, tiled=True, axis_index_groups=along_x)
    total, wire = summed(pieces)
    other = permuted(wire, "grid", partner)
    resid = residuals(total, other, data, pieces_count, inv_norm)
    mine = lax.all_to_all(resid, "grid", 0, 0, tiled=True, axis_index_groups=along_x)
    mate_resid = permuted(mine[:, :1], "cable", partner)
    far_resid = permuted(mine, "cable", far_chip)
    early, kernel_part = early_fields(par, mine, mate_resid, own, mate, near, mate_near)
    kernel = kernel_part[0] * kernel_scale
    adjoint = late_fields(par, scale, far_resid, far, early, mate_near, inv_norm)
    distance = block_count // 2
    swapped = [permuted(kernel, "cable", lambda i: i ^ d) for d in (1, distance, distance + 1)]
    kernel = (kernel + swapped[0]) + (swapped[1] + swapped[2])
    step = 2
    while step < distance:
        kernel = kernel + permuted(kernel, "cable", lambda i: i ^ step)
        step *= 2
    return (adjoint, kernel)


def solution(mesh):
    in_specs = (
        P(None, "cable", "grid"),
        P("grid"),
        P(None, None, "cable", None),
        P(None, "cable", None),
        P("cable", None),
    )
    out_specs = (P(None, "cable", "grid"), P("grid"))

    return jax.shard_map(shards, mesh=mesh, in_specs=in_specs, out_specs=out_specs, check_vma=False)
```

time: 162 us -> 123 us (0.76); the launches traced: 159 us -> 122 us
  starting transfers between devices: 57.5 us -> 29.1 us
  blocking collectives: 0 us -> 12.8 us
  local copies, waits for them, and re-layouts: 13.7 us -> 2.95 us
  Pallas kernels: 24.8 us -> 18.5 us
  waiting for transfers between devices: 58.1 us -> 52 us
  other arithmetic: 3.96 us -> 5.6 us
    all_to_all x4 -> x1, starting transfers between devices: 35.7 us -> 4.01 us  [shards(): lax.all_to_all(partials, 'grid', 0, 0, tiled=True, axis_index_groups=alon...]
    all_to_all x4 -> x1, waiting for transfers between devices: 24.7 us -> 5.07 us  [shards(): lax.all_to_all(partials, 'grid', 0, 0, tiled=True, axis_index_groups=alon...]
    ppermute x17 -> x15, waiting for transfers between devices: 33.4 us -> 46.9 us  [permuted(): lax.ppermute(block, axis, [(source_of(i) % size, i) for i in range(size)])]
    all_to_all x0 -> x1, blocking collectives: none -> 12.8 us  [shards(): lax.all_to_all(resid, 'grid', 0, 0, tiled=True, axis_index_groups=along_x)]
    unnamed x26 -> x10, local copies, waits for them, and re-layouts: 10.6 us -> 2.93 us
    pallas_call x4 -> x3, Pallas kernels: 12.3 us -> 5.84 us  [the longest x1 5.72 us: correlations(): pl.pallas_call(corr_kernel, out_shape=jax.ShapeDtypeStruct((parts, 2, 2,...]
    ppermute x17 -> x15, starting transfers between devices: 21.8 us -> 25.1 us  [permuted(): lax.ppermute(block, axis, [(source_of(i) % size, i) for i in range(size)])]
    slice x3 -> x1, local copies, waits for them, and re-layouts: 3.13 us -> 0.02 us  [shards(): mate_resid = permuted(mine[:, :1], 'cable', partner)]
  transfers between devices with their start and end apart: 21 -> 16, of which waited for: 10 -> 7; matrix products, arithmetic and copies ran while one was open for 4% -> 4% of each run, Pallas kernels for 12% -> 15%
where the time goes in v3:
time: 123 us; the launch traced here: 122 us
  waiting for transfers between devices  52 us (42%)
  starting transfers between devices  29.1 us (24%)
  Pallas kernels  18.5 us (15%)
  blocking collectives  12.8 us (10%)
  other arithmetic  5.6 us (5%)
  local copies, waits for them, and re-layouts  2.95 us (2%)
    ppermute x15, waiting for transfers between devices, permuted(): lax.ppermute(block, axis, [(source_of(i) % size, i) for i in range(size)])  46.9 us
    ppermute x15, starting transfers between devices, permuted(): lax.ppermute(block, axis, [(source_of(i) % size, i) for i in range(size)])  25.1 us
    all_to_all x1, blocking collectives, shards(): lax.all_to_all(resid, 'grid', 0, 0, tiled=True, axis_index_groups=along_x)  12.8 us
    pallas_call x1, Pallas kernels, late_fields(): pl.pallas_call(body, out_shape=jax.ShapeDtypeStruct((2, both // 2, cols),...  6.39 us
    pallas_call x1, Pallas kernels, correlations(): pl.pallas_call(corr_kernel, out_shape=jax.ShapeDtypeStruct((parts, 2, 2,...  5.72 us
    pallas_call x1, Pallas kernels, early_fields(): pl.pallas_call(early_kernel, out_shape=(jax.ShapeDtypeStruct((both, cols)...  5.71 us
    all_to_all x1, waiting for transfers between devices, shards(): lax.all_to_all(partials, 'grid', 0, 0, tiled=True, axis_index_groups=alon...  5.07 us
    all_to_all x1, starting transfers between devices, shards(): lax.all_to_all(partials, 'grid', 0, 0, tiled=True, axis_index_groups=alon...  4.01 us
  transfers between devices with their start and end apart: 16, of which 7 were waited for; matrix products, arithmetic and copies ran while one was open for 4% of the time, Pallas kernels for 15%

profile of v3, /device:TPU:1, one launch (start us, length us, event | category | flops | bytes accessed | tf_op | source)
XLA Modules:
  0.0 121.8 jit_solution(9862939681018421338)
XLA Ops:
  0.6 3.3 %collective-permute-start.3 = (bf16[512,2048]{1,0:T(8,128)(2,1)}, bf16[512,2048]{1,0:T(8,128)(2,1)}, u32[]{:S(2)}, u32[]{:S(2)}) collective-permute-start(bf16[512,2048]{1,0:T(8,128)(2,1)} %bitcast.9), channel_id=1, source_target_pairs={{8,0},{0,8},{24,16},{16,24},{40,32},{32,40},{56,48},{48,56},{72,64... | collective-permute-start | bytes 6291464 | tf_op jit(solution)/shard_map/ppermute | solution.py:17
  3.9 0.0 collective-permute-start
  3.9 1.2 %copy-done.1 = f32[2,2,256,256]{3,2,1,0:T(8,128)S(1)} copy-done((f32[2,2,256,256]{3,2,1,0:T(8,128)S(1)}, f32[2,2,256,256]{3,2,1,0:T(8,128)}, u32[]{:S(2)}) %copy-start.1) | copy-done | bytes 1048600
  5.1 1.0 copy-done.2
  6.2 0.7 copy-done.4
  6.8 0.6 prep.1
  7.4 1.6 %collective-permute-start.2 = (f32[3,64,256]{2,1,0:T(8,128)S(1)}, f32[3,64,256]{2,1,0:T(8,128)S(1)}, u32[]{:S(2)}, u32[]{:S(2)}) collective-permute-start(f32[3,64,256]{2,1,0:T(8,128)S(1)} %get-tuple-element.13), channel_id=1, source_target_pairs={{16,0},{248,8},{32,16},{8,24},{48,32},{24,40},{64,48},{40,56},{80,... | collective-permute-start | bytes 589832 | tf_op jit(solution)/shard_map/ppermute | solution.py:17
  9.1 5.0 %collective-permute-start.1 = (f32[3,64,256]{2,1,0:T(8,128)S(1)}, f32[3,64,256]{2,1,0:T(8,128)S(1)}, u32[]{:S(2)}, u32[]{:S(2)}) collective-permute-start(f32[3,64,256]{2,1,0:T(8,128)S(1)} %get-tuple-element.12), channel_id=1, source_target_pairs={{8,0},{0,8},{24,16},{16,24},{40,32},{32,40},{56,48},{48,56},{72,64... | collective-permute-start | bytes 589832 | tf_op jit(solution)/shard_map/ppermute | solution.py:17
  14.0 0.7 broadcast_select_fusion
  14.7 2.0 %multiply_convert_fusion.lhs_second = bf16[512,2048]{1,0:T(8,128)(2,1)S(1)} fusion(f32[2048]{0:T(1024)S(1)} %broadcast_select_fusion, bf16[2,256,2048]{2,1,0:T(8,128)(2,1)} %param.5), kind=kLoop, calls=%fused_computation | loop fusion | flops 3145728 | bytes 4202496 | tf_op jit(solution)/shard_map/convert_element_type | solution.py:314
  16.8 17.8 %collective-permute-done.2 = f32[3,64,256]{2,1,0:T(8,128)S(1)} collective-permute-done((f32[3,64,256]{2,1,0:T(8,128)S(1)}, f32[3,64,256]{2,1,0:T(8,128)S(1)}, u32[]{:S(2)}, u32[]{:S(2)}) %collective-permute-start.2) | collective-permute-done | bytes 196640 | tf_op jit(solution)/shard_map/ppermute | solution.py:17
  34.6 0.0 collective-permute-done.1
  34.6 0.0 copy-start
  34.6 0.0 collective-permute-done.3.mate
  34.6 0.0 copy-done.3
  34.6 2.2 %multiply_convert_fusion.1.lhs_first = bf16[512,2048]{1,0:T(8,128)(2,1)S(1)} fusion(bf16[512,2048]{1,0:T(8,128)(2,1)} %collective-permute-done.3.mate, f32[2048]{0:T(1024)S(1)} %copy-done.3), kind=kLoop, calls=%fused_computation.1 | loop fusion | flops 3145728 | bytes 4202496 | tf_op jit(solution)/shard_map/convert_element_type | solution.py:313
  36.8 0.0 collective-permute-done.near
  36.8 0.6 collective-permute-start.8
  37.4 5.7 %corr.1 = bf16[4,2,2,64,256]{4,3,2,1,0:T(8,128)(2,1)} custom-call(s32[1]{0:T(128)} %bitcast.par.refs_0_, f32[1,2048]{1,0:T(1,128)S(1)} %bitcast.14, bf16[512,2048]{1,0:T(8,128)(2,1)S(1)} %multiply_convert_fusion.1.lhs_first, bf16[512,2048]{1,0:T(8,128)(2,1)S(1)} %multiply_convert_fusion.lhs_second, bf16[512,2048]{1,0:T(8,128)(2,1)S(1)} %bitcast.11, ...), custom_call_target="tpu_custom_call" | custom-call | flops 2147483648 | bytes 8388608 | tf_op jit(solution)/shard_map/corr/pallas_call | solution.py:147
  43.2 4.0 %all-to-all-start = ((bf16[4,2,2,64,256]{4,3,2,1,0:T(8,128)(2,1)}), bf16[4,2,2,64,256]{4,3,2,1,0:T(8,128)(2,1)S(1)}, u32[]{:S(2)}, u32[]{:S(2)}) async-start(bf16[4,2,2,64,256]{4,3,2,1,0:T(8,128)(2,1)} %corr.1), calls=%async_computation | async-start | bytes 1048576 | tf_op jit(solution)/shard_map/all_to_all | solution.py:320
  47.2 4.3 %collective-permute-start.6 = (bf16[512,2048]{1,0:T(8,128)(2,1)S(1)}, bf16[512,2048]{1,0:T(8,128)(2,1)}, u32[]{:S(2)}, u32[]{:S(2)}) collective-permute-start(bf16[512,2048]{1,0:T(8,128)(2,1)S(1)} %bitcast.12), channel_id=1, source_target_pairs={{240,0},{24,8},{0,16},{40,24},{16,32},{56,40},{32,48},{72,56},{48,... | collective-permute-start | bytes 6291464 | tf_op jit(solution)/shard_map/ppermute | solution.py:17
  51.5 5.1 %all-to-all-done.pieces = bf16[4,2,2,64,256]{4,3,2,1,0:T(8,128)(2,1)S(1)} async-done(((bf16[4,2,2,64,256]{4,3,2,1,0:T(8,128)(2,1)}), bf16[4,2,2,64,256]{4,3,2,1,0:T(8,128)(2,1)S(1)}, u32[]{:S(2)}, u32[]{:S(2)}) %all-to-all-start) | async-done | bytes 524320 | tf_op jit(solution)/shard_map/all_to_all | solution.py:320
  56.5 0.1 summed.1
  56.6 2.7 %collective-permute-start.4 = (bf16[2,2,64,256]{3,2,1,0:T(8,128)(2,1)S(1)}, bf16[2,2,64,256]{3,2,1,0:T(8,128)(2,1)S(1)}, u32[]{:S(2)}, u32[]{:S(2)}) collective-permute-start(bf16[2,2,64,256]{3,2,1,0:T(8,128)(2,1)S(1)} %get-tuple-element.18), channel_id=1, source_target_pairs={{1,0},{0,1},{3,2},{2,3},{5,4},{4,5},{7,6},{6,7},{9,8},{8,9},{11,10... | collective-permute-start | bytes 393224 | tf_op jit(solution)/shard_map/ppermute | solution.py:17
  59.3 20.7 %collective-permute-done.4.refs_1_ = bf16[2,2,64,256]{3,2,1,0:T(8,128)(2,1)S(1)} collective-permute-done((bf16[2,2,64,256]{3,2,1,0:T(8,128)(2,1)S(1)}, bf16[2,2,64,256]{3,2,1,0:T(8,128)(2,1)S(1)}, u32[]{:S(2)}, u32[]{:S(2)}) %collective-permute-start.4) | collective-permute-done | bytes 131104 | tf_op jit(solution)/shard_map/ppermute | solution.py:17
  80.0 0.1 resid.1
  80.1 12.8 %all_to_all.10.mine = bf16[4,2,2,64,256]{4,3,2,1,0:T(8,128)(2,1)S(1)} all-to-all(bf16[4,2,2,64,256]{4,3,2,1,0:T(8,128)(2,1)S(1)} %resid.1), channel_id=1, replica_groups={{0,2,4,6},{1,3,5,7},{8,10,12,14},{9,11,13,15},{16,18,20,22},{17,19,21,2..., dimensions={0} | all-to-all | bytes 1048576 | tf_op jit(solution)/shard_map/all_to_all | solution.py:324
  92.9 2.0 %collective-permute-start.7 = (bf16[4,1,2,64,256]{4,3,2,1,0:T(8,128)(2,1)S(1)}, bf16[4,1,2,64,256]{4,3,2,1,0:T(8,128)(2,1)S(1)}, u32[]{:S(2)}, u32[]{:S(2)}) collective-permute-start(bf16[4,1,2,64,256]{4,3,2,1,0:T(8,128)(2,1)S(1)} %slice.4), channel_id=1, source_target_pairs={{8,0},{0,8},{24,16},{16,24},{40,32},{32,40},{56,48},{48,56},{72,64... | collective-permute-start | bytes 786440 | tf_op jit(solution)/shard_map/ppermute | solution.py:17
  94.9 2.2 %collective-permute-start.5 = (bf16[4,2,2,64,256]{4,3,2,1,0:T(8,128)(2,1)S(1)}, bf16[4,2,2,64,256]{4,3,2,1,0:T(8,128)(2,1)S(1)}, u32[]{:S(2)}, u32[]{:S(2)}) collective-permute-start(bf16[4,2,2,64,256]{4,3,2,1,0:T(8,128)(2,1)S(1)} %all_to_all.10.mine), channel_id=1, source_target_pairs={{240,0},{24,8},{0,16},{40,24},{16,32},{56,40},{32,48},{72,56},{48,... | collective-permute-start | bytes 1572872 | tf_op jit(solution)/shard_map/ppermute | solution.py:17
  97.1 0.0 collective-permute-done.7.mate_resid
  97.1 0.0 collective-permute-done.8.mate_near.refs_5_
  97.1 5.7 %early.1 = (f32[512,2048]{1,0:T(8,128)S(1)}, f32[1,2048]{1,0:T(1,128)S(1)}) custom-call(s32[1]{0:T(128)} %bitcast.par.refs_0_, bf16[4,2,2,64,256]{4,3,2,1,0:T(8,128)(2,1)S(1)} %all_to_all.10.mine, bf16[4,1,2,64,256]{4,3,2,1,0:T(8,128)(2,1)S(1)} %collective-permute-done.7.mate_resid, bf16[512,2048]{1,0:T(8,128)(2,1)S(1)} %bitcast.13, ...), custom_call_target="tpu_custom_call" | custom-call | flops 3221225472 | bytes 12582912 | tf_op jit(solution)/shard_map/early/pallas_call | solution.py:248
  102.9 1.7 %collective-permute-start.10 = (f32[2048]{0:T(1024)S(1)}, f32[2048]{0:T(1024)S(1)}, u32[]{:S(2)}, u32[]{:S(2)}) collective-permute-start(f32[2048]{0:T(1024)S(1)} %bitcast.17), channel_id=1, source_target_pairs={{128,0},{136,8},{144,16},{152,24},{160,32},{168,40},{176,48},{184,... | collective-permute-start | bytes 24584 | tf_op jit(solution)/shard_map/ppermute | solution.py:17
  104.6 0.2 collective-permute-start.11
  104.8 0.3 collective-permute-start.9
  105.1 0.9 collective-permute-done.10
  105.9 1.7 %collective-permute-done.11 = f32[2048]{0:T(1024)S(1)} collective-permute-done((f32[2048]{0:T(1024)S(1)}, f32[2048]{0:T(1024)S(1)}, u32[]{:S(2)}, u32[]{:S(2)}) %collective-permute-start.11) | collective-permute-done | bytes 8224 | tf_op jit(solution)/shard_map/ppermute | solution.py:17
  107.6 0.0 collective-permute-done.9
  107.6 0.1 collective-permute-start.12
  107.7 2.5 %collective-permute-done.12 = f32[2048]{0:T(1024)S(1)} collective-permute-done((f32[2048]{0:T(1024)S(1)}, f32[2048]{0:T(1024)S(1)}, u32[]{:S(2)}, u32[]{:S(2)}) %collective-permute-start.12) | collective-permute-done | bytes 8224 | tf_op jit(solution)/shard_map/ppermute | solution.py:17
  110.2 0.0 collective-permute-start.13
  110.2 3.4 %collective-permute-done.13 = f32[2048]{0:T(1024)S(1)} collective-permute-done((f32[2048]{0:T(1024)S(1)}, f32[2048]{0:T(1024)S(1)}, u32[]{:S(2)}, u32[]{:S(2)}) %collective-permute-start.13) | collective-permute-done | bytes 8224 | tf_op jit(solution)/shard_map/ppermute | solution.py:17
  113.6 1.1 collective-permute-start.14
  114.8 0.0 collective-permute-done.6.refs_3_
  114.8 0.0 collective-permute-done.5.refs_2_
  114.8 6.4 %late.1 = f32[2,256,2048]{2,1,0:T(8,128)} custom-call(s32[1]{0:T(128)} %bitcast.par.refs_0_, f32[1,2048]{1,0:T(1,128)S(1)} %bitcast.15, bf16[4,2,2,64,256]{4,3,2,1,0:T(8,128)(2,1)S(1)} %collective-permute-done.5.refs_2_, bf16[512,2048]{1,0:T(8,128)(2,1)} %collective-permute-done.6.refs_3_, f32[512,2048]{1,0:T(8,128)S(1)} %get-tuple-element.20.refs_4_, ...), custom_call_target="tpu_custom_call" | custom-call | flops 2147483648 | bytes 12582912 | tf_op jit(solution)/shard_map/late/pallas_call | solution.py:274
  121.2 0.0 collective-permute-done.14
  121.2 0.6 add.29
  (12 shorter events, 0.1 us)
Async XLA Ops:
  0.6 34.0 %collective-permute-start.3 = (bf16[512,2048]{1,0:T(8,128)(2,1)}, bf16[512,2048]{1,0:T(8,128)(2,1)}, u32[]{:S(2)}, u32[]{:S(2)}) collective-permute-start(bf16[512,2048]{1,0:T(8,128)(2,1)} %bitcast.9), channel_id=1, source_target_pairs={{8,0},{0,8},{24,16},{16,24},{40,32},{32,40},{56,48},{48,56},{72,64... | collective-permute-start | bytes 6291464 | tf_op jit(solution)/shard_map/ppermute | solution.py:17
  3.9 32.9 %collective-permute-start = (bf16[512,2048]{1,0:T(8,128)(2,1)}, bf16[512,2048]{1,0:T(8,128)(2,1)}, u32[]{:S(2)}, u32[]{:S(2)}) collective-permute-start(bf16[512,2048]{1,0:T(8,128)(2,1)} %bitcast.10), channel_id=1, source_target_pairs={{16,0},{248,8},{32,16},{8,24},{48,32},{24,40},{64,48},{40,56},{80,... | collective-permute-start | bytes 6291464 | tf_op jit(solution)/shard_map/ppermute | solution.py:17
  3.9 1.2 %copy-start.1 = (f32[2,2,256,256]{3,2,1,0:T(8,128)S(1)}, f32[2,2,256,256]{3,2,1,0:T(8,128)}, u32[]{:S(2)}) copy-start(f32[2,2,256,256]{3,2,1,0:T(8,128)} %observed.1) | copy-start | bytes 3145732
  5.1 1.0 copy-start.2
  6.2 0.7 copy-start.4
  7.4 27.1 %collective-permute-start.2 = (f32[3,64,256]{2,1,0:T(8,128)S(1)}, f32[3,64,256]{2,1,0:T(8,128)S(1)}, u32[]{:S(2)}, u32[]{:S(2)}) collective-permute-start(f32[3,64,256]{2,1,0:T(8,128)S(1)} %get-tuple-element.13), channel_id=1, source_target_pairs={{16,0},{248,8},{32,16},{8,24},{48,32},{24,40},{64,48},{40,56},{80,... | collective-permute-start | bytes 589832 | tf_op jit(solution)/shard_map/ppermute | solution.py:17
  9.1 25.5 %collective-permute-start.1 = (f32[3,64,256]{2,1,0:T(8,128)S(1)}, f32[3,64,256]{2,1,0:T(8,128)S(1)}, u32[]{:S(2)}, u32[]{:S(2)}) collective-permute-start(f32[3,64,256]{2,1,0:T(8,128)S(1)} %get-tuple-element.12), channel_id=1, source_target_pairs={{8,0},{0,8},{24,16},{16,24},{40,32},{32,40},{56,48},{48,56},{72,64... | collective-permute-start | bytes 589832 | tf_op jit(solution)/shard_map/ppermute | solution.py:17
  14.7 19.9 %copy-start.3 = (f32[2048]{0:T(1024)S(1)}, f32[2048]{0:T(1024)}, u32[]{:S(2)}) copy-start(f32[2048]{0:T(1024)} %param.6) | copy-start | bytes 24580
  34.6 2.8 %copy-start = (bf16[2,256,2048]{2,1,0:T(8,128)(2,1)S(1)}, bf16[2,256,2048]{2,1,0:T(8,128)(2,1)}, u32[]{:S(2)}) copy-start(bf16[2,256,2048]{2,1,0:T(8,128)(2,1)} %param.5) | copy-start | bytes 6291460
  36.8 60.3 %collective-permute-start.8 = (bf16[512,2048]{1,0:T(8,128)(2,1)}, bf16[512,2048]{1,0:T(8,128)(2,1)}, u32[]{:S(2)}, u32[]{:S(2)}) collective-permute-start(bf16[512,2048]{1,0:T(8,128)(2,1)} %collective-permute-done.near), channel_id=1, source_target_pairs={{8,0},{0,8},{24,16},{16,24},{40,32},{32,40},{56,48},{48,56},{72,64... | collective-permute-start | bytes 6291464 | tf_op jit(solution)/shard_map/ppermute | solution.py:17
  43.2 13.4 %all-to-all-start = ((bf16[4,2,2,64,256]{4,3,2,1,0:T(8,128)(2,1)}), bf16[4,2,2,64,256]{4,3,2,1,0:T(8,128)(2,1)S(1)}, u32[]{:S(2)}, u32[]{:S(2)}) async-start(bf16[4,2,2,64,256]{4,3,2,1,0:T(8,128)(2,1)} %corr.1), calls=%async_computation | async-start | bytes 1048576 | tf_op jit(solution)/shard_map/all_to_all | solution.py:320
  47.2 67.6 %collective-permute-start.6 = (bf16[512,2048]{1,0:T(8,128)(2,1)S(1)}, bf16[512,2048]{1,0:T(8,128)(2,1)}, u32[]{:S(2)}, u32[]{:S(2)}) collective-permute-start(bf16[512,2048]{1,0:T(8,128)(2,1)S(1)} %bitcast.12), channel_id=1, source_target_pairs={{240,0},{24,8},{0,16},{40,24},{16,32},{56,40},{32,48},{72,56},{48,... | collective-permute-start | bytes 6291464 | tf_op jit(solution)/shard_map/ppermute | solution.py:17
  56.6 23.4 %collective-permute-start.4 = (bf16[2,2,64,256]{3,2,1,0:T(8,128)(2,1)S(1)}, bf16[2,2,64,256]{3,2,1,0:T(8,128)(2,1)S(1)}, u32[]{:S(2)}, u32[]{:S(2)}) collective-permute-start(bf16[2,2,64,256]{3,2,1,0:T(8,128)(2,1)S(1)} %get-tuple-element.18), channel_id=1, source_target_pairs={{1,0},{0,1},{3,2},{2,3},{5,4},{4,5},{7,6},{6,7},{9,8},{8,9},{11,10... | collective-permute-start | bytes 393224 | tf_op jit(solution)/shard_map/ppermute | solution.py:17
  92.9 4.2 %collective-permute-start.7 = (bf16[4,1,2,64,256]{4,3,2,1,0:T(8,128)(2,1)S(1)}, bf16[4,1,2,64,256]{4,3,2,1,0:T(8,128)(2,1)S(1)}, u32[]{:S(2)}, u32[]{:S(2)}) collective-permute-start(bf16[4,1,2,64,256]{4,3,2,1,0:T(8,128)(2,1)S(1)} %slice.4), channel_id=1, source_target_pairs={{8,0},{0,8},{24,16},{16,24},{40,32},{32,40},{56,48},{48,56},{72,64... | collective-permute-start | bytes 786440 | tf_op jit(solution)/shard_map/ppermute | solution.py:17
  94.9 19.8 %collective-permute-start.5 = (bf16[4,2,2,64,256]{4,3,2,1,0:T(8,128)(2,1)S(1)}, bf16[4,2,2,64,256]{4,3,2,1,0:T(8,128)(2,1)S(1)}, u32[]{:S(2)}, u32[]{:S(2)}) collective-permute-start(bf16[4,2,2,64,256]{4,3,2,1,0:T(8,128)(2,1)S(1)} %all_to_all.10.mine), channel_id=1, source_target_pairs={{240,0},{24,8},{0,16},{40,24},{16,32},{56,40},{32,48},{72,56},{48,... | collective-permute-start | bytes 1572872 | tf_op jit(solution)/shard_map/ppermute | solution.py:17
  102.9 3.0 %collective-permute-start.10 = (f32[2048]{0:T(1024)S(1)}, f32[2048]{0:T(1024)S(1)}, u32[]{:S(2)}, u32[]{:S(2)}) collective-permute-start(f32[2048]{0:T(1024)S(1)} %bitcast.17), channel_id=1, source_target_pairs={{128,0},{136,8},{144,16},{152,24},{160,32},{168,40},{176,48},{184,... | collective-permute-start | bytes 24584 | tf_op jit(solution)/shard_map/ppermute | solution.py:17
  104.6 3.1 %collective-permute-start.11 = (f32[2048]{0:T(1024)S(1)}, f32[2048]{0:T(1024)S(1)}, u32[]{:S(2)}, u32[]{:S(2)}) collective-permute-start(f32[2048]{0:T(1024)S(1)} %bitcast.18), channel_id=1, source_target_pairs={{136,0},{128,8},{152,16},{144,24},{168,32},{160,40},{184,48},{176,... | collective-permute-start | bytes 24584 | tf_op jit(solution)/shard_map/ppermute | solution.py:17
  104.8 2.9 %collective-permute-start.9 = (f32[2048]{0:T(1024)S(1)}, f32[2048]{0:T(1024)S(1)}, u32[]{:S(2)}, u32[]{:S(2)}) collective-permute-start(f32[2048]{0:T(1024)S(1)} %bitcast.19), channel_id=1, source_target_pairs={{8,0},{0,8},{24,16},{16,24},{40,32},{32,40},{56,48},{48,56},{72,64... | collective-permute-start | bytes 24584 | tf_op jit(solution)/shard_map/ppermute | solution.py:17
  107.6 2.6 %collective-permute-start.12 = (f32[2048]{0:T(1024)S(1)}, f32[2048]{0:T(1024)S(1)}, u32[]{:S(2)}, u32[]{:S(2)}) collective-permute-start(f32[2048]{0:T(1024)S(1)} %add_add_fusion), channel_id=1, source_target_pairs={{16,0},{24,8},{0,16},{8,24},{48,32},{56,40},{32,48},{40,56},{80,64... | collective-permute-start | bytes 24584 | tf_op jit(solution)/shard_map/ppermute | solution.py:17
  110.2 3.4 %collective-permute-start.13 = (f32[2048]{0:T(1024)S(1)}, f32[2048]{0:T(1024)S(1)}, u32[]{:S(2)}, u32[]{:S(2)}) collective-permute-start(f32[2048]{0:T(1024)S(1)} %add.27), channel_id=1, source_target_pairs={{32,0},{40,8},{48,16},{56,24},{0,32},{8,40},{16,48},{24,56},{96,64... | collective-permute-start | bytes 24584 | tf_op jit(solution)/shard_map/ppermute | solution.py:17
  113.6 7.5 %collective-permute-start.14 = (f32[2048]{0:T(1024)S(1)}, f32[2048]{0:T(1024)S(1)}, u32[]{:S(2)}, u32[]{:S(2)}) collective-permute-start(f32[2048]{0:T(1024)S(1)} %add.28), channel_id=1, source_target_pairs={{64,0},{72,8},{80,16},{88,24},{96,32},{104,40},{112,48},{120,56},{... | collective-permute-start | bytes 24584 | tf_op jit(solution)/shard_map/ppermute | solution.py:17

commit v4 on v3

--- a/solution.py
+++ b/solution.py
@@ -178,62 +178,67 @@
 
 
 def early_kernel(par, mine, mate_resid, own, mate, near, mate_near, early, kernel_part, mat):
+    both = early.shape[0]
+
+    @pl.when(pl.program_id(0) == 0)
+    def _():
+        place(mat, 0, assembled(mine, 1, False))
+        place(mat, both, assembled(mate_resid, 0, False))
+
+    second = jnp.where(par[0] == 0, mate_near[...], mate[...])
+    fields = applied(mat, 0, near) + applied(mat, both, second)
+    kernel_part[...] = jnp.sum(own[...].astype(jnp.float32) * fields, axis=0, keepdims=True)
+    early[...] = fields
+
+
+def late_kernel(inv_norm, par, scale, mine, far_resid, far_real, far_imag, early, mate, mate_near, adjoint, mat):
     first = pl.program_id(0) == 0
     even = par[0] == 0
     both = early.shape[0]
 
     @pl.when(first)
     def _():
-        place(mat, 0, assembled(mine, 1, False))
+        place(mat, 0, assembled(far_resid, 1, True))
 
     @pl.when(first & even)
     def _():
         place(mat, both, assembled(mine, 0, True))
-        place(mat, 2 * both, assembled(mate_resid, 0, False))
 
     @pl.when(first & jnp.logical_not(even))
     def _():
-        place(mat, both, assembled(mate_resid, 0, False))
-
-    def finish(term):
-        mate_term = applied(mat, both, mate)
-        own_cols = own[...].astype(jnp.float32)
-        kernel_part[...] = jnp.sum(own_cols * (term + 0.5 * mate_term), axis=0, keepdims=True)
-        early[...] = term + mate_term
-
-    @pl.when(even)
-    def _():
-        finish(applied(mat, 0, near) + applied(mat, 2 * both, mate_near))
-
-    @pl.when(jnp.logical_not(even))
-    def _():
-        finish(applied(mat, 0, near))
-
-
-def late_kernel(inv_norm, par, scale, far_resid, far, early, mate_near, adjoint, mat):
-    first = pl.program_id(0) == 0
-    even = par[0] == 0
-    both = early.shape[0]
-
-    @pl.when(first)
-    def _():
-        place(mat, 0, assembled(far_resid, 1, True))
-
-    @pl.when(first & jnp.logical_not(even))
-    def _():
         place(mat, both, assembled(far_resid, 0, True))
 
-    def finish(term):
-        fields = early[...] + term
-        adjoint[...] = (fields * (inv_norm * scale[...])).reshape(adjoint.shape)
-
-    @pl.when(even)
-    def _():
-        finish(applied(mat, 0, far))
-
-    @pl.when(jnp.logical_not(even))
-    def _():
-        finish(applied(mat, 0, far) + applied(mat, both, mate_near))
+    second = jnp.where(even, mate[...], mate_near[...])
+    term = applied(mat, 0, far_real) + applied(mat, both // 2, far_imag) + applied(mat, both, second)
+    adjoint[...] = ((early[...] + term) * (inv_norm * scale[...])).reshape(adjoint.shape)
+
+
+def ring_kernel(place_of, rows, above, below, out, slots):
+    count = slots.shape[0]
+    position = 0
+    for piece, offset in ((below, -3), (rows, -1), (above, 2)):
+        for i in range(piece.shape[0]):
+            slots[lax.rem(place_of[0] + (offset + i + count), count)] = piece[i]
+            position += 1
+    assert position == count
+    total = slots[0]
+    for i in range(1, count):
+        total = total + slots[i]
+    out[...] = total
+
+
+def ring_sum(place_of, rows, above, below, count):
+    vmem = pl.BlockSpec(memory_space=pltpu.VMEM)
+    return pl.pallas_call(
+        ring_kernel,
+        out_shape=jax.ShapeDtypeStruct(rows.shape[1:], jnp.float32),
+        in_specs=[pl.BlockSpec(memory_space=pltpu.SMEM)] + [vmem] * 3,
+        out_specs=vmem,
+        scratch_shapes=[pltpu.VMEM((count,) + rows.shape[1:], jnp.float32)],
+        cost_estimate=pl.CostEstimate(flops=0, bytes_accessed=1 << 17, transcendentals=0),
+        compiler_params=pltpu.CompilerParams(vmem_limit_bytes=1 << 20),
+        name="ring_sum",
+    )(place_of, rows, above, below)
 
 
 def column_block(array):
@@ -248,7 +253,7 @@
     return pl.pallas_call(
         early_kernel,
         out_shape=(
-            jax.ShapeDtypeStruct((both, cols), jnp.float32),
+            pltpu.HBM((both, cols), jnp.float32),
             jax.ShapeDtypeStruct((1, cols), jnp.float32),
         ),
         grid=(cols // CHUNK,),
@@ -257,16 +262,16 @@
             pl.BlockSpec((both, CHUNK), lambda j: (0, j)),
             pl.BlockSpec((1, CHUNK), lambda j: (0, j)),
         ),
-        scratch_shapes=[pltpu.VMEM((both, 3 * both), jnp.bfloat16)],
-        cost_estimate=pl.CostEstimate(flops=6 * both * both * cols, bytes_accessed=12 * both * cols, transcendentals=0),
+        scratch_shapes=[pltpu.VMEM((both, 2 * both), jnp.bfloat16)],
+        cost_estimate=pl.CostEstimate(flops=4 * both * both * cols, bytes_accessed=12 * both * cols, transcendentals=0),
         compiler_params=pltpu.CompilerParams(vmem_limit_bytes=24 << 20),
         name="early",
     )(par, *wholes, *blocks)
 
 
-def late_fields(par, scale, far_resid, far, early, mate_near, inv_norm):
+def late_fields(par, scale, mine, far_resid, far, early, mate, mate_near, inv_norm):
     both, cols = early.shape
-    blocks = (far, early, mate_near)
+    blocks = (*far, early, mate, mate_near)
 
     def body(*refs):
         late_kernel(inv_norm, *refs)
@@ -276,14 +281,14 @@
         out_shape=jax.ShapeDtypeStruct((2, both // 2, cols), jnp.float32),
         grid=(cols // CHUNK,),
         in_specs=[pl.BlockSpec(memory_space=pltpu.SMEM), column_block(scale)]
-        + [whole(far_resid)]
+        + [whole(mine), whole(far_resid)]
         + [column_block(x) for x in blocks],
         out_specs=pl.BlockSpec((2, both // 2, CHUNK), lambda j: (0, 0, j)),
         scratch_shapes=[pltpu.VMEM((both, 2 * both), jnp.bfloat16)],
         cost_estimate=pl.CostEstimate(flops=4 * both * both * cols, bytes_accessed=12 * both * cols, transcendentals=0),
         compiler_params=pltpu.CompilerParams(vmem_limit_bytes=24 << 20),
         name="late",
-    )(par, scale, far_resid, *blocks)
+    )(par, scale, mine, far_resid, *blocks)
 
 
 def shards(green, source_weight, observed, amp_weight, pair_used):
@@ -312,10 +317,13 @@
 
     lhs_first = (mate.astype(jnp.float32) * scale).astype(jnp.bfloat16)
     lhs_second = (own.astype(jnp.float32) * jnp.where(even, 1.0, scale)).astype(jnp.bfloat16)
-    near, data, lhs_first, lhs_second = lax.optimization_barrier((near, data, lhs_first, lhs_second))
+    cuts = (green[0], green[1])
+    near, lhs_first, lhs_second, cuts = lax.optimization_barrier((near, lhs_first, lhs_second, cuts))
 
     partials = correlations(par, scale, lhs_first, lhs_second, own, near, pieces_count)
-    far = permuted(own, "cable", far_chip)
+    far = []
+    for component in range(2):
+        far.append(permuted(cuts[component], "cable", far_chip))
     mate_near = permuted(near, "cable", partner)
     pieces = lax.all_to_all(partials, "grid", 0, 0, tiled=True, axis_index_groups=along_x)
     total, wire = summed(pieces)
@@ -326,14 +334,21 @@
     far_resid = permuted(mine, "cable", far_chip)
     early, kernel_part = early_fields(par, mine, mate_resid, own, mate, near, mate_near)
     kernel = kernel_part[0] * kernel_scale
-    adjoint = late_fields(par, scale, far_resid, far, early, mate_near, inv_norm)
+    adjoint = late_fields(par, scale, mine, far_resid, far, early, mate, mate_near, inv_norm)
     distance = block_count // 2
     swapped = [permuted(kernel, "cable", lambda i: i ^ d) for d in (1, distance, distance + 1)]
     kernel = (kernel + swapped[0]) + (swapped[1] + swapped[2])
-    step = 2
-    while step < distance:
-        kernel = kernel + permuted(kernel, "cable", lambda i: i ^ step)
-        step *= 2
+
+    def along_z(hops):
+        return lambda i: i // distance * distance + (i + 2 * hops) % distance
+
+    kernel = kernel.reshape(1, 16, -1)
+    neighbours = [permuted(kernel, "cable", along_z(hops)) for hops in (-1, 1)]
+    rows = jnp.concatenate([neighbours[0], kernel, neighbours[1]], axis=0)
+    above = permuted(rows, "cable", along_z(3))
+    below = permuted(rows[1:], "cable", along_z(-3))
+    place_of = lax.axis_index("cable") % distance // 2
+    kernel = ring_sum(place_of.reshape(1), rows, above, below, distance // 2).reshape(col_count)
     return (adjoint, kernel)
 
 

time: 123 us -> 125 us (1.016)
  local copies, waits for them, and re-layouts: 2.95 us -> 6.87 us
  starting transfers between devices: 29.1 us -> 32 us
  other arithmetic: 5.6 us -> 3.39 us
  blocking collectives: 12.8 us -> 10.6 us
  Pallas kernels: 18.5 us -> 20.5 us
  waiting for transfers between devices: 52 us -> 50.3 us
    squeeze x0 -> x1, local copies, waits for them, and re-layouts: none -> 3.34 us  [shards(): cuts = (green[0], green[1])]
    ppermute x15 -> x17, starting transfers between devices: 25.1 us -> 28 us  [permuted(): lax.ppermute(block, axis, [(source_of(i) % size, i) for i in range(size)])]
    all_to_all x1, waiting for transfers between devices: 5.07 us -> 2.26 us  [shards(): lax.all_to_all(partials, 'grid', 0, 0, tiled=True, axis_index_groups=alon...]
    all_to_all x1, blocking collectives: 12.8 us -> 10.6 us  [shards(): lax.all_to_all(resid, 'grid', 0, 0, tiled=True, axis_index_groups=along_x)]
    pallas_call x1 -> x2, Pallas kernels: 5.71 us -> 7.27 us  [the longest x1 6.63 us: early_fields(): pl.pallas_call(early_kernel, out_shape=(pltpu.HBM((both, cols), jnp.float...]
    convert_element_type x1, other arithmetic: 2.04 us -> 0.58 us  [shards(): (own.astype(jnp.float32) * jnp.where(even, 1.0, scale)).astype(jnp.bfloat16)]
    ppermute x15 -> x17, waiting for transfers between devices: 46.9 us -> 48 us  [permuted(): lax.ppermute(block, axis, [(source_of(i) % size, i) for i in range(size)])]
    unnamed x10 -> x12, local copies, waits for them, and re-layouts: 2.93 us -> 3.51 us
  transfers between devices with their start and end apart: 16 -> 18, of which waited for: 7 -> 7; matrix products, arithmetic and copies ran while one was open for 4% -> 5% of each run, Pallas kernels for 15% -> 16%
where the time goes in v4:
time: 125 us; the launch traced here: 124 us
  waiting for transfers between devices  50.3 us (40%)
  starting transfers between devices  32 us (26%)
  Pallas kernels  20.5 us (16%)
  blocking collectives  10.6 us (8%)
  local copies, waits for them, and re-layouts  6.87 us (5%)
  other arithmetic  3.39 us (3%)
    ppermute x17, waiting for transfers between devices, permuted(): lax.ppermute(block, axis, [(source_of(i) % size, i) for i in range(size)])  48 us
    ppermute x17, starting transfers between devices, permuted(): lax.ppermute(block, axis, [(source_of(i) % size, i) for i in range(size)])  28 us
    all_to_all x1, blocking collectives, shards(): lax.all_to_all(resid, 'grid', 0, 0, tiled=True, axis_index_groups=along_x)  10.6 us
    pallas_call x1, Pallas kernels, late_fields(): pl.pallas_call(body, out_shape=jax.ShapeDtypeStruct((2, both // 2, cols),...  6.8 us
    pallas_call x1, Pallas kernels, early_fields(): pl.pallas_call(early_kernel, out_shape=(pltpu.HBM((both, cols), jnp.float...  6.63 us
    pallas_call x1, Pallas kernels, correlations(): pl.pallas_call(corr_kernel, out_shape=jax.ShapeDtypeStruct((parts, 2, 2,...  5.78 us
    all_to_all x1, starting transfers between devices, shards(): lax.all_to_all(partials, 'grid', 0, 0, tiled=True, axis_index_groups=alon...  4.01 us
    unnamed x12, local copies, waits for them, and re-layouts  3.51 us
  transfers between devices with their start and end apart: 18, of which 7 were waited for; matrix products, arithmetic and copies ran while one was open for 5% of the time, Pallas kernels for 16%

profile of v4, /device:TPU:1, one launch (start us, length us, event | category | flops | bytes accessed | tf_op | source)
XLA Modules:
  0.0 124.5 jit_solution(1157154855758626789)
XLA Ops:
  0.6 3.3 %collective-permute-start.1 = (bf16[512,2048]{1,0:T(8,128)(2,1)}, bf16[512,2048]{1,0:T(8,128)(2,1)}, u32[]{:S(2)}, u32[]{:S(2)}) collective-permute-start(bf16[512,2048]{1,0:T(8,128)(2,1)} %bitcast.17), channel_id=1, source_target_pairs={{8,0},{0,8},{24,16},{16,24},{40,32},{32,40},{56,48},{48,56},{72,64... | collective-permute-start | bytes 6291464 | tf_op jit(solution)/shard_map/ppermute | solution.py:17
  3.9 0.0 collective-permute-start
  3.9 0.7 broadcast_select_fusion
  4.6 3.3 %slice_bitcast_fusion = (bf16[256,2048]{1,0:T(8,128)(2,1)}, bf16[256,2048]{1,0:T(8,128)(2,1)}) fusion(bf16[2,256,2048]{2,1,0:T(8,128)(2,1)} %param.5), kind=kLoop, calls=%fused_computation.2 | loop fusion | bytes 4194304 | tf_op jit(solution)/shard_map/squeeze | solution.py:320
  8.0 0.6 multiply_convert_fusion.lhs_second
  8.6 0.0 collective-permute-done.1.mate.refs_7_
  8.6 0.1 copy-done.4
  8.7 2.0 %multiply_convert_fusion.1.lhs_first = bf16[512,2048]{1,0:T(8,128)(2,1)S(1)} fusion(bf16[512,2048]{1,0:T(8,128)(2,1)} %collective-permute-done.1.mate.refs_7_, f32[2048]{0:T(1024)S(1)} %copy-done.4), kind=kLoop, calls=%fused_computation.1 | loop fusion | flops 3145728 | bytes 4202496 | tf_op jit(solution)/shard_map/convert_element_type | solution.py:318
  10.7 21.8 %collective-permute-done.near = bf16[512,2048]{1,0:T(8,128)(2,1)} collective-permute-done((bf16[512,2048]{1,0:T(8,128)(2,1)}, bf16[512,2048]{1,0:T(8,128)(2,1)}, u32[]{:S(2)}, u32[]{:S(2)}) %collective-permute-start) | collective-permute-done | bytes 2097184 | tf_op jit(solution)/shard_map/ppermute | solution.py:17
  32.5 0.5 collective-permute-start.9
  33.0 5.8 %corr.1 = bf16[4,2,2,64,256]{4,3,2,1,0:T(8,128)(2,1)} custom-call(s32[1]{0:T(128)} %bitcast.par.refs_0_, f32[1,2048]{1,0:T(1,128)S(1)} %bitcast.21, bf16[512,2048]{1,0:T(8,128)(2,1)S(1)} %multiply_convert_fusion.1.lhs_first, bf16[512,2048]{1,0:T(8,128)(2,1)S(1)} %multiply_convert_fusion.lhs_second, bf16[512,2048]{1,0:T(8,128)(2,1)S(1)} %bitcast.19, ...), custom_call_target="tpu_custom_call" | custom-call | flops 2147483648 | bytes 8388608 | tf_op jit(solution)/shard_map/corr/pallas_call | solution.py:147
  38.8 4.0 %all-to-all-start = ((bf16[4,2,2,64,256]{4,3,2,1,0:T(8,128)(2,1)}), bf16[4,2,2,64,256]{4,3,2,1,0:T(8,128)(2,1)S(1)}, u32[]{:S(2)}, u32[]{:S(2)}) async-start(bf16[4,2,2,64,256]{4,3,2,1,0:T(8,128)(2,1)} %corr.1), calls=%async_computation | async-start | bytes 1048576 | tf_op jit(solution)/shard_map/all_to_all | solution.py:328
  42.8 1.2 copy-done.2
  44.1 0.6 prep.1
  44.6 0.1 collective-permute-start.4
  44.7 5.1 %collective-permute-start.3 = (f32[3,64,256]{2,1,0:T(8,128)S(1)}, f32[3,64,256]{2,1,0:T(8,128)S(1)}, u32[]{:S(2)}, u32[]{:S(2)}) collective-permute-start(f32[3,64,256]{2,1,0:T(8,128)S(1)} %get-tuple-element.18), channel_id=1, source_target_pairs={{8,0},{0,8},{24,16},{16,24},{40,32},{32,40},{56,48},{48,56},{72,64... | collective-permute-start | bytes 589832 | tf_op jit(solution)/shard_map/ppermute | solution.py:17
  49.9 2.3 %all-to-all-done.pieces = bf16[4,2,2,64,256]{4,3,2,1,0:T(8,128)(2,1)S(1)} async-done(((bf16[4,2,2,64,256]{4,3,2,1,0:T(8,128)(2,1)}), bf16[4,2,2,64,256]{4,3,2,1,0:T(8,128)(2,1)S(1)}, u32[]{:S(2)}, u32[]{:S(2)}) %all-to-all-start) | async-done | bytes 524320 | tf_op jit(solution)/shard_map/all_to_all | solution.py:328
  52.1 0.1 summed.1
  52.2 2.7 %collective-permute-start.2 = (bf16[2,2,64,256]{3,2,1,0:T(8,128)(2,1)S(1)}, bf16[2,2,64,256]{3,2,1,0:T(8,128)(2,1)S(1)}, u32[]{:S(2)}, u32[]{:S(2)}) collective-permute-start(bf16[2,2,64,256]{3,2,1,0:T(8,128)(2,1)S(1)} %get-tuple-element.17), channel_id=1, source_target_pairs={{1,0},{0,1},{3,2},{2,3},{5,4},{4,5},{7,6},{6,7},{9,8},{8,9},{11,10... | collective-permute-start | bytes 393224 | tf_op jit(solution)/shard_map/ppermute | solution.py:17
  54.9 0.0 collective-permute-done.4
  54.9 0.0 collective-permute-done.3
  55.0 2.6 %collective-permute-done.2.refs_1_ = bf16[2,2,64,256]{3,2,1,0:T(8,128)(2,1)S(1)} collective-permute-done((bf16[2,2,64,256]{3,2,1,0:T(8,128)(2,1)S(1)}, bf16[2,2,64,256]{3,2,1,0:T(8,128)(2,1)S(1)}, u32[]{:S(2)}, u32[]{:S(2)}) %collective-permute-start.2) | collective-permute-done | bytes 131104 | tf_op jit(solution)/shard_map/ppermute | solution.py:17
  57.6 0.1 resid.1
  57.7 10.6 %all_to_all.10.mine.refs_2_ = bf16[4,2,2,64,256]{4,3,2,1,0:T(8,128)(2,1)S(1)} all-to-all(bf16[4,2,2,64,256]{4,3,2,1,0:T(8,128)(2,1)S(1)} %resid.1), channel_id=1, replica_groups={{0,2,4,6},{1,3,5,7},{8,10,12,14},{9,11,13,15},{16,18,20,22},{17,19,21,2..., dimensions={0} | all-to-all | bytes 1048576 | tf_op jit(solution)/shard_map/all_to_all | solution.py:332
  68.3 2.8 %collective-permute-start.8 = (bf16[4,1,2,64,256]{4,3,2,1,0:T(8,128)(2,1)S(1)}, bf16[4,1,2,64,256]{4,3,2,1,0:T(8,128)(2,1)S(1)}, u32[]{:S(2)}, u32[]{:S(2)}) collective-permute-start(bf16[4,1,2,64,256]{4,3,2,1,0:T(8,128)(2,1)S(1)} %slice.14), channel_id=1, source_target_pairs={{8,0},{0,8},{24,16},{16,24},{40,32},{32,40},{56,48},{48,56},{72,64... | collective-permute-start | bytes 786440 | tf_op jit(solution)/shard_map/ppermute | solution.py:17
  71.1 3.8 %collective-permute-start.6 = (bf16[256,2048]{1,0:T(8,128)(2,1)}, bf16[256,2048]{1,0:T(8,128)(2,1)}, u32[]{:S(2)}, u32[]{:S(2)}) collective-permute-start(bf16[256,2048]{1,0:T(8,128)(2,1)} %get-tuple-element.20), channel_id=1, source_target_pairs={{240,0},{24,8},{0,16},{40,24},{16,32},{56,40},{32,48},{72,56},{48,... | collective-permute-start | bytes 3145736 | tf_op jit(solution)/shard_map/ppermute | solution.py:17
  74.9 0.0 collective-permute-start.7
  74.9 0.0 collective-permute-start.5
  75.0 0.0 collective-permute-done.8.mate_resid
  75.0 0.0 collective-permute-done.9.mate_near.refs_8_
  75.0 6.6 %early.1 = (f32[512,2048]{1,0:T(8,128)}, f32[1,2048]{1,0:T(1,128)S(1)}) custom-call(s32[1]{0:T(128)} %bitcast.par.refs_0_, bf16[4,2,2,64,256]{4,3,2,1,0:T(8,128)(2,1)S(1)} %all_to_all.10.mine.refs_2_, bf16[4,1,2,64,256]{4,3,2,1,0:T(8,128)(2,1)S(1)} %collective-permute-done.8.mate_resid, bf16[512,2048]{1,0:T(8,128)(2,1)S(1)} %bitcast.20, ...), custom_call_target="tpu_custom_call" | custom-call | flops 2147483648 | bytes 12582912 | tf_op jit(solution)/shard_map/early/pallas_call | solution.py:253
  81.6 0.1 collective-permute-start.10
  81.7 2.4 %collective-permute-start.11 = (f32[2048]{0:T(1024)S(1)}, f32[2048]{0:T(1024)S(1)}, u32[]{:S(2)}, u32[]{:S(2)}) collective-permute-start(f32[2048]{0:T(1024)S(1)} %bitcast.25), channel_id=1, source_target_pairs={{128,0},{136,8},{144,16},{152,24},{160,32},{168,40},{176,48},{184,... | collective-permute-start | bytes 24584 | tf_op jit(solution)/shard_map/ppermute | solution.py:17
  84.1 0.0 collective-permute-done.10
  84.1 1.1 collective-permute-start.12
  85.2 19.6 %collective-permute-done.11 = f32[2048]{0:T(1024)S(1)} collective-permute-done((f32[2048]{0:T(1024)S(1)}, f32[2048]{0:T(1024)S(1)}, u32[]{:S(2)}, u32[]{:S(2)}) %collective-permute-start.11) | collective-permute-done | bytes 8224 | tf_op jit(solution)/shard_map/ppermute | solution.py:17
  104.9 0.2 collective-permute-done.12
  105.0 4.5 %collective-permute-start.14 = (f32[1,16,128]{2,1,0:T(8,128)S(1)}, f32[1,16,128]{2,1,0:T(8,128)S(1)}, u32[]{:S(2)}, u32[]{:S(2)}) collective-permute-start(f32[1,16,128]{2,1,0:T(8,128)S(1)} %add_bitcast_fusion), channel_id=1, source_target_pairs={{16,0},{24,8},{32,16},{40,24},{48,32},{56,40},{64,48},{72,56},{80,... | collective-permute-start | bytes 24584 | tf_op jit(solution)/shard_map/ppermute | solution.py:17
  109.5 0.0 collective-permute-start.13
  109.6 0.8 collective-permute-done.14
  110.3 0.0 collective-permute-start.16
  110.3 2.9 %collective-permute-done.13 = f32[1,16,128]{2,1,0:T(8,128)S(1)} collective-permute-done((f32[1,16,128]{2,1,0:T(8,128)S(1)}, f32[1,16,128]{2,1,0:T(8,128)S(1)}, u32[]{:S(2)}, u32[]{:S(2)}) %collective-permute-start.13) | collective-permute-done | bytes 8224 | tf_op jit(solution)/shard_map/ppermute | solution.py:17
  113.3 1.6 %collective-permute-start.15 = (f32[3,16,128]{2,1,0:T(8,128)S(1)}, f32[3,16,128]{2,1,0:T(8,128)S(1)}, u32[]{:S(2)}, u32[]{:S(2)}) collective-permute-start(f32[3,16,128]{2,1,0:T(8,128)S(1)} %pad_maximum_fusion.1.rows), channel_id=1, source_target_pairs={{48,0},{56,8},{64,16},{72,24},{80,32},{88,40},{96,48},{104,56},{11... | collective-permute-start | bytes 73736 | tf_op jit(solution)/shard_map/ppermute | solution.py:17
  114.8 0.0 collective-permute-done.6.refs_4_
  114.8 0.0 copy-start.1
  114.8 2.2 %copy-done.1 = f32[512,2048]{1,0:T(8,128)S(1)} copy-done((f32[512,2048]{1,0:T(8,128)S(1)}, f32[512,2048]{1,0:T(8,128)}, u32[]{:S(2)}) %copy-start.1) | copy-done | bytes 4194328
  117.0 6.8 %late.1 = f32[2,256,2048]{2,1,0:T(8,128)} custom-call(s32[1]{0:T(128)} %bitcast.par.refs_0_, f32[1,2048]{1,0:T(1,128)S(1)} %bitcast.22, bf16[4,2,2,64,256]{4,3,2,1,0:T(8,128)(2,1)S(1)} %all_to_all.10.mine.refs_2_, bf16[4,2,2,64,256]{4,3,2,1,0:T(8,128)(2,1)S(1)} %collective-permute-done.5.refs_3_, bf16[256,2048]{1,0:T(8,128)(2,1)} %collective-permute-done.6.refs_4_, ...), custom_call_target="tpu_custom_call" | custom-call | flops 2147483648 | bytes 12582912 | tf_op jit(solution)/shard_map/late/pallas_call | solution.py:279
  123.8 0.6 ring_sum.1
  (19 shorter events, 0.1 us)
Async XLA Ops:
  0.6 7.9 %collective-permute-start.1 = (bf16[512,2048]{1,0:T(8,128)(2,1)}, bf16[512,2048]{1,0:T(8,128)(2,1)}, u32[]{:S(2)}, u32[]{:S(2)}) collective-permute-start(bf16[512,2048]{1,0:T(8,128)(2,1)} %bitcast.17), channel_id=1, source_target_pairs={{8,0},{0,8},{24,16},{16,24},{40,32},{32,40},{56,48},{48,56},{72,64... | collective-permute-start | bytes 6291464 | tf_op jit(solution)/shard_map/ppermute | solution.py:17
  3.9 28.6 %collective-permute-start = (bf16[512,2048]{1,0:T(8,128)(2,1)}, bf16[512,2048]{1,0:T(8,128)(2,1)}, u32[]{:S(2)}, u32[]{:S(2)}) collective-permute-start(bf16[512,2048]{1,0:T(8,128)(2,1)} %bitcast.18), channel_id=1, source_target_pairs={{16,0},{248,8},{32,16},{8,24},{48,32},{24,40},{64,48},{40,56},{80,... | collective-permute-start | bytes 6291464 | tf_op jit(solution)/shard_map/ppermute | solution.py:17
  4.6 3.3 %copy-start = (bf16[2,256,2048]{2,1,0:T(8,128)(2,1)S(1)}, bf16[2,256,2048]{2,1,0:T(8,128)(2,1)}, u32[]{:S(2)}) copy-start(bf16[2,256,2048]{2,1,0:T(8,128)(2,1)} %param.5) | copy-start | bytes 6291460
  8.0 0.7 copy-start.4
  32.5 42.4 %collective-permute-start.9 = (bf16[512,2048]{1,0:T(8,128)(2,1)}, bf16[512,2048]{1,0:T(8,128)(2,1)}, u32[]{:S(2)}, u32[]{:S(2)}) collective-permute-start(bf16[512,2048]{1,0:T(8,128)(2,1)} %collective-permute-done.near), channel_id=1, source_target_pairs={{8,0},{0,8},{24,16},{16,24},{40,32},{32,40},{56,48},{48,56},{72,64... | collective-permute-start | bytes 6291464 | tf_op jit(solution)/shard_map/ppermute | solution.py:17
  33.0 9.8 %copy-start.3 = (f32[2,256,256]{2,1,0:T(8,128)S(1)}, f32[2,256,256]{2,1,0:T(8,128)}, u32[]{:S(2)}) copy-start(f32[2,256,256]{2,1,0:T(8,128)} %amp_weight.1) | copy-start | bytes 1572868
  33.0 9.8 %copy-start.5 = (s32[1,2]{1,0:T(1,128)S(1)}, s32[1,2]{1,0:T(1,128)}, u32[]{:S(2)}) copy-start(s32[1,2]{1,0:T(1,128)} %used.1) | copy-start | bytes 28
  38.8 13.3 %all-to-all-start = ((bf16[4,2,2,64,256]{4,3,2,1,0:T(8,128)(2,1)}), bf16[4,2,2,64,256]{4,3,2,1,0:T(8,128)(2,1)S(1)}, u32[]{:S(2)}, u32[]{:S(2)}) async-start(bf16[4,2,2,64,256]{4,3,2,1,0:T(8,128)(2,1)} %corr.1), calls=%async_computation | async-start | bytes 1048576 | tf_op jit(solution)/shard_map/all_to_all | solution.py:328
  42.8 1.2 copy-start.2
  44.6 10.3 %collective-permute-start.4 = (f32[3,64,256]{2,1,0:T(8,128)S(1)}, f32[3,64,256]{2,1,0:T(8,128)S(1)}, u32[]{:S(2)}, u32[]{:S(2)}) collective-permute-start(f32[3,64,256]{2,1,0:T(8,128)S(1)} %get-tuple-element.19), channel_id=1, source_target_pairs={{16,0},{248,8},{32,16},{8,24},{48,32},{24,40},{64,48},{40,56},{80,... | collective-permute-start | bytes 589832 | tf_op jit(solution)/shard_map/ppermute | solution.py:17
  44.7 10.2 %collective-permute-start.3 = (f32[3,64,256]{2,1,0:T(8,128)S(1)}, f32[3,64,256]{2,1,0:T(8,128)S(1)}, u32[]{:S(2)}, u32[]{:S(2)}) collective-permute-start(f32[3,64,256]{2,1,0:T(8,128)S(1)} %get-tuple-element.18), channel_id=1, source_target_pairs={{8,0},{0,8},{24,16},{16,24},{40,32},{32,40},{56,48},{48,56},{72,64... | collective-permute-start | bytes 589832 | tf_op jit(solution)/shard_map/ppermute | solution.py:17
  52.2 5.4 %collective-permute-start.2 = (bf16[2,2,64,256]{3,2,1,0:T(8,128)(2,1)S(1)}, bf16[2,2,64,256]{3,2,1,0:T(8,128)(2,1)S(1)}, u32[]{:S(2)}, u32[]{:S(2)}) collective-permute-start(bf16[2,2,64,256]{3,2,1,0:T(8,128)(2,1)S(1)} %get-tuple-element.17), channel_id=1, source_target_pairs={{1,0},{0,1},{3,2},{2,3},{5,4},{4,5},{7,6},{6,7},{9,8},{8,9},{11,10... | collective-permute-start | bytes 393224 | tf_op jit(solution)/shard_map/ppermute | solution.py:17
  68.3 6.7 %collective-permute-start.8 = (bf16[4,1,2,64,256]{4,3,2,1,0:T(8,128)(2,1)S(1)}, bf16[4,1,2,64,256]{4,3,2,1,0:T(8,128)(2,1)S(1)}, u32[]{:S(2)}, u32[]{:S(2)}) collective-permute-start(bf16[4,1,2,64,256]{4,3,2,1,0:T(8,128)(2,1)S(1)} %slice.14), channel_id=1, source_target_pairs={{8,0},{0,8},{24,16},{16,24},{40,32},{32,40},{56,48},{48,56},{72,64... | collective-permute-start | bytes 786440 | tf_op jit(solution)/shard_map/ppermute | solution.py:17
  71.1 43.7 %collective-permute-start.6 = (bf16[256,2048]{1,0:T(8,128)(2,1)}, bf16[256,2048]{1,0:T(8,128)(2,1)}, u32[]{:S(2)}, u32[]{:S(2)}) collective-permute-start(bf16[256,2048]{1,0:T(8,128)(2,1)} %get-tuple-element.20), channel_id=1, source_target_pairs={{240,0},{24,8},{0,16},{40,24},{16,32},{56,40},{32,48},{72,56},{48,... | collective-permute-start | bytes 3145736 | tf_op jit(solution)/shard_map/ppermute | solution.py:17
  74.9 39.9 %collective-permute-start.7 = (bf16[256,2048]{1,0:T(8,128)(2,1)}, bf16[256,2048]{1,0:T(8,128)(2,1)}, u32[]{:S(2)}, u32[]{:S(2)}) collective-permute-start(bf16[256,2048]{1,0:T(8,128)(2,1)} %get-tuple-element.21), channel_id=1, source_target_pairs={{240,0},{24,8},{0,16},{40,24},{16,32},{56,40},{32,48},{72,56},{48,... | collective-permute-start | bytes 3145736 | tf_op jit(solution)/shard_map/ppermute | solution.py:17
  74.9 39.9 %collective-permute-start.5 = (bf16[4,2,2,64,256]{4,3,2,1,0:T(8,128)(2,1)S(1)}, bf16[4,2,2,64,256]{4,3,2,1,0:T(8,128)(2,1)S(1)}, u32[]{:S(2)}, u32[]{:S(2)}) collective-permute-start(bf16[4,2,2,64,256]{4,3,2,1,0:T(8,128)(2,1)S(1)} %all_to_all.10.mine.refs_2_), channel_id=1, source_target_pairs={{240,0},{24,8},{0,16},{40,24},{16,32},{56,40},{32,48},{72,56},{48,... | collective-permute-start | bytes 1572872 | tf_op jit(solution)/shard_map/ppermute | solution.py:17
  81.6 2.5 %collective-permute-start.10 = (f32[2048]{0:T(1024)S(1)}, f32[2048]{0:T(1024)S(1)}, u32[]{:S(2)}, u32[]{:S(2)}) collective-permute-start(f32[2048]{0:T(1024)S(1)} %bitcast.24), channel_id=1, source_target_pairs={{8,0},{0,8},{24,16},{16,24},{40,32},{32,40},{56,48},{48,56},{72,64... | collective-permute-start | bytes 24584 | tf_op jit(solution)/shard_map/ppermute | solution.py:17
  81.7 23.2 %collective-permute-start.11 = (f32[2048]{0:T(1024)S(1)}, f32[2048]{0:T(1024)S(1)}, u32[]{:S(2)}, u32[]{:S(2)}) collective-permute-start(f32[2048]{0:T(1024)S(1)} %bitcast.25), channel_id=1, source_target_pairs={{128,0},{136,8},{144,16},{152,24},{160,32},{168,40},{176,48},{184,... | collective-permute-start | bytes 24584 | tf_op jit(solution)/shard_map/ppermute | solution.py:17
  84.1 20.9 %collective-permute-start.12 = (f32[2048]{0:T(1024)S(1)}, f32[2048]{0:T(1024)S(1)}, u32[]{:S(2)}, u32[]{:S(2)}) collective-permute-start(f32[2048]{0:T(1024)S(1)} %bitcast.26), channel_id=1, source_target_pairs={{136,0},{128,8},{152,16},{144,24},{168,32},{160,40},{184,48},{176,... | collective-permute-start | bytes 24584 | tf_op jit(solution)/shard_map/ppermute | solution.py:17
  105.0 5.3 %collective-permute-start.14 = (f32[1,16,128]{2,1,0:T(8,128)S(1)}, f32[1,16,128]{2,1,0:T(8,128)S(1)}, u32[]{:S(2)}, u32[]{:S(2)}) collective-permute-start(f32[1,16,128]{2,1,0:T(8,128)S(1)} %add_bitcast_fusion), channel_id=1, source_target_pairs={{16,0},{24,8},{32,16},{40,24},{48,32},{56,40},{64,48},{72,56},{80,... | collective-permute-start | bytes 24584 | tf_op jit(solution)/shard_map/ppermute | solution.py:17
  109.5 3.7 %collective-permute-start.13 = (f32[1,16,128]{2,1,0:T(8,128)S(1)}, f32[1,16,128]{2,1,0:T(8,128)S(1)}, u32[]{:S(2)}, u32[]{:S(2)}) collective-permute-start(f32[1,16,128]{2,1,0:T(8,128)S(1)} %add_bitcast_fusion), channel_id=1, source_target_pairs={{112,0},{120,8},{0,16},{8,24},{16,32},{24,40},{32,48},{40,56},{48,... | collective-permute-start | bytes 24584 | tf_op jit(solution)/shard_map/ppermute | solution.py:17
  110.3 13.5 %collective-permute-start.16 = (f32[2,16,128]{2,1,0:T(8,128)S(1)}, f32[2,16,128]{2,1,0:T(8,128)S(1)}, u32[]{:S(2)}, u32[]{:S(2)}) collective-permute-start(f32[2,16,128]{2,1,0:T(8,128)S(1)} %pad_maximum_fusion.2), channel_id=1, source_target_pairs={{80,0},{88,8},{96,16},{104,24},{112,32},{120,40},{0,48},{8,56},{16... | collective-permute-start | bytes 49160 | tf_op jit(solution)/shard_map/ppermute | solution.py:17
  113.3 10.6 %collective-permute-start.15 = (f32[3,16,128]{2,1,0:T(8,128)S(1)}, f32[3,16,128]{2,1,0:T(8,128)S(1)}, u32[]{:S(2)}, u32[]{:S(2)}) collective-permute-start(f32[3,16,128]{2,1,0:T(8,128)S(1)} %pad_maximum_fusion.1.rows), channel_id=1, source_target_pairs={{48,0},{56,8},{64,16},{72,24},{80,32},{88,40},{96,48},{104,56},{11... | collective-permute-start | bytes 73736 | tf_op jit(solution)/shard_map/ppermute | solution.py:17
  114.8 2.2 %copy-start.1 = (f32[512,2048]{1,0:T(8,128)S(1)}, f32[512,2048]{1,0:T(8,128)}, u32[]{:S(2)}) copy-start(f32[512,2048]{1,0:T(8,128)} %get-tuple-element.22.refs_6_) | copy-start | bytes 12582916

commit v5 on v4

--- a/solution.py
+++ b/solution.py
@@ -115,21 +115,38 @@
     )(total, other, data)
 
 
-def corr_kernel(par, scale, lhs_first, lhs_second, own, near, out, acc):
+def fetches(pairs, sems):
+    chunks = pairs[0][1].shape[1] // CHUNK
+    copies = []
+    for j in range(chunks):
+        cols = pl.ds(j * CHUNK, CHUNK)
+        row = []
+        for i, (source, target) in enumerate(pairs):
+            copy = pltpu.make_async_copy(source.at[:, cols], target.at[:, cols], sems.at[i, j])
+            copy.start()
+            row.append(copy)
+        copies.append(row)
+    return copies
+
+
+def corr_kernel(par, scale, lhs_first, lhs_second, own, near_source, out, acc, near, sems):
     even = par[0] == 0
-    acc[...] = jnp.zeros_like(acc)
-
-    @pl.loop(0, own.shape[1] // CHUNK)
-    def _(step):
-        cols = pl.ds(pl.multiple_of(step * CHUNK, CHUNK), CHUNK)
+    for j, copies in enumerate(fetches([(near_source, near)], sems)):
+        for copy in copies:
+            copy.wait()
+        cols = pl.ds(j * CHUNK, CHUNK)
         near_cols = near[:, cols]
         rhs_first = jnp.where(even, own[:, cols], near_cols)
         near_scale = jnp.where(even, scale[:, cols], 1.0)
         rhs_second = (near_cols.astype(jnp.float32) * near_scale).astype(jnp.bfloat16)
         for pair, (lhs, rhs) in enumerate(((lhs_first, rhs_first), (lhs_second, rhs_second))):
-            acc[pair] += lax.dot_general(
+            products = lax.dot_general(
                 lhs[:, cols], rhs, (((1,), (1,)), ((), ())), preferred_element_type=jnp.float32
             )
+            if j == 0:
+                acc[pair] = products
+            else:
+                acc[pair] += products
 
     parts, _, _, rows, cols = out.shape
     half = parts * rows
@@ -147,9 +164,13 @@
     return pl.pallas_call(
         corr_kernel,
         out_shape=jax.ShapeDtypeStruct((parts, 2, 2, half // parts, half), WIRE),
-        in_specs=[pl.BlockSpec(memory_space=pltpu.SMEM)] + [vmem] * 5,
+        in_specs=[pl.BlockSpec(memory_space=pltpu.SMEM)] + [vmem] * 4 + [pl.BlockSpec(memory_space=pl.ANY)],
         out_specs=vmem,
-        scratch_shapes=[pltpu.VMEM((2, both, both), jnp.float32)],
+        scratch_shapes=[
+            pltpu.VMEM((2, both, both), jnp.float32),
+            pltpu.VMEM((both, cols), jnp.bfloat16),
+            pltpu.SemaphoreType.DMA((1, cols // CHUNK)),
+        ],
         cost_estimate=pl.CostEstimate(flops=4 * both * both * cols, bytes_accessed=8 * both * cols, transcendentals=0),
         compiler_params=pltpu.CompilerParams(vmem_limit_bytes=24 << 20),
         name="corr",
@@ -173,44 +194,67 @@
     mat[half:, base : base + half] = -imag
 
 
-def applied(mat, base, block):
-    return jnp.dot(mat[:, base : base + block.shape[0]], block[...], preferred_element_type=jnp.float32)
-
-
-def early_kernel(par, mine, mate_resid, own, mate, near, mate_near, early, kernel_part, mat):
+def early_kernel(par, mine, mate_resid, own_source, mate_source, near_source, mate_near_source, early, kernel_part, mat, own, second, near, out, sems, out_sems):
     both = early.shape[0]
 
-    @pl.when(pl.program_id(0) == 0)
-    def _():
+    def run(second_source):
+        copies = fetches([(near_source, near), (second_source, second), (own_source, own)], sems)
         place(mat, 0, assembled(mine, 1, False))
         place(mat, both, assembled(mate_resid, 0, False))
-
-    second = jnp.where(par[0] == 0, mate_near[...], mate[...])
-    fields = applied(mat, 0, near) + applied(mat, both, second)
-    kernel_part[...] = jnp.sum(own[...].astype(jnp.float32) * fields, axis=0, keepdims=True)
-    early[...] = fields
-
-
-def late_kernel(inv_norm, par, scale, mine, far_resid, far_real, far_imag, early, mate, mate_near, adjoint, mat):
-    first = pl.program_id(0) == 0
-    even = par[0] == 0
+        sends = []
+        for j, row in enumerate(copies):
+            for copy in row:
+                copy.wait()
+            cols = pl.ds(j * CHUNK, CHUNK)
+            fields = jnp.dot(mat[:, :both], near[:, cols], preferred_element_type=jnp.float32)
+            fields = fields + jnp.dot(mat[:, both:], second[:, cols], preferred_element_type=jnp.float32)
+            out[j] = fields
+            send = pltpu.make_async_copy(out.at[j], early.at[:, cols], out_sems.at[j])
+            send.start()
+            sends.append(send)
+            kernel_part[:, cols] = jnp.sum(own[:, cols].astype(jnp.float32) * fields, axis=0, keepdims=True)
+        for send in sends:
+            send.wait()
+
+    @pl.when(par[0] == 0)
+    def _():
+        run(mate_near_source)
+
+    @pl.when(par[0] == 1)
+    def _():
+        run(mate_source)
+
+
+def late_kernel(inv_norm, par, scale, mine, far_resid, early_source, far_real, far_imag, mate_source, mate_near_source, adjoint, mat, far, second, early, out, sems, out_sems):
     both = early.shape[0]
-
-    @pl.when(first)
-    def _():
+    half = both // 2
+
+    def run(second_source, second_resid):
+        parts = [(far_real, far.at[:half]), (far_imag, far.at[half:]), (second_source, second), (early_source, early)]
+        copies = fetches(parts, sems)
         place(mat, 0, assembled(far_resid, 1, True))
-
-    @pl.when(first & even)
-    def _():
-        place(mat, both, assembled(mine, 0, True))
-
-    @pl.when(first & jnp.logical_not(even))
-    def _():
-        place(mat, both, assembled(far_resid, 0, True))
-
-    second = jnp.where(even, mate[...], mate_near[...])
-    term = applied(mat, 0, far_real) + applied(mat, both // 2, far_imag) + applied(mat, both, second)
-    adjoint[...] = ((early[...] + term) * (inv_norm * scale[...])).reshape(adjoint.shape)
+        place(mat, both, assembled(second_resid, 0, True))
+        sends = []
+        for j, row in enumerate(copies):
+            for copy in row:
+                copy.wait()
+            cols = pl.ds(j * CHUNK, CHUNK)
+            fields = early[:, cols] + jnp.dot(mat[:, :both], far[:, cols], preferred_element_type=jnp.float32)
+            fields = fields + jnp.dot(mat[:, both:], second[:, cols], preferred_element_type=jnp.float32)
+            out[j] = (fields * (inv_norm * scale[:, cols])).reshape(out.shape[1:])
+            send = pltpu.make_async_copy(out.at[j], adjoint.at[:, :, cols], out_sems.at[j])
+            send.start()
+            sends.append(send)
+        for send in sends:
+            send.wait()
+
+    @pl.when(par[0] == 0)
+    def _():
+        run(mate_source, mine)
+
+    @pl.when(par[0] == 1)
+    def _():
+        run(mate_near_source, far_resid)
 
 
 def ring_kernel(place_of, rows, above, below, out, slots):
@@ -241,54 +285,58 @@
     )(place_of, rows, above, below)
 
 
-def column_block(array):
-    shape = array.shape[:-1] + (CHUNK,)
-    return pl.BlockSpec(shape, lambda j: (0,) * (array.ndim - 1) + (j,))
-
-
 def early_fields(par, mine, mate_resid, own, mate, near, mate_near):
     both, cols = own.shape
-    wholes = (mine, mate_resid)
-    blocks = (own, mate, near, mate_near)
+    vmem = pl.BlockSpec(memory_space=pltpu.VMEM)
+    anywhere = pl.BlockSpec(memory_space=pl.ANY)
     return pl.pallas_call(
         early_kernel,
         out_shape=(
             pltpu.HBM((both, cols), jnp.float32),
             jax.ShapeDtypeStruct((1, cols), jnp.float32),
         ),
-        grid=(cols // CHUNK,),
-        in_specs=[pl.BlockSpec(memory_space=pltpu.SMEM)] + [whole(x) for x in wholes] + [column_block(x) for x in blocks],
-        out_specs=(
-            pl.BlockSpec((both, CHUNK), lambda j: (0, j)),
-            pl.BlockSpec((1, CHUNK), lambda j: (0, j)),
-        ),
-        scratch_shapes=[pltpu.VMEM((both, 2 * both), jnp.bfloat16)],
-        cost_estimate=pl.CostEstimate(flops=4 * both * both * cols, bytes_accessed=12 * both * cols, transcendentals=0),
-        compiler_params=pltpu.CompilerParams(vmem_limit_bytes=24 << 20),
+        in_specs=[pl.BlockSpec(memory_space=pltpu.SMEM)] + [vmem] * 2 + [anywhere] * 4,
+        out_specs=(pl.BlockSpec(memory_space=pltpu.HBM), vmem),
+        scratch_shapes=[pltpu.VMEM((both, 2 * both), jnp.bfloat16)]
+        + [pltpu.VMEM((both, cols), jnp.bfloat16)] * 3
+        + [
+            pltpu.VMEM((cols // CHUNK, both, CHUNK), jnp.float32),
+            pltpu.SemaphoreType.DMA((3, cols // CHUNK)),
+            pltpu.SemaphoreType.DMA((cols // CHUNK,)),
+        ],
+        cost_estimate=pl.CostEstimate(flops=4 * both * both * cols, bytes_accessed=10 * both * cols, transcendentals=0),
+        compiler_params=pltpu.CompilerParams(vmem_limit_bytes=20 << 20),
         name="early",
-    )(par, *wholes, *blocks)
+    )(par, mine, mate_resid, own, mate, near, mate_near)
 
 
 def late_fields(par, scale, mine, far_resid, far, early, mate, mate_near, inv_norm):
     both, cols = early.shape
-    blocks = (*far, early, mate, mate_near)
+    half = both // 2
+    vmem = pl.BlockSpec(memory_space=pltpu.VMEM)
+    hbm = pl.BlockSpec(memory_space=pltpu.HBM)
 
     def body(*refs):
         late_kernel(inv_norm, *refs)
 
     return pl.pallas_call(
         body,
-        out_shape=jax.ShapeDtypeStruct((2, both // 2, cols), jnp.float32),
-        grid=(cols // CHUNK,),
-        in_specs=[pl.BlockSpec(memory_space=pltpu.SMEM), column_block(scale)]
-        + [whole(mine), whole(far_resid)]
-        + [column_block(x) for x in blocks],
-        out_specs=pl.BlockSpec((2, both // 2, CHUNK), lambda j: (0, 0, j)),
-        scratch_shapes=[pltpu.VMEM((both, 2 * both), jnp.bfloat16)],
+        out_shape=jax.ShapeDtypeStruct((2, half, cols), jnp.float32),
+        in_specs=[pl.BlockSpec(memory_space=pltpu.SMEM)] + [vmem] * 3 + [hbm] * 5,
+        out_specs=hbm,
+        scratch_shapes=[
+            pltpu.VMEM((both, 2 * both), jnp.bfloat16),
+            pltpu.VMEM((both, cols), jnp.bfloat16),
+            pltpu.VMEM((both, cols), jnp.bfloat16),
+            pltpu.VMEM((both, cols), jnp.float32),
+            pltpu.VMEM((cols // CHUNK, 2, half, CHUNK), jnp.float32),
+            pltpu.SemaphoreType.DMA((4, cols // CHUNK)),
+            pltpu.SemaphoreType.DMA((cols // CHUNK,)),
+        ],
         cost_estimate=pl.CostEstimate(flops=4 * both * both * cols, bytes_accessed=12 * both * cols, transcendentals=0),
-        compiler_params=pltpu.CompilerParams(vmem_limit_bytes=24 << 20),
+        compiler_params=pltpu.CompilerParams(vmem_limit_bytes=62 << 20),
         name="late",
-    )(par, scale, mine, far_resid, *blocks)
+    )(par, scale, mine, far_resid, early, *far, mate, mate_near)
 
 
 def shards(green, source_weight, observed, amp_weight, pair_used):

time: 125 us -> 122 us (0.976)
  Pallas kernels: 20.5 us -> 18.4 us
  local copies, waits for them, and re-layouts: 6.87 us -> 5.46 us
    unnamed x12 -> x14, local copies, waits for them, and re-layouts: 3.51 us -> 2.19 us
  transfers between devices with their start and end apart: 18 -> 18, of which waited for: 7 -> 7; matrix products, arithmetic and copies ran while one was open for 5% -> 5% of each run, Pallas kernels for 16% -> 15%
where the time goes in v5:
time: 122 us
  waiting for transfers between devices  51.4 us (42%)
  starting transfers between devices  32 us (26%)
  Pallas kernels  18.4 us (15%)
  blocking collectives  10.6 us (9%)
  local copies, waits for them, and re-layouts  5.46 us (4%)
  other arithmetic  3.39 us (3%)
    ppermute x17, waiting for transfers between devices, permuted(): lax.ppermute(block, axis, [(source_of(i) % size, i) for i in range(size)])  49.2 us
    ppermute x17, starting transfers between devices, permuted(): lax.ppermute(block, axis, [(source_of(i) % size, i) for i in range(size)])  28 us
    all_to_all x1, blocking collectives, shards(): lax.all_to_all(resid, 'grid', 0, 0, tiled=True, axis_index_groups=along_x)  10.6 us
    pallas_call x1, Pallas kernels, late_fields(): pl.pallas_call(body, out_shape=jax.ShapeDtypeStruct((2, half, cols), jnp....  6.91 us
    pallas_call x1, Pallas kernels, early_fields(): pl.pallas_call(early_kernel, out_shape=(pltpu.HBM((both, cols), jnp.float...  5.51 us
    pallas_call x1, Pallas kernels, correlations(): pl.pallas_call(corr_kernel, out_shape=jax.ShapeDtypeStruct((parts, 2, 2,...  4.65 us
    all_to_all x1, starting transfers between devices, shards(): lax.all_to_all(partials, 'grid', 0, 0, tiled=True, axis_index_groups=alon...  4.02 us
    squeeze x1, local copies, waits for them, and re-layouts, shards(): cuts = (green[0], green[1])  3.25 us
  transfers between devices with their start and end apart: 18, of which 7 were waited for; matrix products, arithmetic and copies ran while one was open for 5% of the time, Pallas kernels for 15%

profile of v5, /device:TPU:1, one launch (start us, length us, event | category | flops | bytes accessed | tf_op | source)
XLA Modules:
  0.0 122.1 jit_solution(13245017281031574431)
XLA Ops:
  0.6 3.3 %collective-permute-start.1 = (bf16[512,2048]{1,0:T(8,128)(2,1)}, bf16[512,2048]{1,0:T(8,128)(2,1)}, u32[]{:S(2)}, u32[]{:S(2)}) collective-permute-start(bf16[512,2048]{1,0:T(8,128)(2,1)} %bitcast.17), channel_id=1, source_target_pairs={{8,0},{0,8},{24,16},{16,24},{40,32},{32,40},{56,48},{48,56},{72,64... | collective-permute-start | bytes 6291464 | tf_op jit(solution)/shard_map/ppermute | solution.py:17
  3.9 0.0 collective-permute-start
  3.9 0.7 broadcast_select_fusion
  4.6 3.3 %slice_bitcast_fusion = (bf16[256,2048]{1,0:T(8,128)(2,1)}, bf16[256,2048]{1,0:T(8,128)(2,1)}) fusion(bf16[2,256,2048]{2,1,0:T(8,128)(2,1)} %param.5), kind=kLoop, calls=%fused_computation.2 | loop fusion | bytes 4194304 | tf_op jit(solution)/shard_map/squeeze | solution.py:368
  7.9 0.6 multiply_convert_fusion.lhs_second
  8.5 0.0 collective-permute-done.1.mate_source.refs_7_
  8.5 0.1 copy-done.4
  8.6 2.0 %multiply_convert_fusion.1.lhs_first = bf16[512,2048]{1,0:T(8,128)(2,1)S(1)} fusion(bf16[512,2048]{1,0:T(8,128)(2,1)} %collective-permute-done.1.mate_source.refs_7_, f32[2048]{0:T(1024)S(1)} %copy-done.4), kind=kLoop, calls=%fused_computation.1 | loop fusion | flops 3145728 | bytes 4202496 | tf_op jit(solution)/shard_map/convert_element_type | solution.py:366
  10.6 21.9 %collective-permute-done.near_source = bf16[512,2048]{1,0:T(8,128)(2,1)} collective-permute-done((bf16[512,2048]{1,0:T(8,128)(2,1)}, bf16[512,2048]{1,0:T(8,128)(2,1)}, u32[]{:S(2)}, u32[]{:S(2)}) %collective-permute-start) | collective-permute-done | bytes 2097184 | tf_op jit(solution)/shard_map/ppermute | solution.py:17
  32.5 0.5 collective-permute-start.7
  33.0 4.6 %corr.1 = bf16[4,2,2,64,256]{4,3,2,1,0:T(8,128)(2,1)} custom-call(s32[1]{0:T(128)} %bitcast.par.refs_0_, f32[1,2048]{1,0:T(1,128)S(1)} %bitcast.22, bf16[512,2048]{1,0:T(8,128)(2,1)S(1)} %multiply_convert_fusion.1.lhs_first, bf16[512,2048]{1,0:T(8,128)(2,1)S(1)} %multiply_convert_fusion.lhs_second, bf16[512,2048]{1,0:T(8,128)(2,1)S(1)} %bitcast.19, ...), custom_call_target="tpu_custom_call" | custom-call | flops 2147483648 | bytes 8388608 | tf_op jit(solution)/shard_map/corr/pallas_call | solution.py:164
  37.7 4.0 %all-to-all-start = ((bf16[4,2,2,64,256]{4,3,2,1,0:T(8,128)(2,1)}), bf16[4,2,2,64,256]{4,3,2,1,0:T(8,128)(2,1)S(1)}, u32[]{:S(2)}, u32[]{:S(2)}) async-start(bf16[4,2,2,64,256]{4,3,2,1,0:T(8,128)(2,1)} %corr.1), calls=%async_computation | async-start | bytes 1048576 | tf_op jit(solution)/shard_map/all_to_all | solution.py:376
  41.7 1.2 copy-done.2
  43.0 0.6 prep.1
  43.5 0.1 collective-permute-start.4
  43.6 5.1 %collective-permute-start.3 = (f32[3,64,256]{2,1,0:T(8,128)S(1)}, f32[3,64,256]{2,1,0:T(8,128)S(1)}, u32[]{:S(2)}, u32[]{:S(2)}) collective-permute-start(f32[3,64,256]{2,1,0:T(8,128)S(1)} %get-tuple-element.18), channel_id=1, source_target_pairs={{8,0},{0,8},{24,16},{16,24},{40,32},{32,40},{56,48},{48,56},{72,64... | collective-permute-start | bytes 589832 | tf_op jit(solution)/shard_map/ppermute | solution.py:17
  48.8 2.3 %all-to-all-done.pieces = bf16[4,2,2,64,256]{4,3,2,1,0:T(8,128)(2,1)S(1)} async-done(((bf16[4,2,2,64,256]{4,3,2,1,0:T(8,128)(2,1)}), bf16[4,2,2,64,256]{4,3,2,1,0:T(8,128)(2,1)S(1)}, u32[]{:S(2)}, u32[]{:S(2)}) %all-to-all-start) | async-done | bytes 524320 | tf_op jit(solution)/shard_map/all_to_all | solution.py:376
  51.0 0.1 summed.1
  51.1 2.7 %collective-permute-start.2 = (bf16[2,2,64,256]{3,2,1,0:T(8,128)(2,1)S(1)}, bf16[2,2,64,256]{3,2,1,0:T(8,128)(2,1)S(1)}, u32[]{:S(2)}, u32[]{:S(2)}) collective-permute-start(bf16[2,2,64,256]{3,2,1,0:T(8,128)(2,1)S(1)} %get-tuple-element.17), channel_id=1, source_target_pairs={{1,0},{0,1},{3,2},{2,3},{5,4},{4,5},{7,6},{6,7},{9,8},{8,9},{11,10... | collective-permute-start | bytes 393224 | tf_op jit(solution)/shard_map/ppermute | solution.py:17
  53.8 0.0 collective-permute-done.4
  53.9 2.6 %collective-permute-done.2.refs_1_ = bf16[2,2,64,256]{3,2,1,0:T(8,128)(2,1)S(1)} collective-permute-done((bf16[2,2,64,256]{3,2,1,0:T(8,128)(2,1)S(1)}, bf16[2,2,64,256]{3,2,1,0:T(8,128)(2,1)S(1)}, u32[]{:S(2)}, u32[]{:S(2)}) %collective-permute-start.2) | collective-permute-done | bytes 131104 | tf_op jit(solution)/shard_map/ppermute | solution.py:17
  56.5 0.1 resid.1
  56.6 10.6 %all_to_all.10.mine.refs_2_ = bf16[4,2,2,64,256]{4,3,2,1,0:T(8,128)(2,1)S(1)} all-to-all(bf16[4,2,2,64,256]{4,3,2,1,0:T(8,128)(2,1)S(1)} %resid.1), channel_id=1, replica_groups={{0,2,4,6},{1,3,5,7},{8,10,12,14},{9,11,13,15},{16,18,20,22},{17,19,21,2..., dimensions={0} | all-to-all | bytes 1048576 | tf_op jit(solution)/shard_map/all_to_all | solution.py:380
  67.2 2.8 %collective-permute-start.6 = (bf16[4,1,2,64,256]{4,3,2,1,0:T(8,128)(2,1)S(1)}, bf16[4,1,2,64,256]{4,3,2,1,0:T(8,128)(2,1)S(1)}, u32[]{:S(2)}, u32[]{:S(2)}) collective-permute-start(bf16[4,1,2,64,256]{4,3,2,1,0:T(8,128)(2,1)S(1)} %slice.14), channel_id=1, source_target_pairs={{8,0},{0,8},{24,16},{16,24},{40,32},{32,40},{56,48},{48,56},{72,64... | collective-permute-start | bytes 786440 | tf_op jit(solution)/shard_map/ppermute | solution.py:17
  70.0 3.9 %collective-permute-start.8 = (bf16[256,2048]{1,0:T(8,128)(2,1)}, bf16[256,2048]{1,0:T(8,128)(2,1)}, u32[]{:S(2)}, u32[]{:S(2)}) collective-permute-start(bf16[256,2048]{1,0:T(8,128)(2,1)} %get-tuple-element.21), channel_id=1, source_target_pairs={{240,0},{24,8},{0,16},{40,24},{16,32},{56,40},{32,48},{72,56},{48,... | collective-permute-start | bytes 3145736 | tf_op jit(solution)/shard_map/ppermute | solution.py:17
  73.8 0.0 collective-permute-start.9
  73.8 0.0 collective-permute-start.5
  73.9 0.0 collective-permute-done.6.mate_resid
  73.9 0.0 collective-permute-done.7.mate_near_source.refs_8_
  73.9 5.5 %early.1 = (f32[512,2048]{1,0:T(8,128)}, f32[1,2048]{1,0:T(1,128)S(1)}) custom-call(s32[1]{0:T(128)} %bitcast.par.refs_0_, bf16[4,2,2,64,256]{4,3,2,1,0:T(8,128)(2,1)S(1)} %all_to_all.10.mine.refs_2_, bf16[4,1,2,64,256]{4,3,2,1,0:T(8,128)(2,1)S(1)} %collective-permute-done.6.mate_resid, bf16[512,2048]{1,0:T(8,128)(2,1)S(1)} %bitcast.20, ...), custom_call_target="tpu_custom_call" | custom-call | flops 2147483648 | bytes 10485760 | tf_op jit(solution)/shard_map/early/pallas_call | solution.py:292
  79.4 0.1 collective-permute-start.10
  79.5 2.4 %collective-permute-start.11 = (f32[2048]{0:T(1024)S(1)}, f32[2048]{0:T(1024)S(1)}, u32[]{:S(2)}, u32[]{:S(2)}) collective-permute-start(f32[2048]{0:T(1024)S(1)} %bitcast.25), channel_id=1, source_target_pairs={{128,0},{136,8},{144,16},{152,24},{160,32},{168,40},{176,48},{184,... | collective-permute-start | bytes 24584 | tf_op jit(solution)/shard_map/ppermute | solution.py:17
  81.9 0.0 collective-permute-done.10
  81.9 1.1 collective-permute-start.12
  83.0 20.7 %collective-permute-done.11 = f32[2048]{0:T(1024)S(1)} collective-permute-done((f32[2048]{0:T(1024)S(1)}, f32[2048]{0:T(1024)S(1)}, u32[]{:S(2)}, u32[]{:S(2)}) %collective-permute-start.11) | collective-permute-done | bytes 8224 | tf_op jit(solution)/shard_map/ppermute | solution.py:17
  103.8 0.2 collective-permute-done.12
  103.9 4.4 %collective-permute-start.14 = (f32[1,16,128]{2,1,0:T(8,128)S(1)}, f32[1,16,128]{2,1,0:T(8,128)S(1)}, u32[]{:S(2)}, u32[]{:S(2)}) collective-permute-start(f32[1,16,128]{2,1,0:T(8,128)S(1)} %add_bitcast_fusion), channel_id=1, source_target_pairs={{16,0},{24,8},{32,16},{40,24},{48,32},{56,40},{64,48},{72,56},{80,... | collective-permute-start | bytes 24584 | tf_op jit(solution)/shard_map/ppermute | solution.py:17
  108.4 0.0 collective-permute-start.13
  108.4 0.8 collective-permute-done.14
  109.2 0.0 collective-permute-start.16
  109.2 2.9 %collective-permute-done.13 = f32[1,16,128]{2,1,0:T(8,128)S(1)} collective-permute-done((f32[1,16,128]{2,1,0:T(8,128)S(1)}, f32[1,16,128]{2,1,0:T(8,128)S(1)}, u32[]{:S(2)}, u32[]{:S(2)}) %collective-permute-start.13) | collective-permute-done | bytes 8224 | tf_op jit(solution)/shard_map/ppermute | solution.py:17
  112.1 1.6 %collective-permute-start.15 = (f32[3,16,128]{2,1,0:T(8,128)S(1)}, f32[3,16,128]{2,1,0:T(8,128)S(1)}, u32[]{:S(2)}, u32[]{:S(2)}) collective-permute-start(f32[3,16,128]{2,1,0:T(8,128)S(1)} %pad_maximum_fusion.1.rows), channel_id=1, source_target_pairs={{48,0},{56,8},{64,16},{72,24},{80,32},{88,40},{96,48},{104,56},{11... | collective-permute-start | bytes 73736 | tf_op jit(solution)/shard_map/ppermute | solution.py:17
  113.6 0.0 collective-permute-done.8.refs_5_
  113.6 0.0 collective-permute-done.9.refs_6_
  113.6 0.0 collective-permute-done.5.refs_3_
  113.7 0.9 copy-done.6
  114.5 6.9 %late.1 = f32[2,256,2048]{2,1,0:T(8,128)} custom-call(s32[1]{0:T(128)} %bitcast.par.refs_0_, f32[1,2048]{1,0:T(1,128)} %bitcast.21, bf16[4,2,2,64,256]{4,3,2,1,0:T(8,128)(2,1)} %copy-done.1, bf16[4,2,2,64,256]{4,3,2,1,0:T(8,128)(2,1)} %copy-done.6, f32[512,2048]{1,0:T(8,128)} %get-tuple-element.20.refs_4_, bf16[256,2048]{1,0:T(8,128)(2,1)} %collective-permute-done.8.refs_5_, ...), custom_call_target="tpu_custom_call" | custom-call | flops 2147483648 | bytes 12582912 | tf_op jit(solution)/shard_map/late/pallas_call | solution.py:322
  121.5 0.6 ring_sum.1
  (21 shorter events, 0.1 us)
Async XLA Ops:
  0.6 7.8 %collective-permute-start.1 = (bf16[512,2048]{1,0:T(8,128)(2,1)}, bf16[512,2048]{1,0:T(8,128)(2,1)}, u32[]{:S(2)}, u32[]{:S(2)}) collective-permute-start(bf16[512,2048]{1,0:T(8,128)(2,1)} %bitcast.17), channel_id=1, source_target_pairs={{8,0},{0,8},{24,16},{16,24},{40,32},{32,40},{56,48},{48,56},{72,64... | collective-permute-start | bytes 6291464 | tf_op jit(solution)/shard_map/ppermute | solution.py:17
  3.9 28.6 %collective-permute-start = (bf16[512,2048]{1,0:T(8,128)(2,1)}, bf16[512,2048]{1,0:T(8,128)(2,1)}, u32[]{:S(2)}, u32[]{:S(2)}) collective-permute-start(bf16[512,2048]{1,0:T(8,128)(2,1)} %bitcast.18), channel_id=1, source_target_pairs={{16,0},{248,8},{32,16},{8,24},{48,32},{24,40},{64,48},{40,56},{80,... | collective-permute-start | bytes 6291464 | tf_op jit(solution)/shard_map/ppermute | solution.py:17
  4.6 3.3 %copy-start = (bf16[2,256,2048]{2,1,0:T(8,128)(2,1)S(1)}, bf16[2,256,2048]{2,1,0:T(8,128)(2,1)}, u32[]{:S(2)}) copy-start(bf16[2,256,2048]{2,1,0:T(8,128)(2,1)} %param.5) | copy-start | bytes 6291460
  7.9 0.7 copy-start.4
  32.5 41.3 %collective-permute-start.7 = (bf16[512,2048]{1,0:T(8,128)(2,1)}, bf16[512,2048]{1,0:T(8,128)(2,1)}, u32[]{:S(2)}, u32[]{:S(2)}) collective-permute-start(bf16[512,2048]{1,0:T(8,128)(2,1)} %collective-permute-done.near_source), channel_id=1, source_target_pairs={{8,0},{0,8},{24,16},{16,24},{40,32},{32,40},{56,48},{48,56},{72,64... | collective-permute-start | bytes 6291464 | tf_op jit(solution)/shard_map/ppermute | solution.py:17
  33.0 8.7 %copy-start.3 = (f32[2,256,256]{2,1,0:T(8,128)S(1)}, f32[2,256,256]{2,1,0:T(8,128)}, u32[]{:S(2)}) copy-start(f32[2,256,256]{2,1,0:T(8,128)} %amp_weight.1) | copy-start | bytes 1572868
  33.0 8.7 %copy-start.5 = (s32[1,2]{1,0:T(1,128)S(1)}, s32[1,2]{1,0:T(1,128)}, u32[]{:S(2)}) copy-start(s32[1,2]{1,0:T(1,128)} %used.1) | copy-start | bytes 28
  37.7 13.3 %all-to-all-start = ((bf16[4,2,2,64,256]{4,3,2,1,0:T(8,128)(2,1)}), bf16[4,2,2,64,256]{4,3,2,1,0:T(8,128)(2,1)S(1)}, u32[]{:S(2)}, u32[]{:S(2)}) async-start(bf16[4,2,2,64,256]{4,3,2,1,0:T(8,128)(2,1)} %corr.1), calls=%async_computation | async-start | bytes 1048576 | tf_op jit(solution)/shard_map/all_to_all | solution.py:376
  41.7 1.2 %copy-start.2 = (f32[2,2,256,256]{3,2,1,0:T(8,128)S(1)}, f32[2,2,256,256]{3,2,1,0:T(8,128)}, u32[]{:S(2)}) copy-start(f32[2,2,256,256]{3,2,1,0:T(8,128)} %observed.1) | copy-start | bytes 3145732
  43.5 10.3 %collective-permute-start.4 = (f32[3,64,256]{2,1,0:T(8,128)S(1)}, f32[3,64,256]{2,1,0:T(8,128)S(1)}, u32[]{:S(2)}, u32[]{:S(2)}) collective-permute-start(f32[3,64,256]{2,1,0:T(8,128)S(1)} %get-tuple-element.19), channel_id=1, source_target_pairs={{16,0},{248,8},{32,16},{8,24},{48,32},{24,40},{64,48},{40,56},{80,... | collective-permute-start | bytes 589832 | tf_op jit(solution)/shard_map/ppermute | solution.py:17
  43.6 10.2 %collective-permute-start.3 = (f32[3,64,256]{2,1,0:T(8,128)S(1)}, f32[3,64,256]{2,1,0:T(8,128)S(1)}, u32[]{:S(2)}, u32[]{:S(2)}) collective-permute-start(f32[3,64,256]{2,1,0:T(8,128)S(1)} %get-tuple-element.18), channel_id=1, source_target_pairs={{8,0},{0,8},{24,16},{16,24},{40,32},{32,40},{56,48},{48,56},{72,64... | collective-permute-start | bytes 589832 | tf_op jit(solution)/shard_map/ppermute | solution.py:17
  51.1 5.4 %collective-permute-start.2 = (bf16[2,2,64,256]{3,2,1,0:T(8,128)(2,1)S(1)}, bf16[2,2,64,256]{3,2,1,0:T(8,128)(2,1)S(1)}, u32[]{:S(2)}, u32[]{:S(2)}) collective-permute-start(bf16[2,2,64,256]{3,2,1,0:T(8,128)(2,1)S(1)} %get-tuple-element.17), channel_id=1, source_target_pairs={{1,0},{0,1},{3,2},{2,3},{5,4},{4,5},{7,6},{6,7},{9,8},{8,9},{11,10... | collective-permute-start | bytes 393224 | tf_op jit(solution)/shard_map/ppermute | solution.py:17
  67.2 12.2 %copy-start.1 = (bf16[4,2,2,64,256]{4,3,2,1,0:T(8,128)(2,1)}, bf16[4,2,2,64,256]{4,3,2,1,0:T(8,128)(2,1)S(1)}, u32[]{:S(2)}) copy-start(bf16[4,2,2,64,256]{4,3,2,1,0:T(8,128)(2,1)S(1)} %all_to_all.10.mine.refs_2_) | copy-start | bytes 1572868
  67.2 6.7 %collective-permute-start.6 = (bf16[4,1,2,64,256]{4,3,2,1,0:T(8,128)(2,1)S(1)}, bf16[4,1,2,64,256]{4,3,2,1,0:T(8,128)(2,1)S(1)}, u32[]{:S(2)}, u32[]{:S(2)}) collective-permute-start(bf16[4,1,2,64,256]{4,3,2,1,0:T(8,128)(2,1)S(1)} %slice.14), channel_id=1, source_target_pairs={{8,0},{0,8},{24,16},{16,24},{40,32},{32,40},{56,48},{48,56},{72,64... | collective-permute-start | bytes 786440 | tf_op jit(solution)/shard_map/ppermute | solution.py:17
  70.0 43.7 %collective-permute-start.8 = (bf16[256,2048]{1,0:T(8,128)(2,1)}, bf16[256,2048]{1,0:T(8,128)(2,1)}, u32[]{:S(2)}, u32[]{:S(2)}) collective-permute-start(bf16[256,2048]{1,0:T(8,128)(2,1)} %get-tuple-element.21), channel_id=1, source_target_pairs={{240,0},{24,8},{0,16},{40,24},{16,32},{56,40},{32,48},{72,56},{48,... | collective-permute-start | bytes 3145736 | tf_op jit(solution)/shard_map/ppermute | solution.py:17
  73.8 39.8 %collective-permute-start.9 = (bf16[256,2048]{1,0:T(8,128)(2,1)}, bf16[256,2048]{1,0:T(8,128)(2,1)}, u32[]{:S(2)}, u32[]{:S(2)}) collective-permute-start(bf16[256,2048]{1,0:T(8,128)(2,1)} %get-tuple-element.22), channel_id=1, source_target_pairs={{240,0},{24,8},{0,16},{40,24},{16,32},{56,40},{32,48},{72,56},{48,... | collective-permute-start | bytes 3145736 | tf_op jit(solution)/shard_map/ppermute | solution.py:17
  73.8 39.8 %collective-permute-start.5 = (bf16[4,2,2,64,256]{4,3,2,1,0:T(8,128)(2,1)S(1)}, bf16[4,2,2,64,256]{4,3,2,1,0:T(8,128)(2,1)S(1)}, u32[]{:S(2)}, u32[]{:S(2)}) collective-permute-start(bf16[4,2,2,64,256]{4,3,2,1,0:T(8,128)(2,1)S(1)} %all_to_all.10.mine.refs_2_), channel_id=1, source_target_pairs={{240,0},{24,8},{0,16},{40,24},{16,32},{56,40},{32,48},{72,56},{48,... | collective-permute-start | bytes 1572872 | tf_op jit(solution)/shard_map/ppermute | solution.py:17
  79.4 2.5 %collective-permute-start.10 = (f32[2048]{0:T(1024)S(1)}, f32[2048]{0:T(1024)S(1)}, u32[]{:S(2)}, u32[]{:S(2)}) collective-permute-start(f32[2048]{0:T(1024)S(1)} %bitcast.24), channel_id=1, source_target_pairs={{8,0},{0,8},{24,16},{16,24},{40,32},{32,40},{56,48},{48,56},{72,64... | collective-permute-start | bytes 24584 | tf_op jit(solution)/shard_map/ppermute | solution.py:17
  79.5 24.2 %collective-permute-start.11 = (f32[2048]{0:T(1024)S(1)}, f32[2048]{0:T(1024)S(1)}, u32[]{:S(2)}, u32[]{:S(2)}) collective-permute-start(f32[2048]{0:T(1024)S(1)} %bitcast.25), channel_id=1, source_target_pairs={{128,0},{136,8},{144,16},{152,24},{160,32},{168,40},{176,48},{184,... | collective-permute-start | bytes 24584 | tf_op jit(solution)/shard_map/ppermute | solution.py:17
  81.9 22.0 %collective-permute-start.12 = (f32[2048]{0:T(1024)S(1)}, f32[2048]{0:T(1024)S(1)}, u32[]{:S(2)}, u32[]{:S(2)}) collective-permute-start(f32[2048]{0:T(1024)S(1)} %bitcast.26), channel_id=1, source_target_pairs={{136,0},{128,8},{152,16},{144,24},{168,32},{160,40},{184,48},{176,... | collective-permute-start | bytes 24584 | tf_op jit(solution)/shard_map/ppermute | solution.py:17
  103.9 5.2 %collective-permute-start.14 = (f32[1,16,128]{2,1,0:T(8,128)S(1)}, f32[1,16,128]{2,1,0:T(8,128)S(1)}, u32[]{:S(2)}, u32[]{:S(2)}) collective-permute-start(f32[1,16,128]{2,1,0:T(8,128)S(1)} %add_bitcast_fusion), channel_id=1, source_target_pairs={{16,0},{24,8},{32,16},{40,24},{48,32},{56,40},{64,48},{72,56},{80,... | collective-permute-start | bytes 24584 | tf_op jit(solution)/shard_map/ppermute | solution.py:17
  108.4 3.7 %collective-permute-start.13 = (f32[1,16,128]{2,1,0:T(8,128)S(1)}, f32[1,16,128]{2,1,0:T(8,128)S(1)}, u32[]{:S(2)}, u32[]{:S(2)}) collective-permute-start(f32[1,16,128]{2,1,0:T(8,128)S(1)} %add_bitcast_fusion), channel_id=1, source_target_pairs={{112,0},{120,8},{0,16},{8,24},{16,32},{24,40},{32,48},{40,56},{48,... | collective-permute-start | bytes 24584 | tf_op jit(solution)/shard_map/ppermute | solution.py:17
  109.2 12.3 %collective-permute-start.16 = (f32[2,16,128]{2,1,0:T(8,128)S(1)}, f32[2,16,128]{2,1,0:T(8,128)S(1)}, u32[]{:S(2)}, u32[]{:S(2)}) collective-permute-start(f32[2,16,128]{2,1,0:T(8,128)S(1)} %pad_maximum_fusion.2), channel_id=1, source_target_pairs={{80,0},{88,8},{96,16},{104,24},{112,32},{120,40},{0,48},{8,56},{16... | collective-permute-start | bytes 49160 | tf_op jit(solution)/shard_map/ppermute | solution.py:17
  112.1 9.4 %collective-permute-start.15 = (f32[3,16,128]{2,1,0:T(8,128)S(1)}, f32[3,16,128]{2,1,0:T(8,128)S(1)}, u32[]{:S(2)}, u32[]{:S(2)}) collective-permute-start(f32[3,16,128]{2,1,0:T(8,128)S(1)} %pad_maximum_fusion.1.rows), channel_id=1, source_target_pairs={{48,0},{56,8},{64,16},{72,24},{80,32},{88,40},{96,48},{104,56},{11... | collective-permute-start | bytes 73736 | tf_op jit(solution)/shard_map/ppermute | solution.py:17
  113.7 0.9 copy-start.6

commit v6 on v5

--- a/solution.py
+++ b/solution.py
@@ -9,6 +9,7 @@
 
 
 CHUNK = 512
+CORR_CHUNK = 1024
 WIRE = jnp.bfloat16
 
 
@@ -115,11 +116,10 @@
     )(total, other, data)
 
 
-def fetches(pairs, sems):
-    chunks = pairs[0][1].shape[1] // CHUNK
+def fetches(pairs, sems, chunk):
     copies = []
-    for j in range(chunks):
-        cols = pl.ds(j * CHUNK, CHUNK)
+    for j in range(pairs[0][1].shape[1] // chunk):
+        cols = pl.ds(j * chunk, chunk)
         row = []
         for i, (source, target) in enumerate(pairs):
             copy = pltpu.make_async_copy(source.at[:, cols], target.at[:, cols], sems.at[i, j])
@@ -131,10 +131,10 @@
 
 def corr_kernel(par, scale, lhs_first, lhs_second, own, near_source, out, acc, near, sems):
     even = par[0] == 0
-    for j, copies in enumerate(fetches([(near_source, near)], sems)):
+    for j, copies in enumerate(fetches([(near_source, near)], sems, CORR_CHUNK)):
         for copy in copies:
             copy.wait()
-        cols = pl.ds(j * CHUNK, CHUNK)
+        cols = pl.ds(j * CORR_CHUNK, CORR_CHUNK)
         near_cols = near[:, cols]
         rhs_first = jnp.where(even, own[:, cols], near_cols)
         near_scale = jnp.where(even, scale[:, cols], 1.0)
@@ -169,7 +169,7 @@
         scratch_shapes=[
             pltpu.VMEM((2, both, both), jnp.float32),
             pltpu.VMEM((both, cols), jnp.bfloat16),
-            pltpu.SemaphoreType.DMA((1, cols // CHUNK)),
+            pltpu.SemaphoreType.DMA((1, cols // CORR_CHUNK)),
         ],
         cost_estimate=pl.CostEstimate(flops=4 * both * both * cols, bytes_accessed=8 * both * cols, transcendentals=0),
         compiler_params=pltpu.CompilerParams(vmem_limit_bytes=24 << 20),
@@ -194,11 +194,12 @@
     mat[half:, base : base + half] = -imag
 
 
-def early_kernel(par, mine, mate_resid, own_source, mate_source, near_source, mate_near_source, early, kernel_part, mat, own, second, near, out, sems, out_sems):
-    both = early.shape[0]
+def early_kernel(par, mine, mate_resid, own_source, mate_source, near_source, mate_near_source, early, kernel_part, mat, own, blocks, out, sems, out_sems):
+    both = own.shape[0]
 
     def run(second_source):
-        copies = fetches([(near_source, near), (second_source, second), (own_source, own)], sems)
+        parts = [(near_source, blocks.at[:both]), (second_source, blocks.at[both:]), (own_source, own)]
+        copies = fetches(parts, sems, CHUNK)
         place(mat, 0, assembled(mine, 1, False))
         place(mat, both, assembled(mate_resid, 0, False))
         sends = []
@@ -206,8 +207,7 @@
             for copy in row:
                 copy.wait()
             cols = pl.ds(j * CHUNK, CHUNK)
-            fields = jnp.dot(mat[:, :both], near[:, cols], preferred_element_type=jnp.float32)
-            fields = fields + jnp.dot(mat[:, both:], second[:, cols], preferred_element_type=jnp.float32)
+            fields = jnp.dot(mat[...], blocks[:, cols], preferred_element_type=jnp.float32)
             out[j] = fields
             send = pltpu.make_async_copy(out.at[j], early.at[:, cols], out_sems.at[j])
             send.start()
@@ -225,22 +225,37 @@
         run(mate_source)
 
 
-def late_kernel(inv_norm, par, scale, mine, far_resid, early_source, far_real, far_imag, mate_source, mate_near_source, adjoint, mat, far, second, early, out, sems, out_sems):
+def turn_kernel(par, mine, far_resid, mat):
+    both = mat.shape[0]
+    place(mat, 0, assembled(far_resid, 1, True))
+
+    @pl.when(par[0] == 0)
+    def _():
+        place(mat, both, assembled(mine, 0, True))
+
+    @pl.when(par[0] == 1)
+    def _():
+        place(mat, both, assembled(far_resid, 0, True))
+
+
+def late_kernel(inv_norm, par, scale, mat, early_source, far_real, far_imag, mate_source, mate_near_source, adjoint, blocks, early, out, sems, out_sems):
     both = early.shape[0]
     half = both // 2
 
-    def run(second_source, second_resid):
-        parts = [(far_real, far.at[:half]), (far_imag, far.at[half:]), (second_source, second), (early_source, early)]
-        copies = fetches(parts, sems)
-        place(mat, 0, assembled(far_resid, 1, True))
-        place(mat, both, assembled(second_resid, 0, True))
+    def run(second_source):
+        parts = [
+            (far_real, blocks.at[:half]),
+            (far_imag, blocks.at[half:both]),
+            (second_source, blocks.at[both:]),
+            (early_source, early),
+        ]
+        copies = fetches(parts, sems, CHUNK)
         sends = []
         for j, row in enumerate(copies):
             for copy in row:
                 copy.wait()
             cols = pl.ds(j * CHUNK, CHUNK)
-            fields = early[:, cols] + jnp.dot(mat[:, :both], far[:, cols], preferred_element_type=jnp.float32)
-            fields = fields + jnp.dot(mat[:, both:], second[:, cols], preferred_element_type=jnp.float32)
+            fields = early[:, cols] + jnp.dot(mat[...], blocks[:, cols], preferred_element_type=jnp.float32)
             out[j] = (fields * (inv_norm * scale[:, cols])).reshape(out.shape[1:])
             send = pltpu.make_async_copy(out.at[j], adjoint.at[:, :, cols], out_sems.at[j])
             send.start()
@@ -250,11 +265,11 @@
 
     @pl.when(par[0] == 0)
     def _():
-        run(mate_source, mine)
+        run(mate_source)
 
     @pl.when(par[0] == 1)
     def _():
-        run(mate_near_source, far_resid)
+        run(mate_near_source)
 
 
 def ring_kernel(place_of, rows, above, below, out, slots):
@@ -298,8 +313,9 @@
         in_specs=[pl.BlockSpec(memory_space=pltpu.SMEM)] + [vmem] * 2 + [anywhere] * 4,
         out_specs=(pl.BlockSpec(memory_space=pltpu.HBM), vmem),
         scratch_shapes=[pltpu.VMEM((both, 2 * both), jnp.bfloat16)]
-        + [pltpu.VMEM((both, cols), jnp.bfloat16)] * 3
         + [
+            pltpu.VMEM((both, cols), jnp.bfloat16),
+            pltpu.VMEM((2 * both, cols), jnp.bfloat16),
             pltpu.VMEM((cols // CHUNK, both, CHUNK), jnp.float32),
             pltpu.SemaphoreType.DMA((3, cols // CHUNK)),
             pltpu.SemaphoreType.DMA((cols // CHUNK,)),
@@ -310,7 +326,20 @@
     )(par, mine, mate_resid, own, mate, near, mate_near)
 
 
-def late_fields(par, scale, mine, far_resid, far, early, mate, mate_near, inv_norm):
+def turned(par, mine, far_resid, both):
+    vmem = pl.BlockSpec(memory_space=pltpu.VMEM)
+    return pl.pallas_call(
+        turn_kernel,
+        out_shape=jax.ShapeDtypeStruct((both, 2 * both), jnp.bfloat16),
+        in_specs=[pl.BlockSpec(memory_space=pltpu.SMEM), vmem, vmem],
+        out_specs=vmem,
+        cost_estimate=pl.CostEstimate(flops=0, bytes_accessed=2 << 20, transcendentals=0),
+        compiler_params=pltpu.CompilerParams(vmem_limit_bytes=8 << 20),
+        name="turned",
+    )(par, mine, far_resid)
+
+
+def late_fields(par, scale, mat, far, early, mate, mate_near, inv_norm):
     both, cols = early.shape
     half = both // 2
     vmem = pl.BlockSpec(memory_space=pltpu.VMEM)
@@ -322,21 +351,19 @@
     return pl.pallas_call(
         body,
         out_shape=jax.ShapeDtypeStruct((2, half, cols), jnp.float32),
-        in_specs=[pl.BlockSpec(memory_space=pltpu.SMEM)] + [vmem] * 3 + [hbm] * 5,
+        in_specs=[pl.BlockSpec(memory_space=pltpu.SMEM)] + [vmem] * 2 + [hbm] * 5,
         out_specs=hbm,
         scratch_shapes=[
-            pltpu.VMEM((both, 2 * both), jnp.bfloat16),
-            pltpu.VMEM((both, cols), jnp.bfloat16),
-            pltpu.VMEM((both, cols), jnp.bfloat16),
+            pltpu.VMEM((2 * both, cols), jnp.bfloat16),
             pltpu.VMEM((both, cols), jnp.float32),
             pltpu.VMEM((cols // CHUNK, 2, half, CHUNK), jnp.float32),
             pltpu.SemaphoreType.DMA((4, cols // CHUNK)),
             pltpu.SemaphoreType.DMA((cols // CHUNK,)),
         ],
         cost_estimate=pl.CostEstimate(flops=4 * both * both * cols, bytes_accessed=12 * both * cols, transcendentals=0),
-        compiler_params=pltpu.CompilerParams(vmem_limit_bytes=62 << 20),
+        compiler_params=pltpu.CompilerParams(vmem_limit_bytes=48 << 20),
         name="late",
-    )(par, scale, mine, far_resid, early, *far, mate, mate_near)
+    )(par, scale, mat, early, *far, mate, mate_near)
 
 
 def shards(green, source_weight, observed, amp_weight, pair_used):
@@ -382,7 +409,8 @@
     far_resid = permuted(mine, "cable", far_chip)
     early, kernel_part = early_fields(par, mine, mate_resid, own, mate, near, mate_near)
     kernel = kernel_part[0] * kernel_scale
-    adjoint = late_fields(par, scale, mine, far_resid, far, early, mate, mate_near, inv_norm)
+    mat = turned(par, mine, far_resid, 2 * row_count)
+    adjoint = late_fields(par, scale, mat, far, early, mate, mate_near, inv_norm)
     distance = block_count // 2
     swapped = [permuted(kernel, "cable", lambda i: i ^ d) for d in (1, distance, distance + 1)]
     kernel = (kernel + swapped[0]) + (swapped[1] + swapped[2])

time: 122 us -> 120 us (0.984)
  transfers between devices with their start and end apart: 18 -> 18, of which waited for: 7 -> 7; matrix products, arithmetic and copies ran while one was open for 5% -> 6% of each run, Pallas kernels for 15% -> 14%
where the time goes in v6:
time: 120 us
  waiting for transfers between devices  51.5 us (43%)
  starting transfers between devices  31.7 us (26%)
  Pallas kernels  17.3 us (14%)
  blocking collectives  10.6 us (9%)
  local copies, waits for them, and re-layouts  4.6 us (4%)
  other arithmetic  3.39 us (3%)
    ppermute x17, waiting for transfers between devices, permuted(): lax.ppermute(block, axis, [(source_of(i) % size, i) for i in range(size)])  49.3 us
    ppermute x17, starting transfers between devices, permuted(): lax.ppermute(block, axis, [(source_of(i) % size, i) for i in range(size)])  27.6 us
    all_to_all x1, blocking collectives, shards(): lax.all_to_all(resid, 'grid', 0, 0, tiled=True, axis_index_groups=along_x)  10.6 us
    pallas_call x1, Pallas kernels, late_fields(): pl.pallas_call(body, out_shape=jax.ShapeDtypeStruct((2, half, cols), jnp....  5.7 us
    pallas_call x1, Pallas kernels, early_fields(): pl.pallas_call(early_kernel, out_shape=(pltpu.HBM((both, cols), jnp.float...  5.43 us
    pallas_call x1, Pallas kernels, correlations(): pl.pallas_call(corr_kernel, out_shape=jax.ShapeDtypeStruct((parts, 2, 2,...  4.57 us
    all_to_all x1, starting transfers between devices, shards(): lax.all_to_all(partials, 'grid', 0, 0, tiled=True, axis_index_groups=alon...  4.03 us
    squeeze x1, local copies, waits for them, and re-layouts, shards(): cuts = (green[0], green[1])  3.26 us
  transfers between devices with their start and end apart: 18, of which 7 were waited for; matrix products, arithmetic and copies ran while one was open for 6% of the time, Pallas kernels for 14%

profile of v6, /device:TPU:1, one launch (start us, length us, event | category | flops | bytes accessed | tf_op | source)
XLA Modules:
  0.0 119.9 jit_solution(9286317375006421683)
XLA Ops:
  0.6 3.3 %collective-permute-start.1 = (bf16[512,2048]{1,0:T(8,128)(2,1)}, bf16[512,2048]{1,0:T(8,128)(2,1)}, u32[]{:S(2)}, u32[]{:S(2)}) collective-permute-start(bf16[512,2048]{1,0:T(8,128)(2,1)} %bitcast.17), channel_id=1, source_target_pairs={{8,0},{0,8},{24,16},{16,24},{40,32},{32,40},{56,48},{48,56},{72,64... | collective-permute-start | bytes 6291464 | tf_op jit(solution)/shard_map/ppermute | solution.py:18
  3.9 0.0 collective-permute-start
  3.9 0.7 broadcast_select_fusion
  4.6 3.3 %slice_bitcast_fusion = (bf16[256,2048]{1,0:T(8,128)(2,1)}, bf16[256,2048]{1,0:T(8,128)(2,1)}) fusion(bf16[2,256,2048]{2,1,0:T(8,128)(2,1)} %param.5), kind=kLoop, calls=%fused_computation.2 | loop fusion | bytes 4194304 | tf_op jit(solution)/shard_map/squeeze | solution.py:395
  7.9 0.6 multiply_convert_fusion.lhs_second
  8.5 0.0 collective-permute-done.1.mate_source.refs_6_
  8.5 0.1 copy-done.3
  8.6 2.0 %multiply_convert_fusion.1.lhs_first = bf16[512,2048]{1,0:T(8,128)(2,1)S(1)} fusion(bf16[512,2048]{1,0:T(8,128)(2,1)} %collective-permute-done.1.mate_source.refs_6_, f32[2048]{0:T(1024)S(1)} %copy-done.3), kind=kLoop, calls=%fused_computation.1 | loop fusion | flops 3145728 | bytes 4202496 | tf_op jit(solution)/shard_map/convert_element_type | solution.py:393
  10.6 21.9 %collective-permute-done.near_source = bf16[512,2048]{1,0:T(8,128)(2,1)} collective-permute-done((bf16[512,2048]{1,0:T(8,128)(2,1)}, bf16[512,2048]{1,0:T(8,128)(2,1)}, u32[]{:S(2)}, u32[]{:S(2)}) %collective-permute-start) | collective-permute-done | bytes 2097184 | tf_op jit(solution)/shard_map/ppermute | solution.py:18
  32.5 0.5 collective-permute-start.7
  33.0 4.6 %corr.1 = bf16[4,2,2,64,256]{4,3,2,1,0:T(8,128)(2,1)} custom-call(s32[1]{0:T(128)} %bitcast.par.refs_0_, f32[1,2048]{1,0:T(1,128)S(1)} %bitcast.21, bf16[512,2048]{1,0:T(8,128)(2,1)S(1)} %multiply_convert_fusion.1.lhs_first, bf16[512,2048]{1,0:T(8,128)(2,1)S(1)} %multiply_convert_fusion.lhs_second, bf16[512,2048]{1,0:T(8,128)(2,1)S(1)} %bitcast.19, ...), custom_call_target="tpu_custom_call" | custom-call | flops 2147483648 | bytes 8388608 | tf_op jit(solution)/shard_map/corr/pallas_call | solution.py:164
  37.6 4.0 %all-to-all-start = ((bf16[4,2,2,64,256]{4,3,2,1,0:T(8,128)(2,1)}), bf16[4,2,2,64,256]{4,3,2,1,0:T(8,128)(2,1)S(1)}, u32[]{:S(2)}, u32[]{:S(2)}) async-start(bf16[4,2,2,64,256]{4,3,2,1,0:T(8,128)(2,1)} %corr.1), calls=%async_computation | async-start | bytes 1048576 | tf_op jit(solution)/shard_map/all_to_all | solution.py:403
  41.7 1.2 %copy-done.1 = f32[2,2,256,256]{3,2,1,0:T(8,128)S(1)} copy-done((f32[2,2,256,256]{3,2,1,0:T(8,128)S(1)}, f32[2,2,256,256]{3,2,1,0:T(8,128)}, u32[]{:S(2)}) %copy-start.1) | copy-done | bytes 1048600
  42.9 0.6 prep.1
  43.5 0.1 collective-permute-start.4
  43.6 5.1 %collective-permute-start.3 = (f32[3,64,256]{2,1,0:T(8,128)S(1)}, f32[3,64,256]{2,1,0:T(8,128)S(1)}, u32[]{:S(2)}, u32[]{:S(2)}) collective-permute-start(f32[3,64,256]{2,1,0:T(8,128)S(1)} %get-tuple-element.18), channel_id=1, source_target_pairs={{8,0},{0,8},{24,16},{16,24},{40,32},{32,40},{56,48},{48,56},{72,64... | collective-permute-start | bytes 589832 | tf_op jit(solution)/shard_map/ppermute | solution.py:18
  48.7 2.3 %all-to-all-done.pieces = bf16[4,2,2,64,256]{4,3,2,1,0:T(8,128)(2,1)S(1)} async-done(((bf16[4,2,2,64,256]{4,3,2,1,0:T(8,128)(2,1)}), bf16[4,2,2,64,256]{4,3,2,1,0:T(8,128)(2,1)S(1)}, u32[]{:S(2)}, u32[]{:S(2)}) %all-to-all-start) | async-done | bytes 524320 | tf_op jit(solution)/shard_map/all_to_all | solution.py:403
  50.9 0.1 summed.1
  51.0 2.7 %collective-permute-start.2 = (bf16[2,2,64,256]{3,2,1,0:T(8,128)(2,1)S(1)}, bf16[2,2,64,256]{3,2,1,0:T(8,128)(2,1)S(1)}, u32[]{:S(2)}, u32[]{:S(2)}) collective-permute-start(bf16[2,2,64,256]{3,2,1,0:T(8,128)(2,1)S(1)} %get-tuple-element.17), channel_id=1, source_target_pairs={{1,0},{0,1},{3,2},{2,3},{5,4},{4,5},{7,6},{6,7},{9,8},{8,9},{11,10... | collective-permute-start | bytes 393224 | tf_op jit(solution)/shard_map/ppermute | solution.py:18
  53.7 0.0 collective-permute-done.4
  53.8 0.0 collective-permute-done.3
  53.8 2.6 %collective-permute-done.2.refs_1_ = bf16[2,2,64,256]{3,2,1,0:T(8,128)(2,1)S(1)} collective-permute-done((bf16[2,2,64,256]{3,2,1,0:T(8,128)(2,1)S(1)}, bf16[2,2,64,256]{3,2,1,0:T(8,128)(2,1)S(1)}, u32[]{:S(2)}, u32[]{:S(2)}) %collective-permute-start.2) | collective-permute-done | bytes 131104 | tf_op jit(solution)/shard_map/ppermute | solution.py:18
  56.4 0.1 resid.1
  56.5 10.6 %all_to_all.10.mine = bf16[4,2,2,64,256]{4,3,2,1,0:T(8,128)(2,1)S(1)} all-to-all(bf16[4,2,2,64,256]{4,3,2,1,0:T(8,128)(2,1)S(1)} %resid.1), channel_id=1, replica_groups={{0,2,4,6},{1,3,5,7},{8,10,12,14},{9,11,13,15},{16,18,20,22},{17,19,21,2..., dimensions={0} | all-to-all | bytes 1048576 | tf_op jit(solution)/shard_map/all_to_all | solution.py:407
  67.1 2.8 %collective-permute-start.6 = (bf16[4,1,2,64,256]{4,3,2,1,0:T(8,128)(2,1)S(1)}, bf16[4,1,2,64,256]{4,3,2,1,0:T(8,128)(2,1)S(1)}, u32[]{:S(2)}, u32[]{:S(2)}) collective-permute-start(bf16[4,1,2,64,256]{4,3,2,1,0:T(8,128)(2,1)S(1)} %slice.14), channel_id=1, source_target_pairs={{8,0},{0,8},{24,16},{16,24},{40,32},{32,40},{56,48},{48,56},{72,64... | collective-permute-start | bytes 786440 | tf_op jit(solution)/shard_map/ppermute | solution.py:18
  69.9 3.8 %collective-permute-start.8 = (bf16[256,2048]{1,0:T(8,128)(2,1)}, bf16[256,2048]{1,0:T(8,128)(2,1)}, u32[]{:S(2)}, u32[]{:S(2)}) collective-permute-start(bf16[256,2048]{1,0:T(8,128)(2,1)} %get-tuple-element.21), channel_id=1, source_target_pairs={{240,0},{24,8},{0,16},{40,24},{16,32},{56,40},{32,48},{72,56},{48,... | collective-permute-start | bytes 3145736 | tf_op jit(solution)/shard_map/ppermute | solution.py:18
  73.7 0.0 collective-permute-start.9
  73.8 0.0 collective-permute-start.5
  73.8 0.0 collective-permute-done.6.mate_resid
  73.8 0.0 collective-permute-done.7.mate_near_source.refs_7_
  73.8 5.4 %early.1 = (f32[512,2048]{1,0:T(8,128)}, f32[1,2048]{1,0:T(1,128)S(1)}) custom-call(s32[1]{0:T(128)} %bitcast.par.refs_0_, bf16[4,2,2,64,256]{4,3,2,1,0:T(8,128)(2,1)S(1)} %all_to_all.10.mine, bf16[4,1,2,64,256]{4,3,2,1,0:T(8,128)(2,1)S(1)} %collective-permute-done.6.mate_resid, bf16[512,2048]{1,0:T(8,128)(2,1)S(1)} %bitcast.20, ...), custom_call_target="tpu_custom_call" | custom-call | flops 2147483648 | bytes 10485760 | tf_op jit(solution)/shard_map/early/pallas_call | solution.py:307
  79.2 0.1 collective-permute-start.10
  79.3 2.4 %collective-permute-start.11 = (f32[2048]{0:T(1024)S(1)}, f32[2048]{0:T(1024)S(1)}, u32[]{:S(2)}, u32[]{:S(2)}) collective-permute-start(f32[2048]{0:T(1024)S(1)} %bitcast.25), channel_id=1, source_target_pairs={{128,0},{136,8},{144,16},{152,24},{160,32},{168,40},{176,48},{184,... | collective-permute-start | bytes 24584 | tf_op jit(solution)/shard_map/ppermute | solution.py:18
  81.7 0.0 collective-permute-done.10
  81.7 1.1 collective-permute-start.12
  82.9 20.8 %collective-permute-done.11 = f32[2048]{0:T(1024)S(1)} collective-permute-done((f32[2048]{0:T(1024)S(1)}, f32[2048]{0:T(1024)S(1)}, u32[]{:S(2)}, u32[]{:S(2)}) %collective-permute-start.11) | collective-permute-done | bytes 8224 | tf_op jit(solution)/shard_map/ppermute | solution.py:18
  103.7 0.2 collective-permute-done.12
  103.9 4.4 %collective-permute-start.14 = (f32[1,16,128]{2,1,0:T(8,128)S(1)}, f32[1,16,128]{2,1,0:T(8,128)S(1)}, u32[]{:S(2)}, u32[]{:S(2)}) collective-permute-start(f32[1,16,128]{2,1,0:T(8,128)S(1)} %add_bitcast_fusion), channel_id=1, source_target_pairs={{16,0},{24,8},{32,16},{40,24},{48,32},{56,40},{64,48},{72,56},{80,... | collective-permute-start | bytes 24584 | tf_op jit(solution)/shard_map/ppermute | solution.py:18
  108.3 0.0 collective-permute-done.5.far_resid
  108.3 0.3 turned.1.refs_2_
  108.6 0.1 collective-permute-start.13
  108.7 0.4 collective-permute-done.14
  109.1 0.0 collective-permute-start.16
  109.1 3.3 %collective-permute-done.13 = f32[1,16,128]{2,1,0:T(8,128)S(1)} collective-permute-done((f32[1,16,128]{2,1,0:T(8,128)S(1)}, f32[1,16,128]{2,1,0:T(8,128)S(1)}, u32[]{:S(2)}, u32[]{:S(2)}) %collective-permute-start.13) | collective-permute-done | bytes 8224 | tf_op jit(solution)/shard_map/ppermute | solution.py:18
  112.4 1.2 collective-permute-start.15
  113.6 5.7 %late.1 = f32[2,256,2048]{2,1,0:T(8,128)} custom-call(s32[1]{0:T(128)} %bitcast.par.refs_0_, f32[1,2048]{1,0:T(1,128)S(1)} %bitcast.22, bf16[512,1024]{1,0:T(8,128)(2,1)S(1)} %turned.1.refs_2_, f32[512,2048]{1,0:T(8,128)} %get-tuple-element.20.refs_3_, bf16[256,2048]{1,0:T(8,128)(2,1)} %collective-permute-done.8.refs_4_, ...), custom_call_target="tpu_custom_call" | custom-call | flops 2147483648 | bytes 12582912 | tf_op jit(solution)/shard_map/late/pallas_call | solution.py:351
  119.3 0.0 collective-permute-done.15.above
  119.3 0.6 ring_sum.1
  (18 shorter events, 0.1 us)
Async XLA Ops:
  0.6 7.9 %collective-permute-start.1 = (bf16[512,2048]{1,0:T(8,128)(2,1)}, bf16[512,2048]{1,0:T(8,128)(2,1)}, u32[]{:S(2)}, u32[]{:S(2)}) collective-permute-start(bf16[512,2048]{1,0:T(8,128)(2,1)} %bitcast.17), channel_id=1, source_target_pairs={{8,0},{0,8},{24,16},{16,24},{40,32},{32,40},{56,48},{48,56},{72,64... | collective-permute-start | bytes 6291464 | tf_op jit(solution)/shard_map/ppermute | solution.py:18
  3.9 28.6 %collective-permute-start = (bf16[512,2048]{1,0:T(8,128)(2,1)}, bf16[512,2048]{1,0:T(8,128)(2,1)}, u32[]{:S(2)}, u32[]{:S(2)}) collective-permute-start(bf16[512,2048]{1,0:T(8,128)(2,1)} %bitcast.18), channel_id=1, source_target_pairs={{16,0},{248,8},{32,16},{8,24},{48,32},{24,40},{64,48},{40,56},{80,... | collective-permute-start | bytes 6291464 | tf_op jit(solution)/shard_map/ppermute | solution.py:18
  4.6 3.3 %copy-start = (bf16[2,256,2048]{2,1,0:T(8,128)(2,1)S(1)}, bf16[2,256,2048]{2,1,0:T(8,128)(2,1)}, u32[]{:S(2)}) copy-start(bf16[2,256,2048]{2,1,0:T(8,128)(2,1)} %param.5) | copy-start | bytes 6291460
  7.9 0.7 copy-start.3
  32.5 41.2 %collective-permute-start.7 = (bf16[512,2048]{1,0:T(8,128)(2,1)}, bf16[512,2048]{1,0:T(8,128)(2,1)}, u32[]{:S(2)}, u32[]{:S(2)}) collective-permute-start(bf16[512,2048]{1,0:T(8,128)(2,1)} %collective-permute-done.near_source), channel_id=1, source_target_pairs={{8,0},{0,8},{24,16},{16,24},{40,32},{32,40},{56,48},{48,56},{72,64... | collective-permute-start | bytes 6291464 | tf_op jit(solution)/shard_map/ppermute | solution.py:18
  33.0 8.6 %copy-start.2 = (f32[2,256,256]{2,1,0:T(8,128)S(1)}, f32[2,256,256]{2,1,0:T(8,128)}, u32[]{:S(2)}) copy-start(f32[2,256,256]{2,1,0:T(8,128)} %amp_weight.1) | copy-start | bytes 1572868
  33.0 8.6 %copy-start.4 = (s32[1,2]{1,0:T(1,128)S(1)}, s32[1,2]{1,0:T(1,128)}, u32[]{:S(2)}) copy-start(s32[1,2]{1,0:T(1,128)} %used.1) | copy-start | bytes 28
  37.6 13.3 %all-to-all-start = ((bf16[4,2,2,64,256]{4,3,2,1,0:T(8,128)(2,1)}), bf16[4,2,2,64,256]{4,3,2,1,0:T(8,128)(2,1)S(1)}, u32[]{:S(2)}, u32[]{:S(2)}) async-start(bf16[4,2,2,64,256]{4,3,2,1,0:T(8,128)(2,1)} %corr.1), calls=%async_computation | async-start | bytes 1048576 | tf_op jit(solution)/shard_map/all_to_all | solution.py:403
  41.7 1.2 %copy-start.1 = (f32[2,2,256,256]{3,2,1,0:T(8,128)S(1)}, f32[2,2,256,256]{3,2,1,0:T(8,128)}, u32[]{:S(2)}) copy-start(f32[2,2,256,256]{3,2,1,0:T(8,128)} %observed.1) | copy-start | bytes 3145732
  43.5 10.3 %collective-permute-start.4 = (f32[3,64,256]{2,1,0:T(8,128)S(1)}, f32[3,64,256]{2,1,0:T(8,128)S(1)}, u32[]{:S(2)}, u32[]{:S(2)}) collective-permute-start(f32[3,64,256]{2,1,0:T(8,128)S(1)} %get-tuple-element.19), channel_id=1, source_target_pairs={{16,0},{248,8},{32,16},{8,24},{48,32},{24,40},{64,48},{40,56},{80,... | collective-permute-start | bytes 589832 | tf_op jit(solution)/shard_map/ppermute | solution.py:18
  43.6 10.2 %collective-permute-start.3 = (f32[3,64,256]{2,1,0:T(8,128)S(1)}, f32[3,64,256]{2,1,0:T(8,128)S(1)}, u32[]{:S(2)}, u32[]{:S(2)}) collective-permute-start(f32[3,64,256]{2,1,0:T(8,128)S(1)} %get-tuple-element.18), channel_id=1, source_target_pairs={{8,0},{0,8},{24,16},{16,24},{40,32},{32,40},{56,48},{48,56},{72,64... | collective-permute-start | bytes 589832 | tf_op jit(solution)/shard_map/ppermute | solution.py:18
  51.0 5.4 %collective-permute-start.2 = (bf16[2,2,64,256]{3,2,1,0:T(8,128)(2,1)S(1)}, bf16[2,2,64,256]{3,2,1,0:T(8,128)(2,1)S(1)}, u32[]{:S(2)}, u32[]{:S(2)}) collective-permute-start(bf16[2,2,64,256]{3,2,1,0:T(8,128)(2,1)S(1)} %get-tuple-element.17), channel_id=1, source_target_pairs={{1,0},{0,1},{3,2},{2,3},{5,4},{4,5},{7,6},{6,7},{9,8},{8,9},{11,10... | collective-permute-start | bytes 393224 | tf_op jit(solution)/shard_map/ppermute | solution.py:18
  67.1 6.6 %collective-permute-start.6 = (bf16[4,1,2,64,256]{4,3,2,1,0:T(8,128)(2,1)S(1)}, bf16[4,1,2,64,256]{4,3,2,1,0:T(8,128)(2,1)S(1)}, u32[]{:S(2)}, u32[]{:S(2)}) collective-permute-start(bf16[4,1,2,64,256]{4,3,2,1,0:T(8,128)(2,1)S(1)} %slice.14), channel_id=1, source_target_pairs={{8,0},{0,8},{24,16},{16,24},{40,32},{32,40},{56,48},{48,56},{72,64... | collective-permute-start | bytes 786440 | tf_op jit(solution)/shard_map/ppermute | solution.py:18
  69.9 43.7 %collective-permute-start.8 = (bf16[256,2048]{1,0:T(8,128)(2,1)}, bf16[256,2048]{1,0:T(8,128)(2,1)}, u32[]{:S(2)}, u32[]{:S(2)}) collective-permute-start(bf16[256,2048]{1,0:T(8,128)(2,1)} %get-tuple-element.21), channel_id=1, source_target_pairs={{240,0},{24,8},{0,16},{40,24},{16,32},{56,40},{32,48},{72,56},{48,... | collective-permute-start | bytes 3145736 | tf_op jit(solution)/shard_map/ppermute | solution.py:18
  73.7 39.8 %collective-permute-start.9 = (bf16[256,2048]{1,0:T(8,128)(2,1)}, bf16[256,2048]{1,0:T(8,128)(2,1)}, u32[]{:S(2)}, u32[]{:S(2)}) collective-permute-start(bf16[256,2048]{1,0:T(8,128)(2,1)} %get-tuple-element.22), channel_id=1, source_target_pairs={{240,0},{24,8},{0,16},{40,24},{16,32},{56,40},{32,48},{72,56},{48,... | collective-permute-start | bytes 3145736 | tf_op jit(solution)/shard_map/ppermute | solution.py:18
  73.8 34.5 %collective-permute-start.5 = (bf16[4,2,2,64,256]{4,3,2,1,0:T(8,128)(2,1)S(1)}, bf16[4,2,2,64,256]{4,3,2,1,0:T(8,128)(2,1)S(1)}, u32[]{:S(2)}, u32[]{:S(2)}) collective-permute-start(bf16[4,2,2,64,256]{4,3,2,1,0:T(8,128)(2,1)S(1)} %all_to_all.10.mine), channel_id=1, source_target_pairs={{240,0},{24,8},{0,16},{40,24},{16,32},{56,40},{32,48},{72,56},{48,... | collective-permute-start | bytes 1572872 | tf_op jit(solution)/shard_map/ppermute | solution.py:18
  79.2 2.5 %collective-permute-start.10 = (f32[2048]{0:T(1024)S(1)}, f32[2048]{0:T(1024)S(1)}, u32[]{:S(2)}, u32[]{:S(2)}) collective-permute-start(f32[2048]{0:T(1024)S(1)} %bitcast.24), channel_id=1, source_target_pairs={{8,0},{0,8},{24,16},{16,24},{40,32},{32,40},{56,48},{48,56},{72,64... | collective-permute-start | bytes 24584 | tf_op jit(solution)/shard_map/ppermute | solution.py:18
  79.3 24.4 %collective-permute-start.11 = (f32[2048]{0:T(1024)S(1)}, f32[2048]{0:T(1024)S(1)}, u32[]{:S(2)}, u32[]{:S(2)}) collective-permute-start(f32[2048]{0:T(1024)S(1)} %bitcast.25), channel_id=1, source_target_pairs={{128,0},{136,8},{144,16},{152,24},{160,32},{168,40},{176,48},{184,... | collective-permute-start | bytes 24584 | tf_op jit(solution)/shard_map/ppermute | solution.py:18
  81.7 22.1 %collective-permute-start.12 = (f32[2048]{0:T(1024)S(1)}, f32[2048]{0:T(1024)S(1)}, u32[]{:S(2)}, u32[]{:S(2)}) collective-permute-start(f32[2048]{0:T(1024)S(1)} %bitcast.26), channel_id=1, source_target_pairs={{136,0},{128,8},{152,16},{144,24},{168,32},{160,40},{184,48},{176,... | collective-permute-start | bytes 24584 | tf_op jit(solution)/shard_map/ppermute | solution.py:18
  103.9 5.2 %collective-permute-start.14 = (f32[1,16,128]{2,1,0:T(8,128)S(1)}, f32[1,16,128]{2,1,0:T(8,128)S(1)}, u32[]{:S(2)}, u32[]{:S(2)}) collective-permute-start(f32[1,16,128]{2,1,0:T(8,128)S(1)} %add_bitcast_fusion), channel_id=1, source_target_pairs={{16,0},{24,8},{32,16},{40,24},{48,32},{56,40},{64,48},{72,56},{80,... | collective-permute-start | bytes 24584 | tf_op jit(solution)/shard_map/ppermute | solution.py:18
  108.6 3.8 %collective-permute-start.13 = (f32[1,16,128]{2,1,0:T(8,128)S(1)}, f32[1,16,128]{2,1,0:T(8,128)S(1)}, u32[]{:S(2)}, u32[]{:S(2)}) collective-permute-start(f32[1,16,128]{2,1,0:T(8,128)S(1)} %add_bitcast_fusion), channel_id=1, source_target_pairs={{112,0},{120,8},{0,16},{8,24},{16,32},{24,40},{32,48},{40,56},{48,... | collective-permute-start | bytes 24584 | tf_op jit(solution)/shard_map/ppermute | solution.py:18
  109.1 10.2 %collective-permute-start.16 = (f32[2,16,128]{2,1,0:T(8,128)S(1)}, f32[2,16,128]{2,1,0:T(8,128)S(1)}, u32[]{:S(2)}, u32[]{:S(2)}) collective-permute-start(f32[2,16,128]{2,1,0:T(8,128)S(1)} %pad_maximum_fusion.2), channel_id=1, source_target_pairs={{80,0},{88,8},{96,16},{104,24},{112,32},{120,40},{0,48},{8,56},{16... | collective-permute-start | bytes 49160 | tf_op jit(solution)/shard_map/ppermute | solution.py:18
  112.4 6.9 %collective-permute-start.15 = (f32[3,16,128]{2,1,0:T(8,128)S(1)}, f32[3,16,128]{2,1,0:T(8,128)S(1)}, u32[]{:S(2)}, u32[]{:S(2)}) collective-permute-start(f32[3,16,128]{2,1,0:T(8,128)S(1)} %pad_maximum_fusion.1.rows), channel_id=1, source_target_pairs={{48,0},{56,8},{64,16},{72,24},{80,32},{88,40},{96,48},{104,56},{11... | collective-permute-start | bytes 73736 | tf_op jit(solution)/shard_map/ppermute | solution.py:18

commit v7 on v6

--- a/solution.py
+++ b/solution.py
@@ -116,13 +116,14 @@
     )(total, other, data)
 
 
-def fetches(pairs, sems, chunk):
+def fetches(pairs, sems, chunk, begin=0):
     copies = []
     for j in range(pairs[0][1].shape[1] // chunk):
-        cols = pl.ds(j * chunk, chunk)
         row = []
         for i, (source, target) in enumerate(pairs):
-            copy = pltpu.make_async_copy(source.at[:, cols], target.at[:, cols], sems.at[i, j])
+            copy = pltpu.make_async_copy(
+                source.at[:, pl.ds(begin + j * chunk, chunk)], target.at[:, pl.ds(j * chunk, chunk)], sems.at[i, j]
+            )
             copy.start()
             row.append(copy)
         copies.append(row)
@@ -238,7 +239,8 @@
         place(mat, both, assembled(far_resid, 0, True))
 
 
-def late_kernel(inv_norm, par, scale, mat, early_source, far_real, far_imag, mate_source, mate_near_source, adjoint, blocks, early, out, sems, out_sems):
+def late_kernel(inv_norm, begin, par, scale, mat_source, early_source, far_real, far_imag, mate_source, mate_near_source, *refs):
+    adjoint, mat, blocks, early, out, mat_sem, sems, out_sems = refs[-8:]
     both = early.shape[0]
     half = both // 2
 
@@ -249,15 +251,19 @@
             (second_source, blocks.at[both:]),
             (early_source, early),
         ]
-        copies = fetches(parts, sems, CHUNK)
+        mat_copy = pltpu.make_async_copy(mat_source, mat, mat_sem)
+        mat_copy.start()
+        copies = fetches(parts, sems, CHUNK, begin)
+        mat_copy.wait()
         sends = []
         for j, row in enumerate(copies):
             for copy in row:
                 copy.wait()
             cols = pl.ds(j * CHUNK, CHUNK)
+            target = pl.ds(begin + j * CHUNK, CHUNK)
             fields = early[:, cols] + jnp.dot(mat[...], blocks[:, cols], preferred_element_type=jnp.float32)
-            out[j] = (fields * (inv_norm * scale[:, cols])).reshape(out.shape[1:])
-            send = pltpu.make_async_copy(out.at[j], adjoint.at[:, :, cols], out_sems.at[j])
+            out[j] = (fields * (inv_norm * scale[:, target])).reshape(out.shape[1:])
+            send = pltpu.make_async_copy(out.at[j], adjoint.at[:, :, target], out_sems.at[j])
             send.start()
             sends.append(send)
         for send in sends:
@@ -330,40 +336,46 @@
     vmem = pl.BlockSpec(memory_space=pltpu.VMEM)
     return pl.pallas_call(
         turn_kernel,
-        out_shape=jax.ShapeDtypeStruct((both, 2 * both), jnp.bfloat16),
+        out_shape=pltpu.HBM((both, 2 * both), jnp.bfloat16),
         in_specs=[pl.BlockSpec(memory_space=pltpu.SMEM), vmem, vmem],
-        out_specs=vmem,
+        out_specs=pl.BlockSpec((both, 2 * both), lambda: (0, 0)),
         cost_estimate=pl.CostEstimate(flops=0, bytes_accessed=2 << 20, transcendentals=0),
         compiler_params=pltpu.CompilerParams(vmem_limit_bytes=8 << 20),
         name="turned",
     )(par, mine, far_resid)
 
 
-def late_fields(par, scale, mat, far, early, mate, mate_near, inv_norm):
+def late_fields(par, scale, mat, far, early, mate, mate_near, inv_norm, begin, count, partial=None):
     both, cols = early.shape
     half = both // 2
     vmem = pl.BlockSpec(memory_space=pltpu.VMEM)
     hbm = pl.BlockSpec(memory_space=pltpu.HBM)
+    before = () if partial is None else (partial,)
 
     def body(*refs):
-        late_kernel(inv_norm, *refs)
+        late_kernel(inv_norm, begin, *refs)
 
     return pl.pallas_call(
         body,
         out_shape=jax.ShapeDtypeStruct((2, half, cols), jnp.float32),
-        in_specs=[pl.BlockSpec(memory_space=pltpu.SMEM)] + [vmem] * 2 + [hbm] * 5,
+        in_specs=[pl.BlockSpec(memory_space=pltpu.SMEM), vmem] + [hbm] * (6 + len(before)),
         out_specs=hbm,
         scratch_shapes=[
-            pltpu.VMEM((2 * both, cols), jnp.bfloat16),
-            pltpu.VMEM((both, cols), jnp.float32),
-            pltpu.VMEM((cols // CHUNK, 2, half, CHUNK), jnp.float32),
-            pltpu.SemaphoreType.DMA((4, cols // CHUNK)),
-            pltpu.SemaphoreType.DMA((cols // CHUNK,)),
+            pltpu.VMEM((both, 2 * both), jnp.bfloat16),
+            pltpu.VMEM((2 * both, count), jnp.bfloat16),
+            pltpu.VMEM((both, count), jnp.float32),
+            pltpu.VMEM((count // CHUNK, 2, half, CHUNK), jnp.float32),
+            pltpu.SemaphoreType.DMA,
+            pltpu.SemaphoreType.DMA((4, count // CHUNK)),
+            pltpu.SemaphoreType.DMA((count // CHUNK,)),
         ],
-        cost_estimate=pl.CostEstimate(flops=4 * both * both * cols, bytes_accessed=12 * both * cols, transcendentals=0),
-        compiler_params=pltpu.CompilerParams(vmem_limit_bytes=48 << 20),
+        input_output_aliases={8: 0} if before else {},
+        cost_estimate=pl.CostEstimate(
+            flops=4 * both * both * count, bytes_accessed=12 * both * count, transcendentals=0
+        ),
+        compiler_params=pltpu.CompilerParams(vmem_limit_bytes=62 << 20),
         name="late",
-    )(par, scale, mat, early, *far, mate, mate_near)
+    )(par, scale, mat, early, *far, mate, mate_near, *before)
 
 
 def shards(green, source_weight, observed, amp_weight, pair_used):
@@ -410,7 +422,12 @@
     early, kernel_part = early_fields(par, mine, mate_resid, own, mate, near, mate_near)
     kernel = kernel_part[0] * kernel_scale
     mat = turned(par, mine, far_resid, 2 * row_count)
-    adjoint = late_fields(par, scale, mat, far, early, mate, mate_near, inv_norm)
+    adjoint = None
+    for part in range(2):
+        count = col_count // 2
+        adjoint = late_fields(
+            par, scale, mat, far, early, mate, mate_near, inv_norm, part * count, count, adjoint
+        )
     distance = block_count // 2
     swapped = [permuted(kernel, "cable", lambda i: i ^ d) for d in (1, distance, distance + 1)]
     kernel = (kernel + swapped[0]) + (swapped[1] + swapped[2])

time: 120 us -> 126 us (1.050)
  Pallas kernels: 17.3 us -> 23.5 us
    pallas_call x1 -> x2, Pallas kernels: 5.7 us -> 10.8 us  [late_fields(): pl.pallas_call(body, out_shape=jax.ShapeDtypeStruct((2, half, cols), jnp....]
  transfers between devices with their start and end apart: 18 -> 18, of which waited for: 7 -> 5; matrix products, arithmetic and copies ran while one was open for 6% -> 5% of each run, Pallas kernels for 14% -> 18%
where the time goes in v7:
time: 126 us; the launch traced here: 125 us
  waiting for transfers between devices  51.3 us (41%)
  starting transfers between devices  31.2 us (25%)
  Pallas kernels  23.5 us (19%)
  blocking collectives  10.6 us (8%)
  local copies, waits for them, and re-layouts  4.6 us (4%)
  other arithmetic  3.39 us (3%)
    ppermute x17, waiting for transfers between devices, permuted(): lax.ppermute(block, axis, [(source_of(i) % size, i) for i in range(size)])  49 us
    ppermute x17, starting transfers between devices, permuted(): lax.ppermute(block, axis, [(source_of(i) % size, i) for i in range(size)])  27.2 us
    pallas_call x2, Pallas kernels, late_fields(): pl.pallas_call(body, out_shape=jax.ShapeDtypeStruct((2, half, cols), jnp....  10.8 us
    all_to_all x1, blocking collectives, shards(): lax.all_to_all(resid, 'grid', 0, 0, tiled=True, axis_index_groups=along_x)  10.6 us
    pallas_call x1, Pallas kernels, early_fields(): pl.pallas_call(early_kernel, out_shape=(pltpu.HBM((both, cols), jnp.float...  5.43 us
    pallas_call x1, Pallas kernels, correlations(): pl.pallas_call(corr_kernel, out_shape=jax.ShapeDtypeStruct((parts, 2, 2,...  4.57 us
    all_to_all x1, starting transfers between devices, shards(): lax.all_to_all(partials, 'grid', 0, 0, tiled=True, axis_index_groups=alon...  4.03 us
    squeeze x1, local copies, waits for them, and re-layouts, shards(): cuts = (green[0], green[1])  3.26 us
  transfers between devices with their start and end apart: 18, of which 5 were waited for; matrix products, arithmetic and copies ran while one was open for 5% of the time, Pallas kernels for 18%

profile of v7, /device:TPU:1, one launch (start us, length us, event | category | flops | bytes accessed | tf_op | source)
XLA Modules:
  0.0 125.4 jit_solution(8766335588841591414)
XLA Ops:
  0.6 3.3 %collective-permute-start.1 = (bf16[512,2048]{1,0:T(8,128)(2,1)}, bf16[512,2048]{1,0:T(8,128)(2,1)}, u32[]{:S(2)}, u32[]{:S(2)}) collective-permute-start(bf16[512,2048]{1,0:T(8,128)(2,1)} %bitcast.17), channel_id=1, source_target_pairs={{8,0},{0,8},{24,16},{16,24},{40,32},{32,40},{56,48},{48,56},{72,64... | collective-permute-start | bytes 6291464 | tf_op jit(solution)/shard_map/ppermute | solution.py:18
  3.9 0.0 collective-permute-start
  3.9 0.7 broadcast_select_fusion
  4.6 3.3 %slice_bitcast_fusion = (bf16[256,2048]{1,0:T(8,128)(2,1)}, bf16[256,2048]{1,0:T(8,128)(2,1)}) fusion(bf16[2,256,2048]{2,1,0:T(8,128)(2,1)} %param.5), kind=kLoop, calls=%fused_computation.2 | loop fusion | bytes 4194304 | tf_op jit(solution)/shard_map/squeeze | solution.py:407
  7.9 0.6 multiply_convert_fusion.lhs_second
  8.5 0.0 collective-permute-done.1.mate_source.refs_6_
  8.5 0.1 copy-done.3
  8.6 2.0 %multiply_convert_fusion.1.lhs_first = bf16[512,2048]{1,0:T(8,128)(2,1)S(1)} fusion(bf16[512,2048]{1,0:T(8,128)(2,1)} %collective-permute-done.1.mate_source.refs_6_, f32[2048]{0:T(1024)S(1)} %copy-done.3), kind=kLoop, calls=%fused_computation.1 | loop fusion | flops 3145728 | bytes 4202496 | tf_op jit(solution)/shard_map/convert_element_type | solution.py:405
  10.6 21.9 %collective-permute-done.near_source = bf16[512,2048]{1,0:T(8,128)(2,1)} collective-permute-done((bf16[512,2048]{1,0:T(8,128)(2,1)}, bf16[512,2048]{1,0:T(8,128)(2,1)}, u32[]{:S(2)}, u32[]{:S(2)}) %collective-permute-start) | collective-permute-done | bytes 2097184 | tf_op jit(solution)/shard_map/ppermute | solution.py:18
  32.5 0.5 collective-permute-start.7
  33.0 4.6 %corr.1 = bf16[4,2,2,64,256]{4,3,2,1,0:T(8,128)(2,1)} custom-call(s32[1]{0:T(128)} %bitcast.par.refs_0_, f32[1,2048]{1,0:T(1,128)S(1)} %bitcast.23, bf16[512,2048]{1,0:T(8,128)(2,1)S(1)} %multiply_convert_fusion.1.lhs_first, bf16[512,2048]{1,0:T(8,128)(2,1)S(1)} %multiply_convert_fusion.lhs_second, bf16[512,2048]{1,0:T(8,128)(2,1)S(1)} %bitcast.19, ...), custom_call_target="tpu_custom_call" | custom-call | flops 2147483648 | bytes 8388608 | tf_op jit(solution)/shard_map/corr/pallas_call | solution.py:165
  37.6 4.0 %all-to-all-start = ((bf16[4,2,2,64,256]{4,3,2,1,0:T(8,128)(2,1)}), bf16[4,2,2,64,256]{4,3,2,1,0:T(8,128)(2,1)S(1)}, u32[]{:S(2)}, u32[]{:S(2)}) async-start(bf16[4,2,2,64,256]{4,3,2,1,0:T(8,128)(2,1)} %corr.1), calls=%async_computation | async-start | bytes 1048576 | tf_op jit(solution)/shard_map/all_to_all | solution.py:415
  41.7 1.2 copy-done.1
  42.9 0.6 prep.1
  43.5 0.1 collective-permute-start.4
  43.6 5.1 %collective-permute-start.3 = (f32[3,64,256]{2,1,0:T(8,128)S(1)}, f32[3,64,256]{2,1,0:T(8,128)S(1)}, u32[]{:S(2)}, u32[]{:S(2)}) collective-permute-start(f32[3,64,256]{2,1,0:T(8,128)S(1)} %get-tuple-element.18), channel_id=1, source_target_pairs={{8,0},{0,8},{24,16},{16,24},{40,32},{32,40},{56,48},{48,56},{72,64... | collective-permute-start | bytes 589832 | tf_op jit(solution)/shard_map/ppermute | solution.py:18
  48.7 2.3 %all-to-all-done.pieces = bf16[4,2,2,64,256]{4,3,2,1,0:T(8,128)(2,1)S(1)} async-done(((bf16[4,2,2,64,256]{4,3,2,1,0:T(8,128)(2,1)}), bf16[4,2,2,64,256]{4,3,2,1,0:T(8,128)(2,1)S(1)}, u32[]{:S(2)}, u32[]{:S(2)}) %all-to-all-start) | async-done | bytes 524320 | tf_op jit(solution)/shard_map/all_to_all | solution.py:415
  50.9 0.1 summed.1
  51.0 2.7 %collective-permute-start.2 = (bf16[2,2,64,256]{3,2,1,0:T(8,128)(2,1)S(1)}, bf16[2,2,64,256]{3,2,1,0:T(8,128)(2,1)S(1)}, u32[]{:S(2)}, u32[]{:S(2)}) collective-permute-start(bf16[2,2,64,256]{3,2,1,0:T(8,128)(2,1)S(1)} %get-tuple-element.17), channel_id=1, source_target_pairs={{1,0},{0,1},{3,2},{2,3},{5,4},{4,5},{7,6},{6,7},{9,8},{8,9},{11,10... | collective-permute-start | bytes 393224 | tf_op jit(solution)/shard_map/ppermute | solution.py:18
  53.7 0.0 collective-permute-done.4
  53.8 0.0 collective-permute-done.3
  53.8 2.6 %collective-permute-done.2.refs_1_ = bf16[2,2,64,256]{3,2,1,0:T(8,128)(2,1)S(1)} collective-permute-done((bf16[2,2,64,256]{3,2,1,0:T(8,128)(2,1)S(1)}, bf16[2,2,64,256]{3,2,1,0:T(8,128)(2,1)S(1)}, u32[]{:S(2)}, u32[]{:S(2)}) %collective-permute-start.2) | collective-permute-done | bytes 131104 | tf_op jit(solution)/shard_map/ppermute | solution.py:18
  56.4 0.1 resid.1
  56.5 10.6 %all_to_all.10.mine = bf16[4,2,2,64,256]{4,3,2,1,0:T(8,128)(2,1)S(1)} all-to-all(bf16[4,2,2,64,256]{4,3,2,1,0:T(8,128)(2,1)S(1)} %resid.1), channel_id=1, replica_groups={{0,2,4,6},{1,3,5,7},{8,10,12,14},{9,11,13,15},{16,18,20,22},{17,19,21,2..., dimensions={0} | all-to-all | bytes 1048576 | tf_op jit(solution)/shard_map/all_to_all | solution.py:419
  67.1 2.8 %collective-permute-start.6 = (bf16[4,1,2,64,256]{4,3,2,1,0:T(8,128)(2,1)S(1)}, bf16[4,1,2,64,256]{4,3,2,1,0:T(8,128)(2,1)S(1)}, u32[]{:S(2)}, u32[]{:S(2)}) collective-permute-start(bf16[4,1,2,64,256]{4,3,2,1,0:T(8,128)(2,1)S(1)} %slice.14), channel_id=1, source_target_pairs={{8,0},{0,8},{24,16},{16,24},{40,32},{32,40},{56,48},{48,56},{72,64... | collective-permute-start | bytes 786440 | tf_op jit(solution)/shard_map/ppermute | solution.py:18
  69.9 3.8 %collective-permute-start.8 = (bf16[256,2048]{1,0:T(8,128)(2,1)}, bf16[256,2048]{1,0:T(8,128)(2,1)}, u32[]{:S(2)}, u32[]{:S(2)}) collective-permute-start(bf16[256,2048]{1,0:T(8,128)(2,1)} %get-tuple-element.21), channel_id=1, source_target_pairs={{240,0},{24,8},{0,16},{40,24},{16,32},{56,40},{32,48},{72,56},{48,... | collective-permute-start | bytes 3145736 | tf_op jit(solution)/shard_map/ppermute | solution.py:18
  73.7 0.0 collective-permute-start.9
  73.8 0.0 collective-permute-start.5
  73.8 0.0 collective-permute-done.6.mate_resid
  73.8 5.4 %early.1 = (f32[512,2048]{1,0:T(8,128)}, f32[1,2048]{1,0:T(1,128)S(1)}) custom-call(s32[1]{0:T(128)} %bitcast.par.refs_0_, bf16[4,2,2,64,256]{4,3,2,1,0:T(8,128)(2,1)S(1)} %all_to_all.10.mine, bf16[4,1,2,64,256]{4,3,2,1,0:T(8,128)(2,1)S(1)} %collective-permute-done.6.mate_resid, bf16[512,2048]{1,0:T(8,128)(2,1)S(1)} %bitcast.20, ...), custom_call_target="tpu_custom_call" | custom-call | flops 2147483648 | bytes 10485760 | tf_op jit(solution)/shard_map/early/pallas_call | solution.py:313
  79.2 0.1 collective-permute-start.12
  79.3 2.4 %collective-permute-start.11 = (f32[2048]{0:T(1024)S(1)}, f32[2048]{0:T(1024)S(1)}, u32[]{:S(2)}, u32[]{:S(2)}) collective-permute-start(f32[2048]{0:T(1024)S(1)} %bitcast.26), channel_id=1, source_target_pairs={{128,0},{136,8},{144,16},{152,24},{160,32},{168,40},{176,48},{184,... | collective-permute-start | bytes 24584 | tf_op jit(solution)/shard_map/ppermute | solution.py:18
  81.7 20.8 %collective-permute-done.5.far_resid = bf16[4,2,2,64,256]{4,3,2,1,0:T(8,128)(2,1)S(1)} collective-permute-done((bf16[4,2,2,64,256]{4,3,2,1,0:T(8,128)(2,1)S(1)}, bf16[4,2,2,64,256]{4,3,2,1,0:T(8,128)(2,1)S(1)}, u32[]{:S(2)}, u32[]{:S(2)}) %collective-permute-start.5) | collective-permute-done | bytes 524320 | tf_op jit(solution)/shard_map/ppermute | solution.py:18
  102.6 1.5 %collective-permute-start.10 = (f32[2048]{0:T(1024)S(1)}, f32[2048]{0:T(1024)S(1)}, u32[]{:S(2)}, u32[]{:S(2)}) collective-permute-start(f32[2048]{0:T(1024)S(1)} %bitcast.27), channel_id=1, source_target_pairs={{8,0},{0,8},{24,16},{16,24},{40,32},{32,40},{56,48},{48,56},{72,64... | collective-permute-start | bytes 24584 | tf_op jit(solution)/shard_map/ppermute | solution.py:18
  104.1 1.4 %turned.1.refs_2_ = bf16[512,1024]{1,0:T(8,128)(2,1)} custom-call(s32[1]{0:T(128)} %bitcast.par.refs_0_, bf16[4,2,2,64,256]{4,3,2,1,0:T(8,128)(2,1)S(1)} %all_to_all.10.mine, bf16[4,2,2,64,256]{4,3,2,1,0:T(8,128)(2,1)S(1)} %collective-permute-done.5.far_resid), custom_call_target="tpu_custom_call" | custom-call | bytes 2097152 | tf_op jit(solution)/shard_map/turned/pallas_call | solution.py:337
  105.4 0.0 collective-permute-done.10
  105.4 3.8 %collective-permute-start.14 = (f32[1,16,128]{2,1,0:T(8,128)S(1)}, f32[1,16,128]{2,1,0:T(8,128)S(1)}, u32[]{:S(2)}, u32[]{:S(2)}) collective-permute-start(f32[1,16,128]{2,1,0:T(8,128)S(1)} %add_bitcast_fusion), channel_id=1, source_target_pairs={{16,0},{24,8},{32,16},{40,24},{48,32},{56,40},{64,48},{72,56},{80,... | collective-permute-start | bytes 24584 | tf_op jit(solution)/shard_map/ppermute | solution.py:18
  109.2 0.0 collective-permute-done.8.refs_4_
  109.2 0.0 collective-permute-done.9.refs_5_
  109.2 5.4 %late.2.refs_8_ = f32[2,256,2048]{2,1,0:T(8,128)} custom-call(s32[1]{0:T(128)} %bitcast.par.refs_0_, f32[1,2048]{1,0:T(1,128)} %bitcast.21, bf16[512,1024]{1,0:T(8,128)(2,1)} %turned.1.refs_2_, f32[512,2048]{1,0:T(8,128)} %get-tuple-element.20.refs_3_, bf16[256,2048]{1,0:T(8,128)(2,1)} %collective-permute-done.8.refs_4_, ...), custom_call_target="tpu_custom_call" | custom-call | flops 1073741824 | bytes 6291456 | tf_op jit(solution)/shard_map/late/pallas_call | solution.py:358
  114.6 0.1 collective-permute-start.13
  114.8 0.1 collective-permute-start.16
  114.9 3.6 %collective-permute-done.13 = f32[1,16,128]{2,1,0:T(8,128)S(1)} collective-permute-done((f32[1,16,128]{2,1,0:T(8,128)S(1)}, f32[1,16,128]{2,1,0:T(8,128)S(1)}, u32[]{:S(2)}, u32[]{:S(2)}) %collective-permute-start.13) | collective-permute-done | bytes 8224 | tf_op jit(solution)/shard_map/ppermute | solution.py:18
  118.4 0.9 collective-permute-start.15
  119.3 5.4 %late.3 = f32[2,256,2048]{2,1,0:T(8,128)} custom-call(s32[1]{0:T(128)} %bitcast.par.refs_0_, f32[1,2048]{1,0:T(1,128)} %bitcast.22, bf16[512,1024]{1,0:T(8,128)(2,1)} %turned.1.refs_2_, f32[512,2048]{1,0:T(8,128)} %get-tuple-element.20.refs_3_, bf16[256,2048]{1,0:T(8,128)(2,1)} %collective-permute-done.8.refs_4_, ...), custom_call_target="tpu_custom_call", output_to_operand_aliasing={{}: (8, {})} | custom-call | flops 1073741824 | bytes 6291456 | tf_op jit(solution)/shard_map/late/pallas_call | solution.py:358
  124.7 0.0 collective-permute-done.16.below
  124.7 0.0 collective-permute-done.15.above
  124.7 0.6 ring_sum.1
  (19 shorter events, 0.1 us)
Async XLA Ops:
  0.6 7.9 %collective-permute-start.1 = (bf16[512,2048]{1,0:T(8,128)(2,1)}, bf16[512,2048]{1,0:T(8,128)(2,1)}, u32[]{:S(2)}, u32[]{:S(2)}) collective-permute-start(bf16[512,2048]{1,0:T(8,128)(2,1)} %bitcast.17), channel_id=1, source_target_pairs={{8,0},{0,8},{24,16},{16,24},{40,32},{32,40},{56,48},{48,56},{72,64... | collective-permute-start | bytes 6291464 | tf_op jit(solution)/shard_map/ppermute | solution.py:18
  3.9 28.6 %collective-permute-start = (bf16[512,2048]{1,0:T(8,128)(2,1)}, bf16[512,2048]{1,0:T(8,128)(2,1)}, u32[]{:S(2)}, u32[]{:S(2)}) collective-permute-start(bf16[512,2048]{1,0:T(8,128)(2,1)} %bitcast.18), channel_id=1, source_target_pairs={{16,0},{248,8},{32,16},{8,24},{48,32},{24,40},{64,48},{40,56},{80,... | collective-permute-start | bytes 6291464 | tf_op jit(solution)/shard_map/ppermute | solution.py:18
  4.6 3.3 %copy-start = (bf16[2,256,2048]{2,1,0:T(8,128)(2,1)S(1)}, bf16[2,256,2048]{2,1,0:T(8,128)(2,1)}, u32[]{:S(2)}) copy-start(bf16[2,256,2048]{2,1,0:T(8,128)(2,1)} %param.5) | copy-start | bytes 6291460
  7.9 0.7 copy-start.3
  32.5 41.2 %collective-permute-start.7 = (bf16[512,2048]{1,0:T(8,128)(2,1)}, bf16[512,2048]{1,0:T(8,128)(2,1)}, u32[]{:S(2)}, u32[]{:S(2)}) collective-permute-start(bf16[512,2048]{1,0:T(8,128)(2,1)} %collective-permute-done.near_source), channel_id=1, source_target_pairs={{8,0},{0,8},{24,16},{16,24},{40,32},{32,40},{56,48},{48,56},{72,64... | collective-permute-start | bytes 6291464 | tf_op jit(solution)/shard_map/ppermute | solution.py:18
  33.0 8.6 %copy-start.2 = (f32[2,256,256]{2,1,0:T(8,128)S(1)}, f32[2,256,256]{2,1,0:T(8,128)}, u32[]{:S(2)}) copy-start(f32[2,256,256]{2,1,0:T(8,128)} %amp_weight.1) | copy-start | bytes 1572868
  33.0 8.6 %copy-start.4 = (s32[1,2]{1,0:T(1,128)S(1)}, s32[1,2]{1,0:T(1,128)}, u32[]{:S(2)}) copy-start(s32[1,2]{1,0:T(1,128)} %used.1) | copy-start | bytes 28
  37.6 13.3 %all-to-all-start = ((bf16[4,2,2,64,256]{4,3,2,1,0:T(8,128)(2,1)}), bf16[4,2,2,64,256]{4,3,2,1,0:T(8,128)(2,1)S(1)}, u32[]{:S(2)}, u32[]{:S(2)}) async-start(bf16[4,2,2,64,256]{4,3,2,1,0:T(8,128)(2,1)} %corr.1), calls=%async_computation | async-start | bytes 1048576 | tf_op jit(solution)/shard_map/all_to_all | solution.py:415
  41.7 1.2 copy-start.1
  43.5 10.3 %collective-permute-start.4 = (f32[3,64,256]{2,1,0:T(8,128)S(1)}, f32[3,64,256]{2,1,0:T(8,128)S(1)}, u32[]{:S(2)}, u32[]{:S(2)}) collective-permute-start(f32[3,64,256]{2,1,0:T(8,128)S(1)} %get-tuple-element.19), channel_id=1, source_target_pairs={{16,0},{248,8},{32,16},{8,24},{48,32},{24,40},{64,48},{40,56},{80,... | collective-permute-start | bytes 589832 | tf_op jit(solution)/shard_map/ppermute | solution.py:18
  43.6 10.2 %collective-permute-start.3 = (f32[3,64,256]{2,1,0:T(8,128)S(1)}, f32[3,64,256]{2,1,0:T(8,128)S(1)}, u32[]{:S(2)}, u32[]{:S(2)}) collective-permute-start(f32[3,64,256]{2,1,0:T(8,128)S(1)} %get-tuple-element.18), channel_id=1, source_target_pairs={{8,0},{0,8},{24,16},{16,24},{40,32},{32,40},{56,48},{48,56},{72,64... | collective-permute-start | bytes 589832 | tf_op jit(solution)/shard_map/ppermute | solution.py:18
  51.0 5.4 %collective-permute-start.2 = (bf16[2,2,64,256]{3,2,1,0:T(8,128)(2,1)S(1)}, bf16[2,2,64,256]{3,2,1,0:T(8,128)(2,1)S(1)}, u32[]{:S(2)}, u32[]{:S(2)}) collective-permute-start(bf16[2,2,64,256]{3,2,1,0:T(8,128)(2,1)S(1)} %get-tuple-element.17), channel_id=1, source_target_pairs={{1,0},{0,1},{3,2},{2,3},{5,4},{4,5},{7,6},{6,7},{9,8},{8,9},{11,10... | collective-permute-start | bytes 393224 | tf_op jit(solution)/shard_map/ppermute | solution.py:18
  67.1 6.6 %collective-permute-start.6 = (bf16[4,1,2,64,256]{4,3,2,1,0:T(8,128)(2,1)S(1)}, bf16[4,1,2,64,256]{4,3,2,1,0:T(8,128)(2,1)S(1)}, u32[]{:S(2)}, u32[]{:S(2)}) collective-permute-start(bf16[4,1,2,64,256]{4,3,2,1,0:T(8,128)(2,1)S(1)} %slice.14), channel_id=1, source_target_pairs={{8,0},{0,8},{24,16},{16,24},{40,32},{32,40},{56,48},{48,56},{72,64... | collective-permute-start | bytes 786440 | tf_op jit(solution)/shard_map/ppermute | solution.py:18
  69.9 39.3 %collective-permute-start.8 = (bf16[256,2048]{1,0:T(8,128)(2,1)}, bf16[256,2048]{1,0:T(8,128)(2,1)}, u32[]{:S(2)}, u32[]{:S(2)}) collective-permute-start(bf16[256,2048]{1,0:T(8,128)(2,1)} %get-tuple-element.21), channel_id=1, source_target_pairs={{240,0},{24,8},{0,16},{40,24},{16,32},{56,40},{32,48},{72,56},{48,... | collective-permute-start | bytes 3145736 | tf_op jit(solution)/shard_map/ppermute | solution.py:18
  73.7 35.5 %collective-permute-start.9 = (bf16[256,2048]{1,0:T(8,128)(2,1)}, bf16[256,2048]{1,0:T(8,128)(2,1)}, u32[]{:S(2)}, u32[]{:S(2)}) collective-permute-start(bf16[256,2048]{1,0:T(8,128)(2,1)} %get-tuple-element.22), channel_id=1, source_target_pairs={{240,0},{24,8},{0,16},{40,24},{16,32},{56,40},{32,48},{72,56},{48,... | collective-permute-start | bytes 3145736 | tf_op jit(solution)/shard_map/ppermute | solution.py:18
  73.8 28.8 %collective-permute-start.5 = (bf16[4,2,2,64,256]{4,3,2,1,0:T(8,128)(2,1)S(1)}, bf16[4,2,2,64,256]{4,3,2,1,0:T(8,128)(2,1)S(1)}, u32[]{:S(2)}, u32[]{:S(2)}) collective-permute-start(bf16[4,2,2,64,256]{4,3,2,1,0:T(8,128)(2,1)S(1)} %all_to_all.10.mine), channel_id=1, source_target_pairs={{240,0},{24,8},{0,16},{40,24},{16,32},{56,40},{32,48},{72,56},{48,... | collective-permute-start | bytes 1572872 | tf_op jit(solution)/shard_map/ppermute | solution.py:18
  79.2 26.2 %collective-permute-start.12 = (f32[2048]{0:T(1024)S(1)}, f32[2048]{0:T(1024)S(1)}, u32[]{:S(2)}, u32[]{:S(2)}) collective-permute-start(f32[2048]{0:T(1024)S(1)} %bitcast.25), channel_id=1, source_target_pairs={{136,0},{128,8},{152,16},{144,24},{168,32},{160,40},{184,48},{176,... | collective-permute-start | bytes 24584 | tf_op jit(solution)/shard_map/ppermute | solution.py:18
  79.3 26.1 %collective-permute-start.11 = (f32[2048]{0:T(1024)S(1)}, f32[2048]{0:T(1024)S(1)}, u32[]{:S(2)}, u32[]{:S(2)}) collective-permute-start(f32[2048]{0:T(1024)S(1)} %bitcast.26), channel_id=1, source_target_pairs={{128,0},{136,8},{144,16},{152,24},{160,32},{168,40},{176,48},{184,... | collective-permute-start | bytes 24584 | tf_op jit(solution)/shard_map/ppermute | solution.py:18
  102.6 2.8 %collective-permute-start.10 = (f32[2048]{0:T(1024)S(1)}, f32[2048]{0:T(1024)S(1)}, u32[]{:S(2)}, u32[]{:S(2)}) collective-permute-start(f32[2048]{0:T(1024)S(1)} %bitcast.27), channel_id=1, source_target_pairs={{8,0},{0,8},{24,16},{16,24},{40,32},{32,40},{56,48},{48,56},{72,64... | collective-permute-start | bytes 24584 | tf_op jit(solution)/shard_map/ppermute | solution.py:18
  105.4 9.3 %collective-permute-start.14 = (f32[1,16,128]{2,1,0:T(8,128)S(1)}, f32[1,16,128]{2,1,0:T(8,128)S(1)}, u32[]{:S(2)}, u32[]{:S(2)}) collective-permute-start(f32[1,16,128]{2,1,0:T(8,128)S(1)} %add_bitcast_fusion), channel_id=1, source_target_pairs={{16,0},{24,8},{32,16},{40,24},{48,32},{56,40},{64,48},{72,56},{80,... | collective-permute-start | bytes 24584 | tf_op jit(solution)/shard_map/ppermute | solution.py:18
  114.6 3.8 %collective-permute-start.13 = (f32[1,16,128]{2,1,0:T(8,128)S(1)}, f32[1,16,128]{2,1,0:T(8,128)S(1)}, u32[]{:S(2)}, u32[]{:S(2)}) collective-permute-start(f32[1,16,128]{2,1,0:T(8,128)S(1)} %add_bitcast_fusion), channel_id=1, source_target_pairs={{112,0},{120,8},{0,16},{8,24},{16,32},{24,40},{32,48},{40,56},{48,... | collective-permute-start | bytes 24584 | tf_op jit(solution)/shard_map/ppermute | solution.py:18
  114.8 10.0 %collective-permute-start.16 = (f32[2,16,128]{2,1,0:T(8,128)S(1)}, f32[2,16,128]{2,1,0:T(8,128)S(1)}, u32[]{:S(2)}, u32[]{:S(2)}) collective-permute-start(f32[2,16,128]{2,1,0:T(8,128)S(1)} %pad_maximum_fusion.2), channel_id=1, source_target_pairs={{80,0},{88,8},{96,16},{104,24},{112,32},{120,40},{0,48},{8,56},{16... | collective-permute-start | bytes 49160 | tf_op jit(solution)/shard_map/ppermute | solution.py:18
  118.4 6.3 %collective-permute-start.15 = (f32[3,16,128]{2,1,0:T(8,128)S(1)}, f32[3,16,128]{2,1,0:T(8,128)S(1)}, u32[]{:S(2)}, u32[]{:S(2)}) collective-permute-start(f32[3,16,128]{2,1,0:T(8,128)S(1)} %pad_maximum_fusion.1.rows), channel_id=1, source_target_pairs={{48,0},{56,8},{64,16},{72,24},{80,32},{88,40},{96,48},{104,56},{11... | collective-permute-start | bytes 73736 | tf_op jit(solution)/shard_map/ppermute | solution.py:18

commit v8 on v6

--- a/solution.py
+++ b/solution.py
@@ -194,68 +194,81 @@
     mat[half:, base : base + half] = -imag
 
 
-def early_kernel(par, mine, mate_resid, own_source, mate_source, near_source, mate_near_source, early, kernel_part, mat, own, blocks, out, sems, out_sems):
+def early_kernel(par, mine, own_source, mate_source, near_source, early, kernel_part, mat, own, blocks, out, sems, out_sems):
     both = own.shape[0]
 
-    def run(second_source):
-        parts = [(near_source, blocks.at[:both]), (second_source, blocks.at[both:]), (own_source, own)]
+    def run(even):
+        parts = [(near_source, blocks.at[:both]), (mate_source, blocks.at[both:]), (own_source, own)]
         copies = fetches(parts, sems, CHUNK)
         place(mat, 0, assembled(mine, 1, False))
-        place(mat, both, assembled(mate_resid, 0, False))
+        place(mat, both, assembled(mine, 0, even))
         sends = []
         for j, row in enumerate(copies):
             for copy in row:
                 copy.wait()
             cols = pl.ds(j * CHUNK, CHUNK)
-            fields = jnp.dot(mat[...], blocks[:, cols], preferred_element_type=jnp.float32)
+            if even:
+                fields = jnp.dot(mat[...], blocks[:, cols], preferred_element_type=jnp.float32)
+            else:
+                fields = jnp.dot(mat[:, :both], blocks[:both, cols], preferred_element_type=jnp.float32)
             out[j] = fields
             send = pltpu.make_async_copy(out.at[j], early.at[:, cols], out_sems.at[j])
             send.start()
             sends.append(send)
-            kernel_part[:, cols] = jnp.sum(own[:, cols].astype(jnp.float32) * fields, axis=0, keepdims=True)
+            share = own[:, cols].astype(jnp.float32) * fields
+            if not even:
+                other = jnp.dot(mat[:, both:], blocks[:both, cols], preferred_element_type=jnp.float32)
+                share = share + blocks[both:, cols].astype(jnp.float32) * other
+            kernel_part[:, cols] = jnp.sum(share, axis=0, keepdims=True)
         for send in sends:
             send.wait()
 
     @pl.when(par[0] == 0)
     def _():
-        run(mate_near_source)
+        run(True)
 
     @pl.when(par[0] == 1)
     def _():
-        run(mate_source)
-
-
-def turn_kernel(par, mine, far_resid, mat):
+        run(False)
+
+
+def turn_kernel(par, mate_resid, far_resid, mat):
     both = mat.shape[0]
     place(mat, 0, assembled(far_resid, 1, True))
 
     @pl.when(par[0] == 0)
     def _():
-        place(mat, both, assembled(mine, 0, True))
+        place(mat, both, assembled(mate_resid, 0, False))
 
     @pl.when(par[0] == 1)
     def _():
         place(mat, both, assembled(far_resid, 0, True))
+        place(mat, 2 * both, assembled(mate_resid, 0, False))
 
 
 def late_kernel(inv_norm, par, scale, mat, early_source, far_real, far_imag, mate_source, mate_near_source, adjoint, blocks, early, out, sems, out_sems):
     both = early.shape[0]
     half = both // 2
 
-    def run(second_source):
+    def run(even):
+        depth = 2 * both if even else 3 * both
         parts = [
             (far_real, blocks.at[:half]),
             (far_imag, blocks.at[half:both]),
-            (second_source, blocks.at[both:]),
+            (mate_near_source, blocks.at[both : 2 * both]),
             (early_source, early),
         ]
+        if not even:
+            parts.append((mate_source, blocks.at[2 * both :]))
         copies = fetches(parts, sems, CHUNK)
         sends = []
         for j, row in enumerate(copies):
             for copy in row:
                 copy.wait()
             cols = pl.ds(j * CHUNK, CHUNK)
-            fields = early[:, cols] + jnp.dot(mat[...], blocks[:, cols], preferred_element_type=jnp.float32)
+            fields = early[:, cols] + jnp.dot(
+                mat[:, :depth], blocks[:depth, cols], preferred_element_type=jnp.float32
+            )
             out[j] = (fields * (inv_norm * scale[:, cols])).reshape(out.shape[1:])
             send = pltpu.make_async_copy(out.at[j], adjoint.at[:, :, cols], out_sems.at[j])
             send.start()
@@ -265,11 +278,11 @@
 
     @pl.when(par[0] == 0)
     def _():
-        run(mate_source)
+        run(True)
 
     @pl.when(par[0] == 1)
     def _():
-        run(mate_near_source)
+        run(False)
 
 
 def ring_kernel(place_of, rows, above, below, out, slots):
@@ -300,7 +313,7 @@
     )(place_of, rows, above, below)
 
 
-def early_fields(par, mine, mate_resid, own, mate, near, mate_near):
+def early_fields(par, mine, own, mate, near):
     both, cols = own.shape
     vmem = pl.BlockSpec(memory_space=pltpu.VMEM)
     anywhere = pl.BlockSpec(memory_space=pl.ANY)
@@ -310,7 +323,7 @@
             pltpu.HBM((both, cols), jnp.float32),
             jax.ShapeDtypeStruct((1, cols), jnp.float32),
         ),
-        in_specs=[pl.BlockSpec(memory_space=pltpu.SMEM)] + [vmem] * 2 + [anywhere] * 4,
+        in_specs=[pl.BlockSpec(memory_space=pltpu.SMEM), vmem] + [anywhere] * 3,
         out_specs=(pl.BlockSpec(memory_space=pltpu.HBM), vmem),
         scratch_shapes=[pltpu.VMEM((both, 2 * both), jnp.bfloat16)]
         + [
@@ -323,20 +336,20 @@
         cost_estimate=pl.CostEstimate(flops=4 * both * both * cols, bytes_accessed=10 * both * cols, transcendentals=0),
         compiler_params=pltpu.CompilerParams(vmem_limit_bytes=20 << 20),
         name="early",
-    )(par, mine, mate_resid, own, mate, near, mate_near)
-
-
-def turned(par, mine, far_resid, both):
+    )(par, mine, own, mate, near)
+
+
+def turned(par, mate_resid, far_resid, both):
     vmem = pl.BlockSpec(memory_space=pltpu.VMEM)
     return pl.pallas_call(
         turn_kernel,
-        out_shape=jax.ShapeDtypeStruct((both, 2 * both), jnp.bfloat16),
+        out_shape=jax.ShapeDtypeStruct((both, 3 * both), jnp.bfloat16),
         in_specs=[pl.BlockSpec(memory_space=pltpu.SMEM), vmem, vmem],
         out_specs=vmem,
         cost_estimate=pl.CostEstimate(flops=0, bytes_accessed=2 << 20, transcendentals=0),
         compiler_params=pltpu.CompilerParams(vmem_limit_bytes=8 << 20),
         name="turned",
-    )(par, mine, far_resid)
+    )(par, mate_resid, far_resid)
 
 
 def late_fields(par, scale, mat, far, early, mate, mate_near, inv_norm):
@@ -354,10 +367,10 @@
         in_specs=[pl.BlockSpec(memory_space=pltpu.SMEM)] + [vmem] * 2 + [hbm] * 5,
         out_specs=hbm,
         scratch_shapes=[
-            pltpu.VMEM((2 * both, cols), jnp.bfloat16),
+            pltpu.VMEM((3 * both, cols), jnp.bfloat16),
             pltpu.VMEM((both, cols), jnp.float32),
             pltpu.VMEM((cols // CHUNK, 2, half, CHUNK), jnp.float32),
-            pltpu.SemaphoreType.DMA((4, cols // CHUNK)),
+            pltpu.SemaphoreType.DMA((5, cols // CHUNK)),
             pltpu.SemaphoreType.DMA((cols // CHUNK,)),
         ],
         cost_estimate=pl.CostEstimate(flops=4 * both * both * cols, bytes_accessed=12 * both * cols, transcendentals=0),
@@ -407,9 +420,9 @@
     mine = lax.all_to_all(resid, "grid", 0, 0, tiled=True, axis_index_groups=along_x)
     mate_resid = permuted(mine[:, :1], "cable", partner)
     far_resid = permuted(mine, "cable", far_chip)
-    early, kernel_part = early_fields(par, mine, mate_resid, own, mate, near, mate_near)
+    early, kernel_part = early_fields(par, mine, own, mate, near)
     kernel = kernel_part[0] * kernel_scale
-    mat = turned(par, mine, far_resid, 2 * row_count)
+    mat = turned(par, mate_resid, far_resid, 2 * row_count)
     adjoint = late_fields(par, scale, mat, far, early, mate, mate_near, inv_norm)
     distance = block_count // 2
     swapped = [permuted(kernel, "cable", lambda i: i ^ d) for d in (1, distance, distance + 1)]

time: 120 us -> 124 us (1.033)
  waiting for transfers between devices: 51.5 us -> 66.5 us
  blocking collectives: 10.6 us -> 0 us
  starting transfers between devices: 31.7 us -> 27.6 us
  Pallas kernels: 17.3 us -> 19.2 us
    all_to_all x1 -> x0, blocking collectives: 10.6 us -> none  [shards(): lax.all_to_all(resid, 'grid', 0, 0, tiled=True, axis_index_groups=along_x)]
    ppermute x17, waiting for transfers between devices: 49.3 us -> 59.8 us  [permuted(): lax.ppermute(block, axis, [(source_of(i) % size, i) for i in range(size)])]
    ppermute x17, starting transfers between devices: 27.6 us -> 19.6 us  [permuted(): lax.ppermute(block, axis, [(source_of(i) % size, i) for i in range(size)])]
    all_to_all x0 -> x1, waiting for transfers between devices: none -> 5.39 us  [shards(): lax.all_to_all(resid, 'grid', 0, 0, tiled=True, axis_index_groups=along_x)]
    all_to_all x0 -> x1, starting transfers between devices: none -> 4 us  [shards(): lax.all_to_all(resid, 'grid', 0, 0, tiled=True, axis_index_groups=along_x)]
  transfers between devices with their start and end apart: 18 -> 19, of which waited for: 7 -> 12; matrix products, arithmetic and copies ran while one was open for 6% -> 6% of each run, Pallas kernels for 14% -> 6%
where the time goes in v8:
time: 124 us; the launch traced here: 123 us
  waiting for transfers between devices  66.5 us (54%)
  starting transfers between devices  27.6 us (22%)
  Pallas kernels  19.2 us (15%)
  other arithmetic  4.53 us (4%)
  local copies, waits for them, and re-layouts  4.5 us (4%)
    ppermute x17, waiting for transfers between devices, permuted(): lax.ppermute(block, axis, [(source_of(i) % size, i) for i in range(size)])  59.8 us
    ppermute x17, starting transfers between devices, permuted(): lax.ppermute(block, axis, [(source_of(i) % size, i) for i in range(size)])  19.6 us
    pallas_call x1, Pallas kernels, late_fields(): pl.pallas_call(body, out_shape=jax.ShapeDtypeStruct((2, half, cols), jnp....  6.83 us
    all_to_all x1, waiting for transfers between devices, shards(): lax.all_to_all(resid, 'grid', 0, 0, tiled=True, axis_index_groups=along_x)  5.39 us
    pallas_call x1, Pallas kernels, early_fields(): pl.pallas_call(early_kernel, out_shape=(pltpu.HBM((both, cols), jnp.float...  5.28 us
    pallas_call x1, Pallas kernels, correlations(): pl.pallas_call(corr_kernel, out_shape=jax.ShapeDtypeStruct((parts, 2, 2,...  4.66 us
    all_to_all x1, starting transfers between devices, shards(): lax.all_to_all(partials, 'grid', 0, 0, tiled=True, axis_index_groups=alon...  4.02 us
    all_to_all x1, starting transfers between devices, shards(): lax.all_to_all(resid, 'grid', 0, 0, tiled=True, axis_index_groups=along_x)  4 us
  transfers between devices with their start and end apart: 19, of which 12 were waited for; matrix products, arithmetic and copies ran while one was open for 6% of the time, Pallas kernels for 6%

profile of v8, /device:TPU:1, one launch (start us, length us, event | category | flops | bytes accessed | tf_op | source)
XLA Modules:
  0.0 123.2 jit_solution(18167230183844089045)
XLA Ops:
  0.6 3.3 %collective-permute-start.1 = (bf16[512,2048]{1,0:T(8,128)(2,1)}, bf16[512,2048]{1,0:T(8,128)(2,1)}, u32[]{:S(2)}, u32[]{:S(2)}) collective-permute-start(bf16[512,2048]{1,0:T(8,128)(2,1)} %bitcast.17), channel_id=1, source_target_pairs={{8,0},{0,8},{24,16},{16,24},{40,32},{32,40},{56,48},{48,56},{72,64... | collective-permute-start | bytes 6291464 | tf_op jit(solution)/shard_map/ppermute | solution.py:18
  3.9 0.0 collective-permute-start
  3.9 0.7 broadcast_select_fusion
  4.6 3.3 %slice_bitcast_fusion = (bf16[256,2048]{1,0:T(8,128)(2,1)}, bf16[256,2048]{1,0:T(8,128)(2,1)}) fusion(bf16[2,256,2048]{2,1,0:T(8,128)(2,1)} %param.5), kind=kLoop, calls=%fused_computation.2 | loop fusion | bytes 4194304 | tf_op jit(solution)/shard_map/squeeze | solution.py:408
  7.9 0.7 multiply_convert_fusion.lhs_second
  8.6 0.0 collective-permute-done.1.mate_source.refs_6_
  8.6 2.1 %multiply_convert_fusion.1.lhs_first = bf16[512,2048]{1,0:T(8,128)(2,1)S(1)} fusion(bf16[512,2048]{1,0:T(8,128)(2,1)} %collective-permute-done.1.mate_source.refs_6_, f32[2048]{0:T(1024)S(1)} %copy-done.3), kind=kLoop, calls=%fused_computation.1 | loop fusion | flops 3145728 | bytes 4202496 | tf_op jit(solution)/shard_map/convert_element_type | solution.py:406
  10.7 21.8 %collective-permute-done.near_source = bf16[512,2048]{1,0:T(8,128)(2,1)} collective-permute-done((bf16[512,2048]{1,0:T(8,128)(2,1)}, bf16[512,2048]{1,0:T(8,128)(2,1)}, u32[]{:S(2)}, u32[]{:S(2)}) %collective-permute-start) | collective-permute-done | bytes 2097184 | tf_op jit(solution)/shard_map/ppermute | solution.py:18
  32.5 4.7 %corr.1 = bf16[4,2,2,64,256]{4,3,2,1,0:T(8,128)(2,1)} custom-call(s32[1]{0:T(128)} %bitcast.par.refs_0_, f32[1,2048]{1,0:T(1,128)S(1)} %bitcast.21, bf16[512,2048]{1,0:T(8,128)(2,1)S(1)} %multiply_convert_fusion.1.lhs_first, bf16[512,2048]{1,0:T(8,128)(2,1)S(1)} %multiply_convert_fusion.lhs_second, bf16[512,2048]{1,0:T(8,128)(2,1)S(1)} %bitcast.19, ...), custom_call_target="tpu_custom_call" | custom-call | flops 2147483648 | bytes 8388608 | tf_op jit(solution)/shard_map/corr/pallas_call | solution.py:164
  37.2 4.0 %all-to-all-start = ((bf16[4,2,2,64,256]{4,3,2,1,0:T(8,128)(2,1)}), bf16[4,2,2,64,256]{4,3,2,1,0:T(8,128)(2,1)S(1)}, u32[]{:S(2)}, u32[]{:S(2)}) async-start(bf16[4,2,2,64,256]{4,3,2,1,0:T(8,128)(2,1)} %corr.1), calls=%async_computation | async-start | bytes 1048576 | tf_op jit(solution)/shard_map/all_to_all | solution.py:416
  41.2 1.2 copy-done.1
  42.5 0.6 prep.1
  43.0 0.1 collective-permute-start.4
  43.1 5.6 %collective-permute-start.3 = (f32[3,64,256]{2,1,0:T(8,128)S(1)}, f32[3,64,256]{2,1,0:T(8,128)}, u32[]{:S(2)}, u32[]{:S(2)}) collective-permute-start(f32[3,64,256]{2,1,0:T(8,128)S(1)} %get-tuple-element.18), channel_id=1, source_target_pairs={{8,0},{0,8},{24,16},{16,24},{40,32},{32,40},{56,48},{48,56},{72,64... | collective-permute-start | bytes 589832 | tf_op jit(solution)/shard_map/ppermute | solution.py:18
  48.8 0.0 collective-permute-start.9
  48.8 1.3 %all-to-all-done.pieces = bf16[4,2,2,64,256]{4,3,2,1,0:T(8,128)(2,1)S(1)} async-done(((bf16[4,2,2,64,256]{4,3,2,1,0:T(8,128)(2,1)}), bf16[4,2,2,64,256]{4,3,2,1,0:T(8,128)(2,1)S(1)}, u32[]{:S(2)}, u32[]{:S(2)}) %all-to-all-start) | async-done | bytes 524320 | tf_op jit(solution)/shard_map/all_to_all | solution.py:416
  50.0 0.1 summed.1
  50.1 2.7 %collective-permute-start.2 = (bf16[2,2,64,256]{3,2,1,0:T(8,128)(2,1)S(1)}, bf16[2,2,64,256]{3,2,1,0:T(8,128)(2,1)S(1)}, u32[]{:S(2)}, u32[]{:S(2)}) collective-permute-start(bf16[2,2,64,256]{3,2,1,0:T(8,128)(2,1)S(1)} %get-tuple-element.17), channel_id=1, source_target_pairs={{1,0},{0,1},{3,2},{2,3},{5,4},{4,5},{7,6},{6,7},{9,8},{8,9},{11,10... | collective-permute-start | bytes 393224 | tf_op jit(solution)/shard_map/ppermute | solution.py:18
  52.8 0.0 collective-permute-done.4
  52.9 0.0 collective-permute-done.3
  52.9 1.0 pad_maximum_fusion.refs_2_
  53.8 1.7 %collective-permute-done.2.refs_1_ = bf16[2,2,64,256]{3,2,1,0:T(8,128)(2,1)S(1)} collective-permute-done((bf16[2,2,64,256]{3,2,1,0:T(8,128)(2,1)S(1)}, bf16[2,2,64,256]{3,2,1,0:T(8,128)(2,1)S(1)}, u32[]{:S(2)}, u32[]{:S(2)}) %collective-permute-start.2) | collective-permute-done | bytes 131104 | tf_op jit(solution)/shard_map/ppermute | solution.py:18
  55.5 0.9 resid.1
  56.4 4.0 %all-to-all-start.1 = ((bf16[4,2,2,64,256]{4,3,2,1,0:T(8,128)(2,1)}), bf16[4,2,2,64,256]{4,3,2,1,0:T(8,128)(2,1)S(1)}, u32[]{:S(2)}, u32[]{:S(2)}) async-start(bf16[4,2,2,64,256]{4,3,2,1,0:T(8,128)(2,1)} %resid.1), calls=%async_computation.1 | async-start | bytes 1048576 | tf_op jit(solution)/shard_map/all_to_all | solution.py:420
  60.4 1.6 %collective-permute-start.7 = (bf16[256,2048]{1,0:T(8,128)(2,1)}, bf16[256,2048]{1,0:T(8,128)(2,1)}, u32[]{:S(2)}, u32[]{:S(2)}) collective-permute-start(bf16[256,2048]{1,0:T(8,128)(2,1)} %get-tuple-element.21), channel_id=1, source_target_pairs={{240,0},{24,8},{0,16},{40,24},{16,32},{56,40},{32,48},{72,56},{48,... | collective-permute-start | bytes 3145736 | tf_op jit(solution)/shard_map/ppermute | solution.py:18
  61.9 0.1 collective-permute-start.8
  62.0 5.4 %all-to-all-done.1.mine = bf16[4,2,2,64,256]{4,3,2,1,0:T(8,128)(2,1)S(1)} async-done(((bf16[4,2,2,64,256]{4,3,2,1,0:T(8,128)(2,1)}), bf16[4,2,2,64,256]{4,3,2,1,0:T(8,128)(2,1)S(1)}, u32[]{:S(2)}, u32[]{:S(2)}) %all-to-all-start.1) | async-done | bytes 524320 | tf_op jit(solution)/shard_map/all_to_all | solution.py:420
  67.4 5.3 %early.1 = (f32[512,2048]{1,0:T(8,128)}, f32[1,2048]{1,0:T(1,128)S(1)}) custom-call(s32[1]{0:T(128)} %bitcast.par.refs_0_, bf16[4,2,2,64,256]{4,3,2,1,0:T(8,128)(2,1)S(1)} %all-to-all-done.1.mine, bf16[512,2048]{1,0:T(8,128)(2,1)S(1)} %bitcast.20, bf16[512,2048]{1,0:T(8,128)(2,1)} %collective-permute-done.1.mate_source.refs_6_, ...), custom_call_target="tpu_custom_call" | custom-call | flops 2147483648 | bytes 10485760 | tf_op jit(solution)/shard_map/early/pallas_call | solution.py:320
  72.7 3.5 %collective-permute-start.10 = (f32[2048]{0:T(1024)S(1)}, f32[2048]{0:T(1024)S(1)}, u32[]{:S(2)}, u32[]{:S(2)}) collective-permute-start(f32[2048]{0:T(1024)S(1)} %bitcast.23), channel_id=1, source_target_pairs={{8,0},{0,8},{24,16},{16,24},{40,32},{32,40},{56,48},{48,56},{72,64... | collective-permute-start | bytes 24584 | tf_op jit(solution)/shard_map/ppermute | solution.py:18
  76.2 0.2 collective-permute-start.11
  76.4 0.7 collective-permute-done.10
  77.1 0.9 collective-permute-start.12
  78.0 12.8 %collective-permute-done.11 = f32[2048]{0:T(1024)S(1)} collective-permute-done((f32[2048]{0:T(1024)S(1)}, f32[2048]{0:T(1024)S(1)}, u32[]{:S(2)}, u32[]{:S(2)}) %collective-permute-start.11) | collective-permute-done | bytes 8224 | tf_op jit(solution)/shard_map/ppermute | solution.py:18
  90.8 0.1 collective-permute-done.12
  91.0 0.0 collective-permute-start.14
  91.0 8.3 %collective-permute-done.14 = f32[1,16,128]{2,1,0:T(8,128)S(1)} collective-permute-done((f32[1,16,128]{2,1,0:T(8,128)S(1)}, f32[1,16,128]{2,1,0:T(8,128)S(1)}, u32[]{:S(2)}, u32[]{:S(2)}) %collective-permute-start.14) | collective-permute-done | bytes 8224 | tf_op jit(solution)/shard_map/ppermute | solution.py:18
  99.3 0.0 collective-permute-start.13
  99.3 3.7 %collective-permute-done.13 = f32[1,16,128]{2,1,0:T(8,128)S(1)} collective-permute-done((f32[1,16,128]{2,1,0:T(8,128)S(1)}, f32[1,16,128]{2,1,0:T(8,128)S(1)}, u32[]{:S(2)}, u32[]{:S(2)}) %collective-permute-start.13) | collective-permute-done | bytes 8224 | tf_op jit(solution)/shard_map/ppermute | solution.py:18
  103.0 5.6 %collective-permute-done.16.below = f32[2,16,128]{2,1,0:T(8,128)S(1)} collective-permute-done((f32[2,16,128]{2,1,0:T(8,128)S(1)}, f32[2,16,128]{2,1,0:T(8,128)S(1)}, u32[]{:S(2)}, u32[]{:S(2)}) %collective-permute-start.16) | collective-permute-done | bytes 16416 | tf_op jit(solution)/shard_map/ppermute | solution.py:18
  108.7 4.5 %collective-permute-done.15.above = f32[3,16,128]{2,1,0:T(8,128)S(1)} collective-permute-done((f32[3,16,128]{2,1,0:T(8,128)S(1)}, f32[3,16,128]{2,1,0:T(8,128)S(1)}, u32[]{:S(2)}, u32[]{:S(2)}) %collective-permute-start.15) | collective-permute-done | bytes 24608 | tf_op jit(solution)/shard_map/ppermute | solution.py:18
  113.1 1.6 %collective-permute-start.5 = (bf16[4,1,2,64,256]{4,3,2,1,0:T(8,128)(2,1)S(1)}, bf16[4,1,2,64,256]{4,3,2,1,0:T(8,128)(2,1)S(1)}, u32[]{:S(2)}, u32[]{:S(2)}) collective-permute-start(bf16[4,1,2,64,256]{4,3,2,1,0:T(8,128)(2,1)S(1)} %slice.14), channel_id=1, source_target_pairs={{8,0},{0,8},{24,16},{16,24},{40,32},{32,40},{56,48},{48,56},{72,64... | collective-permute-start | bytes 786440 | tf_op jit(solution)/shard_map/ppermute | solution.py:18
  114.8 0.6 ring_sum.1
  115.4 0.5 collective-permute-done.5.mate_resid
  115.9 0.0 collective-permute-done.6.far_resid
  115.9 0.3 turned.1.refs_2_
  116.2 0.0 collective-permute-done.7.refs_4_
  116.2 0.0 collective-permute-done.8.refs_5_
  116.3 6.8 %late.1 = f32[2,256,2048]{2,1,0:T(8,128)} custom-call(s32[1]{0:T(128)} %bitcast.par.refs_0_, f32[1,2048]{1,0:T(1,128)S(1)} %bitcast.22, bf16[512,1536]{1,0:T(8,128)(2,1)S(1)} %turned.1.refs_2_, f32[512,2048]{1,0:T(8,128)} %get-tuple-element.20.refs_3_, bf16[256,2048]{1,0:T(8,128)(2,1)} %collective-permute-done.7.refs_4_, ...), custom_call_target="tpu_custom_call" | custom-call | flops 2147483648 | bytes 12582912 | tf_op jit(solution)/shard_map/late/pallas_call | solution.py:364
  (19 shorter events, 0.1 us)
Async XLA Ops:
  0.6 7.9 %collective-permute-start.1 = (bf16[512,2048]{1,0:T(8,128)(2,1)}, bf16[512,2048]{1,0:T(8,128)(2,1)}, u32[]{:S(2)}, u32[]{:S(2)}) collective-permute-start(bf16[512,2048]{1,0:T(8,128)(2,1)} %bitcast.17), channel_id=1, source_target_pairs={{8,0},{0,8},{24,16},{16,24},{40,32},{32,40},{56,48},{48,56},{72,64... | collective-permute-start | bytes 6291464 | tf_op jit(solution)/shard_map/ppermute | solution.py:18
  3.9 28.6 %collective-permute-start = (bf16[512,2048]{1,0:T(8,128)(2,1)}, bf16[512,2048]{1,0:T(8,128)(2,1)}, u32[]{:S(2)}, u32[]{:S(2)}) collective-permute-start(bf16[512,2048]{1,0:T(8,128)(2,1)} %bitcast.18), channel_id=1, source_target_pairs={{16,0},{248,8},{32,16},{8,24},{48,32},{24,40},{64,48},{40,56},{80,... | collective-permute-start | bytes 6291464 | tf_op jit(solution)/shard_map/ppermute | solution.py:18
  4.6 3.3 %copy-start = (bf16[2,256,2048]{2,1,0:T(8,128)(2,1)S(1)}, bf16[2,256,2048]{2,1,0:T(8,128)(2,1)}, u32[]{:S(2)}) copy-start(bf16[2,256,2048]{2,1,0:T(8,128)(2,1)} %param.5) | copy-start | bytes 6291460
  7.9 0.7 copy-start.3
  32.5 8.7 %copy-start.2 = (f32[2,256,256]{2,1,0:T(8,128)S(1)}, f32[2,256,256]{2,1,0:T(8,128)}, u32[]{:S(2)}) copy-start(f32[2,256,256]{2,1,0:T(8,128)} %amp_weight.1) | copy-start | bytes 1572868
  32.5 8.7 %copy-start.4 = (s32[1,2]{1,0:T(1,128)S(1)}, s32[1,2]{1,0:T(1,128)}, u32[]{:S(2)}) copy-start(s32[1,2]{1,0:T(1,128)} %used.1) | copy-start | bytes 28
  37.2 12.8 %all-to-all-start = ((bf16[4,2,2,64,256]{4,3,2,1,0:T(8,128)(2,1)}), bf16[4,2,2,64,256]{4,3,2,1,0:T(8,128)(2,1)S(1)}, u32[]{:S(2)}, u32[]{:S(2)}) async-start(bf16[4,2,2,64,256]{4,3,2,1,0:T(8,128)(2,1)} %corr.1), calls=%async_computation | async-start | bytes 1048576 | tf_op jit(solution)/shard_map/all_to_all | solution.py:416
  41.2 1.2 copy-start.1
  43.0 9.8 %collective-permute-start.4 = (f32[3,64,256]{2,1,0:T(8,128)S(1)}, f32[3,64,256]{2,1,0:T(8,128)}, u32[]{:S(2)}, u32[]{:S(2)}) collective-permute-start(f32[3,64,256]{2,1,0:T(8,128)S(1)} %get-tuple-element.19), channel_id=1, source_target_pairs={{16,0},{248,8},{32,16},{8,24},{48,32},{24,40},{64,48},{40,56},{80,... | collective-permute-start | bytes 589832 | tf_op jit(solution)/shard_map/ppermute | solution.py:18
  43.1 9.7 %collective-permute-start.3 = (f32[3,64,256]{2,1,0:T(8,128)S(1)}, f32[3,64,256]{2,1,0:T(8,128)}, u32[]{:S(2)}, u32[]{:S(2)}) collective-permute-start(f32[3,64,256]{2,1,0:T(8,128)S(1)} %get-tuple-element.18), channel_id=1, source_target_pairs={{8,0},{0,8},{24,16},{16,24},{40,32},{32,40},{56,48},{48,56},{72,64... | collective-permute-start | bytes 589832 | tf_op jit(solution)/shard_map/ppermute | solution.py:18
  48.8 67.5 %collective-permute-start.9 = (bf16[512,2048]{1,0:T(8,128)(2,1)}, bf16[512,2048]{1,0:T(8,128)(2,1)}, u32[]{:S(2)}, u32[]{:S(2)}) collective-permute-start(bf16[512,2048]{1,0:T(8,128)(2,1)} %collective-permute-done.near_source), channel_id=1, source_target_pairs={{8,0},{0,8},{24,16},{16,24},{40,32},{32,40},{56,48},{48,56},{72,64... | collective-permute-start | bytes 6291464 | tf_op jit(solution)/shard_map/ppermute | solution.py:18
  50.1 5.4 %collective-permute-start.2 = (bf16[2,2,64,256]{3,2,1,0:T(8,128)(2,1)S(1)}, bf16[2,2,64,256]{3,2,1,0:T(8,128)(2,1)S(1)}, u32[]{:S(2)}, u32[]{:S(2)}) collective-permute-start(bf16[2,2,64,256]{3,2,1,0:T(8,128)(2,1)S(1)} %get-tuple-element.17), channel_id=1, source_target_pairs={{1,0},{0,1},{3,2},{2,3},{5,4},{4,5},{7,6},{6,7},{9,8},{8,9},{11,10... | collective-permute-start | bytes 393224 | tf_op jit(solution)/shard_map/ppermute | solution.py:18
  56.4 11.0 %all-to-all-start.1 = ((bf16[4,2,2,64,256]{4,3,2,1,0:T(8,128)(2,1)}), bf16[4,2,2,64,256]{4,3,2,1,0:T(8,128)(2,1)S(1)}, u32[]{:S(2)}, u32[]{:S(2)}) async-start(bf16[4,2,2,64,256]{4,3,2,1,0:T(8,128)(2,1)} %resid.1), calls=%async_computation.1 | async-start | bytes 1048576 | tf_op jit(solution)/shard_map/all_to_all | solution.py:420
  60.4 55.9 %collective-permute-start.7 = (bf16[256,2048]{1,0:T(8,128)(2,1)}, bf16[256,2048]{1,0:T(8,128)(2,1)}, u32[]{:S(2)}, u32[]{:S(2)}) collective-permute-start(bf16[256,2048]{1,0:T(8,128)(2,1)} %get-tuple-element.21), channel_id=1, source_target_pairs={{240,0},{24,8},{0,16},{40,24},{16,32},{56,40},{32,48},{72,56},{48,... | collective-permute-start | bytes 3145736 | tf_op jit(solution)/shard_map/ppermute | solution.py:18
  61.9 54.3 %collective-permute-start.8 = (bf16[256,2048]{1,0:T(8,128)(2,1)}, bf16[256,2048]{1,0:T(8,128)(2,1)}, u32[]{:S(2)}, u32[]{:S(2)}) collective-permute-start(bf16[256,2048]{1,0:T(8,128)(2,1)} %get-tuple-element.22), channel_id=1, source_target_pairs={{240,0},{24,8},{0,16},{40,24},{16,32},{56,40},{32,48},{72,56},{48,... | collective-permute-start | bytes 3145736 | tf_op jit(solution)/shard_map/ppermute | solution.py:18
  72.7 4.3 %collective-permute-start.10 = (f32[2048]{0:T(1024)S(1)}, f32[2048]{0:T(1024)S(1)}, u32[]{:S(2)}, u32[]{:S(2)}) collective-permute-start(f32[2048]{0:T(1024)S(1)} %bitcast.23), channel_id=1, source_target_pairs={{8,0},{0,8},{24,16},{16,24},{40,32},{32,40},{56,48},{48,56},{72,64... | collective-permute-start | bytes 24584 | tf_op jit(solution)/shard_map/ppermute | solution.py:18
  76.2 14.6 %collective-permute-start.11 = (f32[2048]{0:T(1024)S(1)}, f32[2048]{0:T(1024)S(1)}, u32[]{:S(2)}, u32[]{:S(2)}) collective-permute-start(f32[2048]{0:T(1024)S(1)} %bitcast.24), channel_id=1, source_target_pairs={{128,0},{136,8},{144,16},{152,24},{160,32},{168,40},{176,48},{184,... | collective-permute-start | bytes 24584 | tf_op jit(solution)/shard_map/ppermute | solution.py:18
  77.1 13.9 %collective-permute-start.12 = (f32[2048]{0:T(1024)S(1)}, f32[2048]{0:T(1024)S(1)}, u32[]{:S(2)}, u32[]{:S(2)}) collective-permute-start(f32[2048]{0:T(1024)S(1)} %bitcast.25), channel_id=1, source_target_pairs={{136,0},{128,8},{152,16},{144,24},{168,32},{160,40},{184,48},{176,... | collective-permute-start | bytes 24584 | tf_op jit(solution)/shard_map/ppermute | solution.py:18
  90.8 25.1 %collective-permute-start.6 = (bf16[4,2,2,64,256]{4,3,2,1,0:T(8,128)(2,1)S(1)}, bf16[4,2,2,64,256]{4,3,2,1,0:T(8,128)(2,1)S(1)}, u32[]{:S(2)}, u32[]{:S(2)}) collective-permute-start(bf16[4,2,2,64,256]{4,3,2,1,0:T(8,128)(2,1)S(1)} %all-to-all-done.1.mine), channel_id=1, source_target_pairs={{240,0},{24,8},{0,16},{40,24},{16,32},{56,40},{32,48},{72,56},{48,... | collective-permute-start | bytes 1572872 | tf_op jit(solution)/shard_map/ppermute | solution.py:18
  91.0 8.3 %collective-permute-start.14 = (f32[1,16,128]{2,1,0:T(8,128)S(1)}, f32[1,16,128]{2,1,0:T(8,128)S(1)}, u32[]{:S(2)}, u32[]{:S(2)}) collective-permute-start(f32[1,16,128]{2,1,0:T(8,128)S(1)} %add_bitcast_fusion), channel_id=1, source_target_pairs={{16,0},{24,8},{32,16},{40,24},{48,32},{56,40},{64,48},{72,56},{80,... | collective-permute-start | bytes 24584 | tf_op jit(solution)/shard_map/ppermute | solution.py:18
  99.3 3.7 %collective-permute-start.13 = (f32[1,16,128]{2,1,0:T(8,128)S(1)}, f32[1,16,128]{2,1,0:T(8,128)S(1)}, u32[]{:S(2)}, u32[]{:S(2)}) collective-permute-start(f32[1,16,128]{2,1,0:T(8,128)S(1)} %add_bitcast_fusion), channel_id=1, source_target_pairs={{112,0},{120,8},{0,16},{8,24},{16,32},{24,40},{32,48},{40,56},{48,... | collective-permute-start | bytes 24584 | tf_op jit(solution)/shard_map/ppermute | solution.py:18
  103.0 5.6 %collective-permute-start.16 = (f32[2,16,128]{2,1,0:T(8,128)S(1)}, f32[2,16,128]{2,1,0:T(8,128)S(1)}, u32[]{:S(2)}, u32[]{:S(2)}) collective-permute-start(f32[2,16,128]{2,1,0:T(8,128)S(1)} %pad_maximum_fusion.2), channel_id=1, source_target_pairs={{80,0},{88,8},{96,16},{104,24},{112,32},{120,40},{0,48},{8,56},{16... | collective-permute-start | bytes 49160 | tf_op jit(solution)/shard_map/ppermute | solution.py:18
  108.6 4.5 %collective-permute-start.15 = (f32[3,16,128]{2,1,0:T(8,128)S(1)}, f32[3,16,128]{2,1,0:T(8,128)S(1)}, u32[]{:S(2)}, u32[]{:S(2)}) collective-permute-start(f32[3,16,128]{2,1,0:T(8,128)S(1)} %pad_maximum_fusion.1.rows), channel_id=1, source_target_pairs={{48,0},{56,8},{64,16},{72,24},{80,32},{88,40},{96,48},{104,56},{11... | collective-permute-start | bytes 73736 | tf_op jit(solution)/shard_map/ppermute | solution.py:18
  113.1 2.8 %collective-permute-start.5 = (bf16[4,1,2,64,256]{4,3,2,1,0:T(8,128)(2,1)S(1)}, bf16[4,1,2,64,256]{4,3,2,1,0:T(8,128)(2,1)S(1)}, u32[]{:S(2)}, u32[]{:S(2)}) collective-permute-start(bf16[4,1,2,64,256]{4,3,2,1,0:T(8,128)(2,1)S(1)} %slice.14), channel_id=1, source_target_pairs={{8,0},{0,8},{24,16},{16,24},{40,32},{32,40},{56,48},{48,56},{72,64... | collective-permute-start | bytes 786440 | tf_op jit(solution)/shard_map/ppermute | solution.py:18
